TPU v7x, 512 devices: a whole 4x4x16 slice. The times are simulated.
512 devices in a mesh: sx: 32 (over z_hi, y, core), sy: 16 (over x, z_lo).
Axes of the slice: x: 4, y: 4, z: 16 (z_hi: 4, z_lo: 4; z = z_hi * 4 + z_lo), core: 2. Of those that a mesh axis runs over, the one named last changes fastest.
Arguments:
- forward_prop: bfloat16 [2, 2, 12, 12, 64, 4096], P(None, None, None, None, 'sx', 'sy'), may hold values from -0.08984375 to 0.08984375
- backward_prop: bfloat16 [2, 2, 12, 12, 64, 4096], P(None, None, None, None, 'sx', 'sy'), may hold values from -0.08984375 to 0.08984375
- gamma_table: int32 [16, 4, 2], replicated, may hold values from 0 to 3, as said below
- source_site: int32 [3], replicated, may hold values from 0 to 63
- momenta: int32 [32, 3], replicated, may hold values from -8 to 7
Outputs:
- corr: float32 [16, 2, 2, 64, 4096], P(None, None, None, 'sx', 'sy')
- listed: float32 [2, 16, 2, 32], replicated
Inputs may be any that keep to these rules, and one draw needn't show every extreme that they name: For every insertion g, gamma_table[g, 0..3, 0] is a permutation of 0..3; gamma_table[g, s, 1] is the power of i of that entry.
All inputs are finite; a program needn't handle non-finite values.
Results may differ from a plain program's by a relative error of at most 0.0003.
Values sent between devices are 32-bit elements; how exact they have to be, the bound alone decides.
A program may use at most 64 MiB of HBM per device.

v0:
```python
import math

import jax
import jax.numpy as jnp
from jax import lax
from jax.sharding import PartitionSpec as P

L = 64
LZ = 64


HIGHEST = lax.Precision.HIGHEST


def gamma_matrices(gamma_table):
    inserts = gamma_table.shape[0]
    columns = gamma_table[:, :, 0]
    powers = gamma_table[:, :, 1]
    spin_ids = jnp.arange(4, dtype=jnp.int32)
    matches = (columns[:, :, None] == spin_ids[None, None, :]).astype(jnp.float32)
    unit_re = (powers == 0).astype(jnp.float32) - (powers == 2).astype(jnp.float32)
    unit_im = (powers == 1).astype(jnp.float32) - (powers == 3).astype(jnp.float32)
    return (
        (matches * unit_re[:, :, None]).reshape(inserts, 16),
        (matches * unit_im[:, :, None]).reshape(inserts, 16),
    )


def dft_table(length, anchor):
    wavenum = jnp.arange(length, dtype=jnp.int32)
    offsets = jnp.mod(wavenum - anchor, length)
    phase_index = jnp.mod(offsets[:, None] * wavenum[None, :], length)
    angles = 2.0 * math.pi / length * phase_index.astype(jnp.float32)
    return (jnp.cos(angles), -jnp.sin(angles))


def complex_step(real_part, imag_part, table_re, table_im, pattern):
    out_re = jnp.einsum(pattern, real_part, table_re, precision=HIGHEST) - jnp.einsum(
        pattern, imag_part, table_im, precision=HIGHEST
    )
    out_im = jnp.einsum(pattern, real_part, table_im, precision=HIGHEST) + jnp.einsum(
        pattern, imag_part, table_re, precision=HIGHEST
    )
    return (out_re, out_im)


def transform(fields, source_site):
    table_re, table_im = dft_table(fields.shape[4], source_site[2])
    along_z = jnp.stack(
        complex_step(fields[:, 0], fields[:, 1], table_re, table_im, "nabz,zk->nabk"), 1
    )
    depth_share = along_z.shape[4] // lax.axis_size("sy")
    first_depth = lax.axis_index("sy") * depth_share
    length_y = along_z.shape[3] * lax.axis_size("sy")
    full_re, full_im = dft_table(length_y, source_site[1])
    part = lax.dynamic_slice_in_dim(
        lax.all_gather(along_z, "sy", axis=3, tiled=True), first_depth, depth_share, 4
    )
    step_re, step_im = complex_step(part[:, 0], part[:, 1], full_re, full_im, "nayc,yk->nakc")
    along_y = jnp.stack([step_re, step_im], 1)
    arrived = lax.all_to_all(along_y, "sx", split_axis=3, concat_axis=2, tiled=True)
    table_re, table_im = dft_table(arrived.shape[2], source_site[0])
    along_x = complex_step(arrived[:, 0], arrived[:, 1], table_re, table_im, "nxbc,xk->nbck")
    return jnp.stack(along_x, 1)


def apply_gammas(mat_re, mat_im, real_part, imag_part):
    extent = real_part.shape
    flat_re = real_part.reshape(extent[0], -1)
    flat_im = imag_part.reshape(extent[0], -1)
    out_re = jnp.dot(mat_re, flat_re, precision=HIGHEST) - jnp.dot(
        mat_im, flat_im, precision=HIGHEST
    )
    out_im = jnp.dot(mat_re, flat_im, precision=HIGHEST) + jnp.dot(
        mat_im, flat_re, precision=HIGHEST
    )
    return (out_re.reshape(extent), out_im.reshape(extent))


def project_sites(fields, source_site, momenta, rows_x, rows_y, length, depth):
    coord_x = lax.axis_index("sx") * rows_x + jnp.arange(rows_x, dtype=jnp.int32) - source_site[0]
    coord_y = lax.axis_index("sy") * rows_y + jnp.arange(rows_y, dtype=jnp.int32) - source_site[1]
    coord_z = jnp.arange(depth, dtype=jnp.int32) - source_site[2]
    part_x = jnp.mod(momenta[:, 0:1] * coord_x[None, :], length)
    part_y = jnp.mod(momenta[:, 1:2] * coord_y[None, :], length)
    part_z = jnp.mod(momenta[:, 2:3] * coord_z[None, :], depth)
    plane = jnp.mod(part_x[:, :, None] + part_y[:, None, :], length).astype(jnp.float32)
    angles = (
        2.0 * math.pi / length * plane[:, :, :, None]
        + 2.0 * math.pi / depth * part_z.astype(jnp.float32)[:, None, None, :]
    )
    angles = angles.reshape(momenta.shape[0], -1)
    cosine = jnp.cos(angles)
    sine = jnp.sin(angles)
    field_re = fields[:, 0].reshape(fields.shape[0], -1)
    field_im = fields[:, 1].reshape(fields.shape[0], -1)
    local_re = jnp.dot(field_re, cosine.T, precision=HIGHEST) + jnp.dot(
        field_im, sine.T, precision=HIGHEST
    )
    local_im = jnp.dot(field_im, cosine.T, precision=HIGHEST) - jnp.dot(
        field_re, sine.T, precision=HIGHEST
    )
    return (local_re, local_im)


def body(forward_prop, backward_prop, gamma_table, source_site, momenta):
    slices = forward_prop.shape[0]
    rows_x = forward_prop.shape[4]
    rows_y = backward_prop.shape[5] // LZ
    inserts = gamma_table.shape[0]
    forward = forward_prop.reshape(slices, 2, 4, 3, 12, -1)
    backward = backward_prop.reshape(slices, 2, 4, 3, 12, -1)
    pattern = "tscjn,tucjn->sutn"
    pair_re = jnp.einsum(
        pattern, backward[:, 0], forward[:, 0], preferred_element_type=jnp.float32
    ) + jnp.einsum(pattern, backward[:, 1], forward[:, 1], preferred_element_type=jnp.float32)
    pair_im = jnp.einsum(
        pattern, backward[:, 0], forward[:, 1], preferred_element_type=jnp.float32
    ) - jnp.einsum(pattern, backward[:, 1], forward[:, 0], preferred_element_type=jnp.float32)
    pair_re = pair_re.reshape(16, slices, -1)
    pair_im = pair_im.reshape(16, slices, -1)
    mat_re, mat_im = gamma_matrices(gamma_table)
    field_re, field_im = apply_gammas(mat_re, mat_im, pair_re, pair_im)
    fields = jnp.stack([field_re, field_im], 2).reshape(inserts * slices, 2, rows_x, rows_y, LZ)
    spectrum = transform(fields, source_site)
    local_re, local_im = project_sites(fields, source_site, momenta, rows_x, rows_y, L, LZ)
    listed_re, listed_im = lax.psum((local_re, local_im), ("sx", "sy"))
    listed_re = listed_re.reshape(inserts, slices, -1)
    listed_im = listed_im.reshape(inserts, slices, -1)
    corr_re = spectrum[:, 0].reshape(inserts, slices, spectrum.shape[2], -1)
    corr_im = spectrum[:, 1].reshape(inserts, slices, spectrum.shape[2], -1)
    return (jnp.stack([corr_re, corr_im], 2), jnp.stack([listed_re, listed_im], 0))


def solution(mesh):
    placed = (
        P(None, None, None, None, "sx", "sy"),
        P(None, None, None, None, "sx", "sy"),
        P(),
        P(),
        P(),
    )
    return jax.shard_map(
        body,
        mesh=mesh,
        in_specs=placed,
        out_specs=(P(None, None, None, "sx", "sy"), P()),
        check_vma=False,
    )
```

profile of v0, /device:TPU:1, one launch (start us, length us, event | category | flops | bytes accessed | tf_op | source)
XLA Modules:
  0.0 323.4 jit_solution(12954592644119887692)
XLA Ops:
  7.2 0.7 fusion.92
  7.9 2.1 reshape.371
  10.0 0.8 fusion.144
  10.9 4.5 %copy.82 = bf16[2,1,4,3,12,512]{4,2,3,5,0,1:T(4,128)(2,1)S(1)} copy(bf16[2,1,4,3,12,512]{5,4,3,2,1,0:T(8,128)(2,1)} %get-tuple-element.11) | data formatting | bytes 589824
  15.3 2.8 reshape.372
  18.1 2.1 fusion.145
  20.2 5.3 %copy.83 = bf16[2,1,4,3,12,512]{4,2,3,5,0,1:T(4,128)(2,1)} copy(bf16[2,1,4,3,12,512]{5,4,3,2,1,0:T(8,128)(2,1)} %get-tuple-element.13) | data formatting | bytes 589824
  25.4 3.8 %copy.80 = bf16[2,1,4,3,12,512]{4,2,3,5,0,1:T(4,128)(2,1)} copy(bf16[2,1,4,3,12,512]{5,4,3,2,1,0:T(8,128)(2,1)S(1)} %get-tuple-element.10) | data formatting | bytes 589824
  29.2 5.3 %copy.81 = bf16[2,1,4,3,12,512]{4,2,3,5,0,1:T(4,128)(2,1)} copy(bf16[2,1,4,3,12,512]{5,4,3,2,1,0:T(8,128)(2,1)} %get-tuple-element.12) | data formatting | bytes 589824
  34.5 5.6 %fusion.2 = f32[2,512,4,4,1]{3,2,4,1,0:T(4,128)S(1)} fusion(bf16[2,1,4,3,12,512]{4,2,3,5,0,1:T(4,128)(2,1)} %copy.83, bf16[2,1,4,3,12,512]{4,2,3,5,0,1:T(4,128)(2,1)S(1)} %copy.82), kind=kOutput, calls=%fused_computation.2 | convolution fusion | flops 1179648 | bytes 655360 | tf_op jit(solution)/shard_map/tscjn,tucjn->sutn/dot_general | solution.py:116
  40.2 5.0 %fusion = f32[2,512,4,4,1]{3,2,4,1,0:T(4,128)} fusion(bf16[2,1,4,3,12,512]{4,2,3,5,0,1:T(4,128)(2,1)S(1)} %copy-done.1, bf16[2,1,4,3,12,512]{4,2,3,5,0,1:T(4,128)(2,1)S(1)} %copy-done.2), kind=kOutput, calls=%fused_computation | convolution fusion | flops 1179648 | bytes 655360 | tf_op jit(solution)/shard_map/tscjn,tucjn->sutn/dot_general | solution.py:119
  45.2 3.7 %fusion.13 = f32[4,4,2,512]{0,1,3,2:T(4,128)} fusion(f32[2,512,4,4,1]{3,2,4,1,0:T(4,128)S(1)} %fusion.2, bf16[2,1,4,3,12,512]{4,2,3,5,0,1:T(4,128)(2,1)S(1)} %copy-done, bf16[2,1,4,3,12,512]{4,2,3,5,0,1:T(4,128)(2,1)S(1)} %copy-done.2), kind=kOutput, calls=%fused_computation.17 | convolution fusion | flops 1196032 | bytes 720896 | tf_op jit(solution)/shard_map/tscjn,tucjn->sutn/dot_general | solution.py:114
  48.8 2.1 copy.48
  51.0 7.5 %fusion.12 = f32[4,4,2,512]{0,1,3,2:T(4,128)} fusion(f32[2,512,4,4,1]{3,2,4,1,0:T(4,128)} %fusion, bf16[2,1,4,3,12,512]{4,2,3,5,0,1:T(4,128)(2,1)} %copy.81, bf16[2,1,4,3,12,512]{4,2,3,5,0,1:T(4,128)(2,1)S(1)} %copy.82), kind=kOutput, calls=%fused_computation.15 | convolution fusion | flops 1196032 | bytes 720896 | tf_op jit(solution)/shard_map/tscjn,tucjn->sutn/dot_general | solution.py:117
  58.5 1.9 copy.49
  60.5 0.7 fusion.146
  62.0 1.3 and_select_fusion.1
  63.3 0.5 fusion.32
  63.8 0.5 fusion.30
  64.6 0.5 fusion.25
  65.1 0.5 fusion.24
  65.5 0.7 pad_maximum_fusion
  66.3 0.6 iota_subtract_fusion
  67.0 0.7 add_subtract_fusion.1
  67.6 0.7 add_subtract_fusion
  68.7 1.1 add_sine_fusion
  70.0 0.7 and_select_fusion.3
  71.1 107.5 %all-gather.2.cloned.1.call-done = f32[32,2,2,64,64]{4,0,3,2,1:T(8,128)} async-done(((f32[32,2,2,4,64]{4,0,3,2,1:T(8,128)}), f32[32,2,2,64,64]{4,0,3,2,1:T(8,128)}) %all-gather.2.cloned.1.call-update) | async-done | bytes 2097168 | tf_op jit(solution)/shard_map/all_gather | solution.py:57
  178.6 4.7 %dynamic-slice_bitcast_fusion = (f32[32,2,64,4]{3,0,2,1:T(8,128)S(1)}, f32[32,2,64,4]{3,0,2,1:T(8,128)}) fusion(f32[32,2,2,64,64]{4,0,3,2,1:T(8,128)} %all-gather.2.cloned.1.call-done, s32[]{:T(128)S(6)} %add.213, s32[]{:T(128)S(6)} %select_n.88), kind=kLoop, calls=%fused_computation.12 | loop fusion | bytes 262152 | tf_op jit(solution)/shard_map/squeeze | solution.py:59
  183.3 2.6 copy.54
  186.0 0.5 fusion.51
  186.4 0.5 fusion.53
  186.9 1.2 copy.55
  188.1 0.5 fusion.23
  188.5 0.5 fusion.22
  189.0 0.3 copy.58
  189.4 1.0 reshape.373
  190.4 13.0 %all-to-all-start = ((f32[32,1,1024]{2,1,0:T(1,128)}), f32[32,1,1024]{2,1,0:T(1,128)S(1)}, u32[]{:S(2)}, u32[]{:S(2)}) async-start(f32[32,1,1024]{2,1,0:T(1,128)} %reshape.373), calls=%async_computation | async-start | bytes 262144 | tf_op jit(solution)/shard_map/all_to_all | solution.py:61
  203.8 106.2 %all-reduce = (f32[1,16,2,32]{3,2,1,0:T(2,128)S(1)}, f32[1,16,2,32]{3,2,1,0:T(2,128)S(1)}) all-reduce(f32[1,16,2,32]{3,2,1,0:T(2,128)S(1)} %bitcast.184, f32[1,16,2,32]{3,2,1,0:T(2,128)S(1)} %bitcast.183), channel_id=1, replica_groups=mesh['sx'=32,'sy'=16] {'sx','sy'}, use_global_device_ids=true, to_apply=%region_1.2 | all-reduce | flops 2048 | bytes 16384 | tf_op jit(solution)/shard_map/psum | solution.py:127
  309.9 0.6 pad_maximum_fusion.3
  310.6 0.5 broadcast.522
  311.1 0.9 reduce
  312.5 0.4 copy.60
  312.9 0.6 fusion.27
  313.5 0.6 fusion.26
  314.1 0.6 convolution_subtract_fusion.2
  315.0 0.6 convolution_add_fusion.2
  315.9 0.7 copy.65
  (45 shorter events, 3.7 us)
Async XLA Ops:
  7.2 171.4 %all-gather.2.cloned.1.call-start = ((), (), s32[]{:S(2)}) async-start(), calls=%async_computation.1 | async-start | bytes 4456448 | tf_op jit(solution)/shard_map/all_gather | solution.py:57
  34.5 5.6 %copy-start.1 = (bf16[2,1,4,3,12,512]{4,2,3,5,0,1:T(4,128)(2,1)S(1)}, bf16[2,1,4,3,12,512]{4,2,3,5,0,1:T(4,128)(2,1)}, u32[]{:S(2)}) copy-start(bf16[2,1,4,3,12,512]{4,2,3,5,0,1:T(4,128)(2,1)} %copy.83) | copy-start | bytes 884740
  34.5 5.6 %copy-start.2 = (bf16[2,1,4,3,12,512]{4,2,3,5,0,1:T(4,128)(2,1)S(1)}, bf16[2,1,4,3,12,512]{4,2,3,5,0,1:T(4,128)(2,1)}, u32[]{:S(2)}) copy-start(bf16[2,1,4,3,12,512]{4,2,3,5,0,1:T(4,128)(2,1)} %copy.80) | copy-start | bytes 884740
  40.2 5.0 %copy-start = (bf16[2,1,4,3,12,512]{4,2,3,5,0,1:T(4,128)(2,1)S(1)}, bf16[2,1,4,3,12,512]{4,2,3,5,0,1:T(4,128)(2,1)}, u32[]{:S(2)}) copy-start(bf16[2,1,4,3,12,512]{4,2,3,5,0,1:T(4,128)(2,1)} %copy.81) | copy-start | bytes 884740
  50.9 9.5 %copy-start.3 = (s32[3]{0:T(128)S(1)}, s32[3]{0:T(128)}, u32[]{:S(2)}) copy-start(s32[3]{0:T(128)} %param.8) | copy-start | bytes 40
  50.9 10.2 %slice-start = ((s32[16,4,2]{0,2,1:T(2,128)}), s32[16,4,1]{0,2,1:T(1,128)S(1)}, s32[]{:S(2)}) async-start(s32[16,4,2]{0,2,1:T(2,128)} %param.7), calls=%async_computation.2 | async-start | bytes 4096 | tf_op jit(solution)/shard_map/slice | solution.py:17
  58.5 9.8 %copy-start.4 = (s32[32,3]{0,1:T(4,128)S(1)}, s32[32,3]{0,1:T(4,128)}, u32[]{:S(2)}) copy-start(s32[32,3]{0,1:T(4,128)} %param.9) | copy-start | bytes 1156
  190.4 120.2 %all-to-all-start = ((f32[32,1,1024]{2,1,0:T(1,128)}), f32[32,1,1024]{2,1,0:T(1,128)S(1)}, u32[]{:S(2)}, u32[]{:S(2)}) async-start(f32[32,1,1024]{2,1,0:T(1,128)} %reshape.373), calls=%async_computation | async-start | bytes 262144 | tf_op jit(solution)/shard_map/all_to_all | solution.py:61
Sparse Core Ops, SparseCore 0:
  66.4 112.1 all-gather.1
where the time goes:
time: 325 us; the launch traced here: 323 us
  waiting for transfers between devices  108 us (33%)
  blocking collectives  106 us (33%)
  local copies, waits for them, and re-layouts  44.1 us (14%)
  matrix products  29.7 us (9%)
  between operations  14.4 us (4%)
  starting transfers between devices  13 us (4%)
  other arithmetic  8.45 us (3%)
    all_gather x1, waiting for transfers between devices, transform(): lax.all_gather(along_z, 'sy', axis=3, tiled=True)  107 us
    psum x1, blocking collectives, body(): listed_re, listed_im = lax.psum((local_re, local_im), ('sx', 'sy'))  106 us
    unnamed x19, local copies, waits for them, and re-layouts  20.8 us
    all_to_all x1, starting transfers between devices, transform(): lax.all_to_all(along_y, 'sx', split_axis=3, concat_axis=2, tiled=True)  13 us
    dot_general x1, matrix products, body(): jnp.einsum(pattern, backward[:, 0], forward[:, 1], preferred_element_type...  7.53 us
  transfers between devices with their start and end apart: 2, of which 1 were waited for; matrix products, arithmetic and copies ran while one was open for 2% of the time, Pallas kernels for 0%

commit v1 on v0

--- a/solution.py
+++ b/solution.py
@@ -34,34 +34,19 @@
     return (jnp.cos(angles), -jnp.sin(angles))
 
 
-def complex_step(real_part, imag_part, table_re, table_im, pattern):
-    out_re = jnp.einsum(pattern, real_part, table_re, precision=HIGHEST) - jnp.einsum(
-        pattern, imag_part, table_im, precision=HIGHEST
-    )
-    out_im = jnp.einsum(pattern, real_part, table_im, precision=HIGHEST) + jnp.einsum(
-        pattern, imag_part, table_re, precision=HIGHEST
-    )
-    return (out_re, out_im)
+def dft_matrix(length, anchor):
+    table_re, table_im = dft_table(length, anchor)
+    rows_re = jnp.stack([table_re, table_im], 1)
+    rows_im = jnp.stack([-table_im, table_re], 1)
+    return jnp.stack([rows_re, rows_im], 0)
 
 
-def transform(fields, source_site):
-    table_re, table_im = dft_table(fields.shape[4], source_site[2])
-    along_z = jnp.stack(
-        complex_step(fields[:, 0], fields[:, 1], table_re, table_im, "nabz,zk->nabk"), 1
-    )
-    depth_share = along_z.shape[4] // lax.axis_size("sy")
-    first_depth = lax.axis_index("sy") * depth_share
-    length_y = along_z.shape[3] * lax.axis_size("sy")
-    full_re, full_im = dft_table(length_y, source_site[1])
-    part = lax.dynamic_slice_in_dim(
-        lax.all_gather(along_z, "sy", axis=3, tiled=True), first_depth, depth_share, 4
-    )
-    step_re, step_im = complex_step(part[:, 0], part[:, 1], full_re, full_im, "nayc,yk->nakc")
-    along_y = jnp.stack([step_re, step_im], 1)
-    arrived = lax.all_to_all(along_y, "sx", split_axis=3, concat_axis=2, tiled=True)
-    table_re, table_im = dft_table(arrived.shape[2], source_site[0])
-    along_x = complex_step(arrived[:, 0], arrived[:, 1], table_re, table_im, "nxbc,xk->nbck")
-    return jnp.stack(along_x, 1)
+def exchange(blocks, shared, axis):
+    parts = blocks.shape[0]
+    width = blocks.shape[1]
+    extra = jnp.broadcast_to(shared.reshape(1, -1), (parts, shared.size))
+    got = lax.all_to_all(jnp.concatenate([blocks, extra], 1), axis, 0, 0, tiled=True)
+    return got[:, :width], got[:, width:].sum(0).reshape(shared.shape)
 
 
 def apply_gammas(mat_re, mat_im, real_part, imag_part):
@@ -122,14 +107,31 @@
     mat_re, mat_im = gamma_matrices(gamma_table)
     field_re, field_im = apply_gammas(mat_re, mat_im, pair_re, pair_im)
     fields = jnp.stack([field_re, field_im], 2).reshape(inserts * slices, 2, rows_x, rows_y, LZ)
-    spectrum = transform(fields, source_site)
+    count = fields.shape[0]
     local_re, local_im = project_sites(fields, source_site, momenta, rows_x, rows_y, L, LZ)
-    listed_re, listed_im = lax.psum((local_re, local_im), ("sx", "sy"))
-    listed_re = listed_re.reshape(inserts, slices, -1)
-    listed_im = listed_im.reshape(inserts, slices, -1)
-    corr_re = spectrum[:, 0].reshape(inserts, slices, spectrum.shape[2], -1)
-    corr_im = spectrum[:, 1].reshape(inserts, slices, spectrum.shape[2], -1)
-    return (jnp.stack([corr_re, corr_im], 2), jnp.stack([listed_re, listed_im], 0))
+    partial = jnp.stack([local_re, local_im], 0)
+    groups_y = lax.axis_size("sy")
+    groups_x = lax.axis_size("sx")
+    along_z = jnp.einsum(
+        "nrxyz,rzsk->nsxyk", fields, dft_matrix(LZ, source_site[2]), precision=HIGHEST
+    )
+    share_z = LZ // groups_y
+    blocks = along_z.reshape(count, 2, rows_x, rows_y, groups_y, share_z)
+    blocks = blocks.transpose(4, 0, 1, 2, 3, 5).reshape(groups_y, -1)
+    blocks, partial = exchange(blocks, partial, "sy")
+    blocks = blocks.reshape(groups_y, count, 2, rows_x, rows_y, share_z)
+    table_y = dft_matrix(rows_y * groups_y, source_site[1]).reshape(2, groups_y, rows_y, 2, -1)
+    along_y = jnp.einsum("jnrxyc,rjysk->nsxkc", blocks, table_y, precision=HIGHEST)
+    share_y = along_y.shape[3] // groups_x
+    blocks = along_y.reshape(count, 2, rows_x, groups_x, share_y, share_z)
+    blocks = blocks.transpose(3, 0, 1, 2, 4, 5).reshape(groups_x, -1)
+    blocks, partial = exchange(blocks, partial, "sx")
+    blocks = blocks.reshape(groups_x, count, 2, rows_x, share_y, share_z)
+    table_x = dft_matrix(rows_x * groups_x, source_site[0]).reshape(2, groups_x, rows_x, 2, -1)
+    spectrum = jnp.einsum("inrxbc,rixsk->nsbck", blocks, table_x, precision=HIGHEST)
+    corr = spectrum.reshape(inserts, slices, 2, share_y, -1)
+    listed = partial.reshape(2, inserts, slices, -1)
+    return (corr, listed)
 
 
 def solution(mesh):

time: 325 us -> 134 us (0.41)
  blocking collectives: 106 us -> 0 us
  waiting for transfers between devices: 108 us -> 32.1 us
  starting transfers between devices: 13 us -> 26.4 us
  between operations: 14.4 us -> 1.04 us
  local copies, waits for them, and re-layouts: 44.1 us -> 40.1 us
  matrix products: 29.7 us -> 26.1 us
    all_gather x1 -> x0, waiting for transfers between devices: 107 us -> none  [transform(): lax.all_gather(along_z, 'sy', axis=3, tiled=True)]
    psum x1 -> x0, blocking collectives: 106 us -> none  [body(): listed_re, listed_im = lax.psum((local_re, local_im), ('sx', 'sy'))]
    all_to_all x1 -> x2, waiting for transfers between devices: 0.01 us -> 32.1 us  [exchange(): lax.all_to_all(jnp.concatenate([blocks, extra], 1), axis, 0, 0, tiled=True)]
    all_to_all x1 -> x2, starting transfers between devices: 13 us -> 26.4 us  [exchange(): lax.all_to_all(jnp.concatenate([blocks, extra], 1), axis, 0, 0, tiled=True)]
    squeeze x5 -> x0, local copies, waits for them, and re-layouts: 8.76 us -> none  [the longest x2 5.88 us: transform(): part[:, 1]]
    dot_general x12 -> x3, matrix products: 6.12 us -> 2.47 us  [the longest x1 1.02 us: body(): jnp.einsum('inrxbc,rixsk->nsbck', blocks, table_x, precision=HIGHEST)]
    unnamed x19 -> x17, local copies, waits for them, and re-layouts: 20.8 us -> 19.1 us
  transfers between devices with their start and end apart: 2 -> 2, of which waited for: 1 -> 2; matrix products, arithmetic and copies ran while one was open for 2% -> 1% of each run, Pallas kernels for 0% -> 0%
where the time goes in v1:
time: 134 us; the launch traced here: 132 us
  local copies, waits for them, and re-layouts  40.1 us (30%)
  waiting for transfers between devices  32.1 us (24%)
  starting transfers between devices  26.4 us (20%)
  matrix products  26.1 us (19%)
  other arithmetic  6.47 us (5%)
    all_to_all x2, waiting for transfers between devices, exchange(): lax.all_to_all(jnp.concatenate([blocks, extra], 1), axis, 0, 0, tiled=True)  32.1 us
    all_to_all x2, starting transfers between devices, exchange(): lax.all_to_all(jnp.concatenate([blocks, extra], 1), axis, 0, 0, tiled=True)  26.4 us
    unnamed x17, local copies, waits for them, and re-layouts  19.1 us
    dot_general x1, matrix products, body(): jnp.einsum(pattern, backward[:, 0], forward[:, 1], preferred_element_type...  7.53 us
    dot_general x1, matrix products, body(): jnp.einsum(pattern, backward[:, 1], forward[:, 1], preferred_element_type...  5.64 us
    dot_general x1, matrix products, body(): jnp.einsum(pattern, backward[:, 1], forward[:, 0], preferred_element_type...  4.99 us
    dot_general x1, matrix products, body(): jnp.einsum(pattern, backward[:, 0], forward[:, 0], preferred_element_type...  3.67 us
    reshape x1, local copies, waits for them, and re-layouts, body(): backward = backward_prop.reshape(slices, 2, 4, 3, 12, -1)  2.78 us
  transfers between devices with their start and end apart: 2, of which 2 were waited for; matrix products, arithmetic and copies ran while one was open for 1% of the time, Pallas kernels for 0%

profile of v1, /device:TPU:1, one launch (start us, length us, event | category | flops | bytes accessed | tf_op | source)
XLA Modules:
  0.0 132.3 jit_solution(10767023476026789172)
XLA Ops:
  0.6 0.7 fusion.81
  1.3 2.1 %reshape.766 = bf16[2,2,4,3,12,512]{5,4,3,2,1,0:T(8,128)(2,1)S(1)} reshape(bf16[2,2,12,12,2,256]{5,4,3,2,1,0:T(2,128)(2,1)} %param.5) | data formatting | bytes 1179648 | tf_op jit(solution)/shard_map/reshape | solution.py:96
  3.5 0.8 fusion.88
  4.3 4.5 %copy.73 = bf16[2,1,4,3,12,512]{4,2,3,5,0,1:T(4,128)(2,1)S(1)} copy(bf16[2,1,4,3,12,512]{5,4,3,2,1,0:T(8,128)(2,1)} %get-tuple-element.2) | data formatting | bytes 589824
  8.7 2.8 %reshape.767 = bf16[2,2,4,3,12,512]{5,4,3,2,1,0:T(8,128)(2,1)} reshape(bf16[2,2,12,12,2,256]{5,4,3,2,1,0:T(2,128)(2,1)} %param.6) | data formatting | bytes 1179648 | tf_op jit(solution)/shard_map/reshape | solution.py:97
  11.5 2.1 %fusion.89 = (bf16[2,1,4,3,12,512]{5,4,3,2,1,0:T(8,128)(2,1)}, bf16[2,1,4,3,12,512]{5,4,3,2,1,0:T(8,128)(2,1)}) fusion(bf16[2,2,4,3,12,512]{5,4,3,2,1,0:T(8,128)(2,1)} %reshape.767), kind=kLoop, calls=%fused_computation.151 | loop fusion | bytes 1179648 | tf_op jit(solution)/shard_map/slice | solution.py:100
  13.6 5.3 %copy.74 = bf16[2,1,4,3,12,512]{4,2,3,5,0,1:T(4,128)(2,1)} copy(bf16[2,1,4,3,12,512]{5,4,3,2,1,0:T(8,128)(2,1)} %get-tuple-element.5) | data formatting | bytes 589824
  18.9 3.8 %copy.71 = bf16[2,1,4,3,12,512]{4,2,3,5,0,1:T(4,128)(2,1)} copy(bf16[2,1,4,3,12,512]{5,4,3,2,1,0:T(8,128)(2,1)S(1)} %get-tuple-element.3) | data formatting | bytes 589824
  22.7 5.3 %copy.72 = bf16[2,1,4,3,12,512]{4,2,3,5,0,1:T(4,128)(2,1)} copy(bf16[2,1,4,3,12,512]{5,4,3,2,1,0:T(8,128)(2,1)} %get-tuple-element.4) | data formatting | bytes 589824
  28.0 5.6 %fusion.2 = f32[2,512,4,4,1]{3,2,4,1,0:T(4,128)S(1)} fusion(bf16[2,1,4,3,12,512]{4,2,3,5,0,1:T(4,128)(2,1)} %copy.74, bf16[2,1,4,3,12,512]{4,2,3,5,0,1:T(4,128)(2,1)S(1)} %copy.73), kind=kOutput, calls=%fused_computation.2 | convolution fusion | flops 1179648 | bytes 655360 | tf_op jit(solution)/shard_map/tscjn,tucjn->sutn/dot_general | solution.py:101
  33.7 5.0 %fusion = f32[2,512,4,4,1]{3,2,4,1,0:T(4,128)} fusion(bf16[2,1,4,3,12,512]{4,2,3,5,0,1:T(4,128)(2,1)S(1)} %copy-done.1, bf16[2,1,4,3,12,512]{4,2,3,5,0,1:T(4,128)(2,1)S(1)} %copy-done.2), kind=kOutput, calls=%fused_computation | convolution fusion | flops 1179648 | bytes 655360 | tf_op jit(solution)/shard_map/tscjn,tucjn->sutn/dot_general | solution.py:104
  38.7 3.7 %fusion.13 = f32[4,4,2,512]{0,1,3,2:T(4,128)} fusion(f32[2,512,4,4,1]{3,2,4,1,0:T(4,128)S(1)} %fusion.2, bf16[2,1,4,3,12,512]{4,2,3,5,0,1:T(4,128)(2,1)S(1)} %copy-done, bf16[2,1,4,3,12,512]{4,2,3,5,0,1:T(4,128)(2,1)S(1)} %copy-done.2), kind=kOutput, calls=%fused_computation.15 | convolution fusion | flops 1196032 | bytes 720896 | tf_op jit(solution)/shard_map/tscjn,tucjn->sutn/dot_general | solution.py:99
  42.3 2.1 %copy.40 = f32[4,4,2,512]{3,2,1,0:T(2,128)S(1)} copy(f32[4,4,2,512]{0,1,3,2:T(4,128)} %fusion.13) | data formatting | bytes 131072 | tf_op jit(solution)/shard_map/add | solution.py:99
  44.5 7.5 %fusion.12 = f32[4,4,2,512]{0,1,3,2:T(4,128)} fusion(f32[2,512,4,4,1]{3,2,4,1,0:T(4,128)} %fusion, bf16[2,1,4,3,12,512]{4,2,3,5,0,1:T(4,128)(2,1)} %copy.72, bf16[2,1,4,3,12,512]{4,2,3,5,0,1:T(4,128)(2,1)S(1)} %copy.73), kind=kOutput, calls=%fused_computation.13 | convolution fusion | flops 1196032 | bytes 720896 | tf_op jit(solution)/shard_map/tscjn,tucjn->sutn/dot_general | solution.py:102
  52.0 1.9 %copy.41 = f32[4,4,2,512]{3,2,1,0:T(2,128)S(1)} copy(f32[4,4,2,512]{0,1,3,2:T(4,128)} %fusion.12) | data formatting | bytes 131072 | tf_op jit(solution)/shard_map/sub | solution.py:102
  54.0 0.3 fusion.91
  54.2 0.3 fusion.92
  54.5 0.3 convolution_subtract_fusion
  54.9 0.3 convolution_add_fusion
  55.3 0.6 fusion.90
  55.9 0.6 add_subtract_fusion.1
  56.8 0.7 and_select_fusion.2
  57.4 0.6 add_subtract_fusion
  58.4 1.1 add_sine_fusion
  60.7 0.2 fusion.74
  60.9 0.4 convolution_bitcast_fusion.2
  61.3 0.2 copy.44
  61.5 1.1 copy.45
  62.7 0.3 copy.47
  63.0 1.0 all_to_all.16
  64.0 9.0 %all-to-all-start = ((f32[16,1,4096]{2,1,0:T(1,128)}), f32[16,1,4096]{2,1,0:T(1,128)S(1)}, u32[]{:S(2)}, u32[]{:S(2)}) async-start(f32[16,1,4096]{2,1,0:T(1,128)} %all_to_all.16), calls=%async_computation | async-start | bytes 524288 | tf_op jit(solution)/shard_map/all_to_all | solution.py:48
  73.0 0.6 add_select_fusion.5
  73.6 0.2 fusion.76
  73.9 8.8 %all-to-all-done = f32[16,1,4096]{2,1,0:T(1,128)S(1)} async-done(((f32[16,1,4096]{2,1,0:T(1,128)}), f32[16,1,4096]{2,1,0:T(1,128)S(1)}, u32[]{:S(2)}, u32[]{:S(2)}) %all-to-all-start) | async-done | bytes 262176 | tf_op jit(solution)/shard_map/all_to_all | solution.py:48
  82.8 0.3 copy.48
  83.1 0.6 copy.49
  83.7 1.0 convolution_bitcast_fusion.1
  85.0 0.5 copy.51
  85.8 1.0 all_to_all.19
  86.8 17.4 %all-to-all-start.1 = ((f32[32,1,3072]{2,1,0:T(1,128)}), f32[32,1,3072]{2,1,0:T(1,128)S(1)}, u32[]{:S(2)}, u32[]{:S(2)}) async-start(f32[32,1,3072]{2,1,0:T(1,128)} %all_to_all.19), calls=%async_computation.1 | async-start | bytes 786432 | tf_op jit(solution)/shard_map/all_to_all | solution.py:48
  104.2 0.7 and_select_fusion.3
  104.9 0.2 fusion.75
  105.1 23.4 %all-to-all-done.1 = f32[32,1,3072]{2,1,0:T(1,128)S(1)} async-done(((f32[32,1,3072]{2,1,0:T(1,128)}), f32[32,1,3072]{2,1,0:T(1,128)S(1)}, u32[]{:S(2)}, u32[]{:S(2)}) %all-to-all-start.1) | async-done | bytes 393248 | tf_op jit(solution)/shard_map/all_to_all | solution.py:48
  128.5 0.6 copy.53
  129.1 0.3 slice_reduce_fusion
  129.5 1.0 convolution_bitcast_fusion
  130.7 0.9 reshape.752
  131.6 0.7 reshape_reshape.12
  (46 shorter events, 2.8 us)
Async XLA Ops:
  28.0 5.6 %copy-start.1 = (bf16[2,1,4,3,12,512]{4,2,3,5,0,1:T(4,128)(2,1)S(1)}, bf16[2,1,4,3,12,512]{4,2,3,5,0,1:T(4,128)(2,1)}, u32[]{:S(2)}) copy-start(bf16[2,1,4,3,12,512]{4,2,3,5,0,1:T(4,128)(2,1)} %copy.74) | copy-start | bytes 884740
  28.0 5.6 %copy-start.2 = (bf16[2,1,4,3,12,512]{4,2,3,5,0,1:T(4,128)(2,1)S(1)}, bf16[2,1,4,3,12,512]{4,2,3,5,0,1:T(4,128)(2,1)}, u32[]{:S(2)}) copy-start(bf16[2,1,4,3,12,512]{4,2,3,5,0,1:T(4,128)(2,1)} %copy.71) | copy-start | bytes 884740
  33.7 5.0 %copy-start = (bf16[2,1,4,3,12,512]{4,2,3,5,0,1:T(4,128)(2,1)S(1)}, bf16[2,1,4,3,12,512]{4,2,3,5,0,1:T(4,128)(2,1)}, u32[]{:S(2)}) copy-start(bf16[2,1,4,3,12,512]{4,2,3,5,0,1:T(4,128)(2,1)} %copy.72) | copy-start | bytes 884740
  44.4 9.5 %slice-start = ((s32[16,4,2]{0,2,1:T(2,128)}), s32[16,4,1]{0,2,1:T(1,128)S(1)}, s32[]{:S(2)}) async-start(s32[16,4,2]{0,2,1:T(2,128)} %param.7), calls=%async_computation.2 | async-start | bytes 4096 | tf_op jit(solution)/shard_map/slice | solution.py:17
  52.0 3.3 %copy-start.3 = (s32[3]{0:T(128)S(1)}, s32[3]{0:T(128)}, u32[]{:S(2)}) copy-start(s32[3]{0:T(128)} %param.8) | copy-start | bytes 40
  52.0 3.9 %copy-start.4 = (s32[32,3]{0,1:T(4,128)S(1)}, s32[32,3]{0,1:T(4,128)}, u32[]{:S(2)}) copy-start(s32[32,3]{0,1:T(4,128)} %param.9) | copy-start | bytes 1156
  64.0 18.6 %all-to-all-start = ((f32[16,1,4096]{2,1,0:T(1,128)}), f32[16,1,4096]{2,1,0:T(1,128)S(1)}, u32[]{:S(2)}, u32[]{:S(2)}) async-start(f32[16,1,4096]{2,1,0:T(1,128)} %all_to_all.16), calls=%async_computation | async-start | bytes 524288 | tf_op jit(solution)/shard_map/all_to_all | solution.py:48
  86.8 41.7 %all-to-all-start.1 = ((f32[32,1,3072]{2,1,0:T(1,128)}), f32[32,1,3072]{2,1,0:T(1,128)S(1)}, u32[]{:S(2)}, u32[]{:S(2)}) async-start(f32[32,1,3072]{2,1,0:T(1,128)} %all_to_all.19), calls=%async_computation.1 | async-start | bytes 786432 | tf_op jit(solution)/shard_map/all_to_all | solution.py:48

commit v2 on v1

--- a/solution.py
+++ b/solution.py
@@ -3,6 +3,8 @@
 import jax
 import jax.numpy as jnp
 from jax import lax
+from jax.experimental import pallas as pl
+from jax.experimental.pallas import tpu as pltpu
 from jax.sharding import PartitionSpec as P
 
 L = 64
@@ -88,25 +90,62 @@
     return (local_re, local_im)
 
 
+def contract_kernel(mix_ref, forward_ref, backward_ref, out_ref, pair_ref):
+    slices = forward_ref.shape[0]
+    rows = forward_ref.shape[3]
+    for t in range(slices):
+        for u in range(4):
+            f_re = [forward_ref[t, 0, 3 * u + c].astype(jnp.float32) for c in range(3)]
+            f_im = [forward_ref[t, 1, 3 * u + c].astype(jnp.float32) for c in range(3)]
+            for s in range(4):
+                acc_re = None
+                acc_im = None
+                for c in range(3):
+                    b_re = backward_ref[t, 0, 3 * s + c].astype(jnp.float32)
+                    b_im = backward_ref[t, 1, 3 * s + c].astype(jnp.float32)
+                    term_re = b_re * f_re[c] + b_im * f_im[c]
+                    term_im = b_re * f_im[c] - b_im * f_re[c]
+                    acc_re = term_re if acc_re is None else acc_re + term_re
+                    acc_im = term_im if acc_im is None else acc_im + term_im
+                base = (s * 4 + u) * 2 * rows
+                pair_ref[base : base + rows, :] = acc_re
+                pair_ref[base + rows : base + 2 * rows, :] = acc_im
+        out_ref[t] = jnp.dot(
+            mix_ref[...], pair_ref[...], precision=HIGHEST, preferred_element_type=jnp.float32
+        )
+
+
+def contract(forward_prop, backward_prop, gamma_table):
+    slices = forward_prop.shape[0]
+    rows_x = forward_prop.shape[4]
+    sites = forward_prop.shape[5]
+    inserts = gamma_table.shape[0]
+    forward = forward_prop.reshape(slices, 2, 12, 12 * rows_x, sites)
+    backward = backward_prop.reshape(slices, 2, 12, 12 * rows_x, sites)
+    mat_re, mat_im = gamma_matrices(gamma_table)
+    mix = jnp.stack([jnp.stack([mat_re, -mat_im], 2), jnp.stack([mat_im, mat_re], 2)], 1)
+    keep = jnp.eye(rows_x, dtype=jnp.float32)
+    mix = jnp.einsum("gasr,xy->gaxsry", mix, keep)[:, :, :, :, :, None, :]
+    mix = jnp.broadcast_to(
+        mix, (inserts, 2, rows_x, 16, 2, 12, rows_x)
+    ).reshape(inserts * 2 * rows_x, 16 * 2 * 12 * rows_x)
+    out = pl.pallas_call(
+        contract_kernel,
+        out_shape=jax.ShapeDtypeStruct((slices, inserts * 2 * rows_x, sites), jnp.float32),
+        in_specs=[pl.BlockSpec(memory_space=pltpu.VMEM)] * 3,
+        out_specs=pl.BlockSpec(memory_space=pltpu.VMEM),
+        scratch_shapes=[pltpu.VMEM((16 * 2 * 12 * rows_x, sites), jnp.float32)],
+    )(mix, forward, backward)
+    return out.reshape(slices, inserts, 2, rows_x, sites).transpose(1, 0, 2, 3, 4)
+
+
 def body(forward_prop, backward_prop, gamma_table, source_site, momenta):
     slices = forward_prop.shape[0]
     rows_x = forward_prop.shape[4]
     rows_y = backward_prop.shape[5] // LZ
     inserts = gamma_table.shape[0]
-    forward = forward_prop.reshape(slices, 2, 4, 3, 12, -1)
-    backward = backward_prop.reshape(slices, 2, 4, 3, 12, -1)
-    pattern = "tscjn,tucjn->sutn"
-    pair_re = jnp.einsum(
-        pattern, backward[:, 0], forward[:, 0], preferred_element_type=jnp.float32
-    ) + jnp.einsum(pattern, backward[:, 1], forward[:, 1], preferred_element_type=jnp.float32)
-    pair_im = jnp.einsum(
-        pattern, backward[:, 0], forward[:, 1], preferred_element_type=jnp.float32
-    ) - jnp.einsum(pattern, backward[:, 1], forward[:, 0], preferred_element_type=jnp.float32)
-    pair_re = pair_re.reshape(16, slices, -1)
-    pair_im = pair_im.reshape(16, slices, -1)
-    mat_re, mat_im = gamma_matrices(gamma_table)
-    field_re, field_im = apply_gammas(mat_re, mat_im, pair_re, pair_im)
-    fields = jnp.stack([field_re, field_im], 2).reshape(inserts * slices, 2, rows_x, rows_y, LZ)
+    fields = contract(forward_prop, backward_prop, gamma_table)
+    fields = fields.reshape(inserts * slices, 2, rows_x, rows_y, LZ)
     count = fields.shape[0]
     local_re, local_im = project_sites(fields, source_site, momenta, rows_x, rows_y, L, LZ)
     partial = jnp.stack([local_re, local_im], 0)

time: 134 us -> 117 us (0.87)
  matrix products: 26.1 us -> 3.25 us
  Pallas kernels: 0 us -> 3.72 us
  local copies, waits for them, and re-layouts: 40.1 us -> 41.8 us
    dot_general x8 -> x0, matrix products: 22.8 us -> none  [the longest x1 7.53 us: body(): jnp.einsum(pattern, backward[:, 0], forward[:, 1], preferred_element_type...]
    unnamed x17 -> x9, local copies, waits for them, and re-layouts: 19.1 us -> 0.17 us
    reshape x2 -> x7, local copies, waits for them, and re-layouts: 4.89 us -> 23.3 us  [the longest x2 20 us: contract(): mix = jnp.broadcast_to(mix, (inserts, 2, rows_x, 16, 2, 12, rows_x)).resh...]
    broadcast_in_dim x0 -> x1, local copies, waits for them, and re-layouts: none -> 8.15 us  [contract(): jnp.broadcast_to(mix, (inserts, 2, rows_x, 16, 2, 12, rows_x))]
    pallas_call x0 -> x1, Pallas kernels: none -> 3.72 us  [contract(): pl.pallas_call(contract_kernel, out_shape=jax.ShapeDtypeStruct((slices, i...]
    slice x2 -> x1, local copies, waits for them, and re-layouts: 2.92 us -> 0.02 us  [project_sites(): field_re = fields[:, 0].reshape(fields.shape[0], -1)]
    add x1 -> x0, local copies, waits for them, and re-layouts: 2.07 us -> none  [body(): jnp.einsum(pattern, backward[:, 0], forward[:, 0], preferred_element_type...]
    sub x1 -> x0, local copies, waits for them, and re-layouts: 1.93 us -> none  [body(): jnp.einsum(pattern, backward[:, 0], forward[:, 1], preferred_element_type...]
  transfers between devices with their start and end apart: 2 -> 2, of which waited for: 2 -> 2; matrix products, arithmetic and copies ran while one was open for 1% -> 2% of each run, Pallas kernels for 0% -> 0%
where the time goes in v2:
time: 117 us; the launch traced here: 116 us
  local copies, waits for them, and re-layouts  41.8 us (36%)
  waiting for transfers between devices  32 us (27%)
  starting transfers between devices  26.4 us (23%)
  other arithmetic  7.49 us (6%)
  Pallas kernels  3.72 us (3%)
  matrix products  3.25 us (3%)
    all_to_all x2, waiting for transfers between devices, exchange(): lax.all_to_all(jnp.concatenate([blocks, extra], 1), axis, 0, 0, tiled=True)  32 us
    all_to_all x2, starting transfers between devices, exchange(): lax.all_to_all(jnp.concatenate([blocks, extra], 1), axis, 0, 0, tiled=True)  26.4 us
    reshape x2, local copies, waits for them, and re-layouts, contract(): mix = jnp.broadcast_to(mix, (inserts, 2, rows_x, 16, 2, 12, rows_x)).resh...  20 us
    broadcast_in_dim x1, local copies, waits for them, and re-layouts, contract(): jnp.broadcast_to(mix, (inserts, 2, rows_x, 16, 2, 12, rows_x))  8.15 us
    pallas_call x1, Pallas kernels, contract(): pl.pallas_call(contract_kernel, out_shape=jax.ShapeDtypeStruct((slices, i...  3.72 us
    all_to_all x3, local copies, waits for them, and re-layouts, exchange(): lax.all_to_all(jnp.concatenate([blocks, extra], 1), axis, 0, 0, tiled=True)  2.6 us
  transfers between devices with their start and end apart: 2, of which 2 were waited for; matrix products, arithmetic and copies ran while one was open for 2% of the time, Pallas kernels for 0%

profile of v2, /device:TPU:1, one launch (start us, length us, event | category | flops | bytes accessed | tf_op | source)
XLA Modules:
  0.0 115.7 jit_solution(17044088292315405830)
XLA Ops:
  0.6 0.7 fusion.56
  1.3 0.7 slice.50
  2.2 0.3 copy.27
  2.5 0.8 multiply_bitcast_fusion
  3.3 8.1 %broadcast_in_dim.8 = f32[16,2,2,16,2,12,2]{2,1,0,6,5,4,3:T(2,128)} broadcast(f32[16,2,2,16,2,2]{2,1,0,5,4,3:T(2,128)S(1)} %multiply_bitcast_fusion), dimensions={0,1,2,3,4,6} | broadcast | bytes 212992 | tf_op jit(solution)/shard_map/broadcast_in_dim | solution.py:129
  11.4 19.1 %reshape.754 = f32[64,768]{0,1:T(8,128)S(1)} reshape(f32[16,2,2,16,2,12,2]{2,1,0,6,5,4,3:T(2,128)} %broadcast_in_dim.8) | data formatting | bytes 393216 | tf_op jit(solution)/shard_map/reshape | solution.py:131
  30.6 0.8 copy.28.mix_ref
  31.4 1.0 reshape.755.forward_ref
  32.5 1.0 reshape.756.backward_ref
  33.5 3.7 %shard_map.68 = f32[2,64,256]{2,1,0:T(8,128)} custom-call(f32[64,768]{1,0:T(8,128)} %copy.28.mix_ref, bf16[2,2,12,24,256]{4,3,2,1,0:T(8,128)(2,1)} %reshape.755.forward_ref, bf16[2,2,12,24,256]{4,3,2,1,0:T(8,128)(2,1)} %reshape.756.backward_ref), custom_call_target="tpu_custom_call" | custom-call | tf_op jit(solution)/shard_map/pallas_call | solution.py:132
  37.2 1.0 reshape.757
  38.2 0.2 reshape.758
  38.6 0.7 fusion.66
  39.3 0.6 add_subtract_fusion.1
  40.1 0.7 and_select_fusion.2
  40.8 0.7 add_subtract_fusion
  41.8 1.1 add_sine_fusion
  43.2 0.2 fusion.67
  43.4 0.2 fusion.68
  43.6 0.2 fusion.1
  43.8 0.2 fusion
  44.1 0.2 fusion.52
  44.4 0.4 convolution_bitcast_fusion.2
  44.8 0.2 copy.31
  45.0 1.1 copy.32
  46.1 0.3 copy.34
  46.5 1.0 all_to_all.16
  47.5 9.0 %all-to-all-start = ((f32[16,1,4096]{2,1,0:T(1,128)}), f32[16,1,4096]{2,1,0:T(1,128)S(1)}, u32[]{:S(2)}, u32[]{:S(2)}) async-start(f32[16,1,4096]{2,1,0:T(1,128)} %all_to_all.16), calls=%async_computation | async-start | bytes 524288 | tf_op jit(solution)/shard_map/all_to_all | solution.py:50
  56.5 0.7 add_select_fusion.5
  57.2 0.2 fusion.54
  57.4 8.7 %all-to-all-done = f32[16,1,4096]{2,1,0:T(1,128)S(1)} async-done(((f32[16,1,4096]{2,1,0:T(1,128)}), f32[16,1,4096]{2,1,0:T(1,128)S(1)}, u32[]{:S(2)}, u32[]{:S(2)}) %all-to-all-start) | async-done | bytes 262176 | tf_op jit(solution)/shard_map/all_to_all | solution.py:50
  66.3 0.3 copy.35
  66.6 0.6 copy.36
  67.2 1.0 convolution_bitcast_fusion.1
  68.2 0.2 copy.37
  68.5 0.5 copy.38
  69.0 0.2 copy.39
  69.2 1.0 all_to_all.19
  70.3 17.4 %all-to-all-start.1 = ((f32[32,1,3072]{2,1,0:T(1,128)}), f32[32,1,3072]{2,1,0:T(1,128)S(1)}, u32[]{:S(2)}, u32[]{:S(2)}) async-start(f32[32,1,3072]{2,1,0:T(1,128)} %all_to_all.19), calls=%async_computation.1 | async-start | bytes 786432 | tf_op jit(solution)/shard_map/all_to_all | solution.py:50
  87.7 0.7 and_select_fusion.3
  88.3 0.2 fusion.53
  88.6 23.4 %all-to-all-done.1 = f32[32,1,3072]{2,1,0:T(1,128)S(1)} async-done(((f32[32,1,3072]{2,1,0:T(1,128)}), f32[32,1,3072]{2,1,0:T(1,128)S(1)}, u32[]{:S(2)}, u32[]{:S(2)}) %all-to-all-start.1) | async-done | bytes 393248 | tf_op jit(solution)/shard_map/all_to_all | solution.py:50
  111.9 0.6 copy.40
  112.6 0.3 slice_reduce_fusion
  112.9 1.0 convolution_bitcast_fusion
  114.0 0.2 copy.42
  114.1 0.9 reshape.765
  115.0 0.7 reshape_reshape.4
  (40 shorter events, 1.6 us)
Async XLA Ops:
  11.4 20.0 %copy-start = (bf16[2,2,12,12,2,256]{5,4,3,2,1,0:T(2,128)(2,1)S(1)}, bf16[2,2,12,12,2,256]{5,4,3,2,1,0:T(2,128)(2,1)}, u32[]{:S(2)}) copy-start(bf16[2,2,12,12,2,256]{5,4,3,2,1,0:T(2,128)(2,1)} %param.5) | copy-start | bytes 1769476
  30.6 1.9 %copy-start.1 = (bf16[2,2,12,12,2,256]{5,4,3,2,1,0:T(2,128)(2,1)S(1)}, bf16[2,2,12,12,2,256]{5,4,3,2,1,0:T(2,128)(2,1)}, u32[]{:S(2)}) copy-start(bf16[2,2,12,12,2,256]{5,4,3,2,1,0:T(2,128)(2,1)} %param.6) | copy-start | bytes 1769476
  33.5 5.1 %copy-start.2 = (s32[3]{0:T(128)S(1)}, s32[3]{0:T(128)}, u32[]{:S(2)}) copy-start(s32[3]{0:T(128)} %param.8) | copy-start | bytes 40
  33.5 5.8 %copy-start.3 = (s32[32,3]{0,1:T(4,128)S(1)}, s32[32,3]{0,1:T(4,128)}, u32[]{:S(2)}) copy-start(s32[32,3]{0,1:T(4,128)} %param.9) | copy-start | bytes 1156
  47.5 18.6 %all-to-all-start = ((f32[16,1,4096]{2,1,0:T(1,128)}), f32[16,1,4096]{2,1,0:T(1,128)S(1)}, u32[]{:S(2)}, u32[]{:S(2)}) async-start(f32[16,1,4096]{2,1,0:T(1,128)} %all_to_all.16), calls=%async_computation | async-start | bytes 524288 | tf_op jit(solution)/shard_map/all_to_all | solution.py:50
  70.3 41.7 %all-to-all-start.1 = ((f32[32,1,3072]{2,1,0:T(1,128)}), f32[32,1,3072]{2,1,0:T(1,128)S(1)}, u32[]{:S(2)}, u32[]{:S(2)}) async-start(f32[32,1,3072]{2,1,0:T(1,128)} %all_to_all.19), calls=%async_computation.1 | async-start | bytes 786432 | tf_op jit(solution)/shard_map/all_to_all | solution.py:50

commit v3 on v2

--- a/solution.py
+++ b/solution.py
@@ -110,9 +110,21 @@
                 base = (s * 4 + u) * 2 * rows
                 pair_ref[base : base + rows, :] = acc_re
                 pair_ref[base + rows : base + 2 * rows, :] = acc_im
-        out_ref[t] = jnp.dot(
-            mix_ref[...], pair_ref[...], precision=HIGHEST, preferred_element_type=jnp.float32
+        width = pair_ref.shape[0]
+        kinds = mix_ref.shape[1]
+        lines = out_ref.shape[1] * kinds
+        row = lax.broadcasted_iota(jnp.int32, (lines, width), 0)
+        col = lax.broadcasted_iota(jnp.int32, (lines, width), 1)
+        pick = jnp.logical_and(row % kinds == col // rows, row // kinds == col % out_ref.shape[1])
+        summed = jnp.dot(
+            pick.astype(jnp.float32), pair_ref[...], precision=HIGHEST,
+            preferred_element_type=jnp.float32,
         )
+        for x in range(out_ref.shape[1]):
+            out_ref[t, x] = jnp.dot(
+                mix_ref[...], summed[x * kinds : (x + 1) * kinds], precision=HIGHEST,
+                preferred_element_type=jnp.float32,
+            )
 
 
 def contract(forward_prop, backward_prop, gamma_table):
@@ -124,19 +136,15 @@
     backward = backward_prop.reshape(slices, 2, 12, 12 * rows_x, sites)
     mat_re, mat_im = gamma_matrices(gamma_table)
     mix = jnp.stack([jnp.stack([mat_re, -mat_im], 2), jnp.stack([mat_im, mat_re], 2)], 1)
-    keep = jnp.eye(rows_x, dtype=jnp.float32)
-    mix = jnp.einsum("gasr,xy->gaxsry", mix, keep)[:, :, :, :, :, None, :]
-    mix = jnp.broadcast_to(
-        mix, (inserts, 2, rows_x, 16, 2, 12, rows_x)
-    ).reshape(inserts * 2 * rows_x, 16 * 2 * 12 * rows_x)
+    mix = mix.reshape(inserts * 2, 16 * 2)
     out = pl.pallas_call(
         contract_kernel,
-        out_shape=jax.ShapeDtypeStruct((slices, inserts * 2 * rows_x, sites), jnp.float32),
+        out_shape=jax.ShapeDtypeStruct((slices, rows_x, inserts * 2, sites), jnp.float32),
         in_specs=[pl.BlockSpec(memory_space=pltpu.VMEM)] * 3,
         out_specs=pl.BlockSpec(memory_space=pltpu.VMEM),
         scratch_shapes=[pltpu.VMEM((16 * 2 * 12 * rows_x, sites), jnp.float32)],
     )(mix, forward, backward)
-    return out.reshape(slices, inserts, 2, rows_x, sites).transpose(1, 0, 2, 3, 4)
+    return out.reshape(slices, rows_x, inserts, 2, sites).transpose(2, 0, 3, 1, 4)
 
 
 def body(forward_prop, backward_prop, gamma_table, source_site, momenta):

time: 117 us -> 91 us (0.78)
  local copies, waits for them, and re-layouts: 41.8 us -> 16.3 us
    reshape x4 -> x3, local copies, waits for them, and re-layouts: 21 us -> 1.83 us  [the longest x2 1.08 us: contract(): out.reshape(slices, rows_x, inserts, 2, sites).transpose(2, 0, 3, 1, 4)]
    broadcast_in_dim x1 -> x0, local copies, waits for them, and re-layouts: 8.15 us -> none  [contract(): jnp.broadcast_to(mix, (inserts, 2, rows_x, 16, 2, 12, rows_x))]
where the time goes in v3:
time: 91 us; the launch traced here: 89.6 us
  waiting for transfers between devices  32.2 us (35%)
  starting transfers between devices  26.4 us (29%)
  local copies, waits for them, and re-layouts  16.3 us (18%)
  other arithmetic  6.48 us (7%)
  Pallas kernels  4.11 us (5%)
  matrix products  3.26 us (4%)
  between operations  0.97 us (1%)
    all_to_all x2, waiting for transfers between devices, exchange(): lax.all_to_all(jnp.concatenate([blocks, extra], 1), axis, 0, 0, tiled=True)  32.2 us
    all_to_all x2, starting transfers between devices, exchange(): lax.all_to_all(jnp.concatenate([blocks, extra], 1), axis, 0, 0, tiled=True)  26.4 us
    pallas_call x1, Pallas kernels, contract(): pl.pallas_call(contract_kernel, out_shape=jax.ShapeDtypeStruct((slices, r...  4.11 us
    all_to_all x3, local copies, waits for them, and re-layouts, exchange(): lax.all_to_all(jnp.concatenate([blocks, extra], 1), axis, 0, 0, tiled=True)  2.59 us
    select_n x3, other arithmetic, dft_table(): offsets = jnp.mod(wavenum - anchor, length)  1.9 us
  transfers between devices with their start and end apart: 2, of which 2 were waited for; matrix products, arithmetic and copies ran while one was open for 2% of the time, Pallas kernels for 0%

profile of v3, /device:TPU:1, one launch (start us, length us, event | category | flops | bytes accessed | tf_op | source)
XLA Modules:
  0.0 89.6 jit_solution(9743213956706119184)
XLA Ops:
  0.7 0.8 slice.50
  1.4 0.7 fusion.56
  2.1 1.4 %fusion.66 = (s32[1]{0:T(128)}, s32[1]{0:T(128)}, s32[1]{0:T(128)}) fusion(s32[3]{0:T(128)} %param.8), kind=kLoop, calls=%fused_computation.137 | loop fusion | bytes 24 | tf_op jit(solution)/shard_map/slice | solution.py:177
  3.6 0.7 and_select_fusion.2
  4.2 0.8 slice_bitcast_fusion.2
  5.1 0.5 add_subtract_fusion.1
  5.8 0.2 fusion.52
  6.1 0.7 add_subtract_fusion
  6.9 0.1 fusion.32
  7.0 1.1 %add_sine_fusion = (f32[32,2,4,64]{3,2,1,0:T(4,128)S(1)}, f32[32,2,4,64]{3,2,1,0:T(4,128)S(1)}) fusion(f32[32,64]{1,0:T(8,128)S(1)} %fusion.43, f32[32,2,4]{2,1,0:T(2,128)S(1)} %fusion.32), kind=kLoop, calls=%fused_computation.16 | loop fusion | flops 16384 | bytes 140288 | tf_op jit(solution)/shard_map/sin | solution.py:81
  8.5 0.3 copy.26
  8.9 0.8 reshape.753.mix_ref
  9.6 1.0 %reshape.754.forward_ref = bf16[2,2,12,24,256]{4,3,2,1,0:T(8,128)(2,1)} reshape(bf16[2,2,12,12,2,256]{5,4,3,2,1,0:T(2,128)(2,1)S(1)} %copy-done) | data formatting | bytes 1179648 | tf_op jit(solution)/shard_map/reshape | solution.py:135
  10.7 1.0 %reshape.755.backward_ref = bf16[2,2,12,24,256]{4,3,2,1,0:T(8,128)(2,1)} reshape(bf16[2,2,12,12,2,256]{5,4,3,2,1,0:T(2,128)(2,1)S(1)} %copy-done.1) | data formatting | bytes 1179648 | tf_op jit(solution)/shard_map/reshape | solution.py:136
  11.7 4.1 %shard_map.68 = f32[2,2,32,256]{3,2,1,0:T(8,128)} custom-call(f32[32,32]{1,0:T(8,128)} %reshape.753.mix_ref, bf16[2,2,12,24,256]{4,3,2,1,0:T(8,128)(2,1)} %reshape.754.forward_ref, bf16[2,2,12,24,256]{4,3,2,1,0:T(8,128)(2,1)} %reshape.755.backward_ref), custom_call_target="tpu_custom_call" | custom-call | tf_op jit(solution)/shard_map/pallas_call | solution.py:140
  15.8 1.0 %reshape.756 = f32[2,2,16,2,256]{4,3,2,1,0:T(2,128)S(1)} reshape(f32[2,2,32,256]{3,2,1,0:T(8,128)} %shard_map.68) | data formatting | bytes 262144 | tf_op jit(solution)/shard_map/reshape | solution.py:147
  16.9 0.2 reshape.757
  17.4 0.2 fusion.67
  17.6 0.2 fusion.68
  17.8 0.2 fusion.1
  18.0 0.2 fusion
  18.3 0.4 convolution_bitcast_fusion.2
  18.7 0.2 copy.29
  18.9 1.1 %copy.30 = f32[16,32,2,2,4,4]{0,5,4,3,2,1:T(4,128)S(1)} copy(f32[16,32,2,2,4,4]{1,5,0,4,3,2:T(4,128)S(1)} %bitcast.103) | data formatting | bytes 262144 | tf_op jit(solution)/shard_map/transpose | solution.py:167
  20.1 0.3 copy.32
  20.4 1.0 %all_to_all.16 = f32[16,1,4096]{2,1,0:T(1,128)} reshape(f32[16,4096]{1,0:T(8,128)S(1)} %pad_maximum_fusion.1) | data formatting | bytes 524288 | tf_op jit(solution)/shard_map/all_to_all | solution.py:50
  21.4 9.0 %all-to-all-start = ((f32[16,1,4096]{2,1,0:T(1,128)}), f32[16,1,4096]{2,1,0:T(1,128)S(1)}, u32[]{:S(2)}, u32[]{:S(2)}) async-start(f32[16,1,4096]{2,1,0:T(1,128)} %all_to_all.16), calls=%async_computation | async-start | bytes 524288 | tf_op jit(solution)/shard_map/all_to_all | solution.py:50
  30.4 0.7 add_select_fusion.5
  31.1 0.2 fusion.54
  31.3 8.7 %all-to-all-done = f32[16,1,4096]{2,1,0:T(1,128)S(1)} async-done(((f32[16,1,4096]{2,1,0:T(1,128)}), f32[16,1,4096]{2,1,0:T(1,128)S(1)}, u32[]{:S(2)}, u32[]{:S(2)}) %all-to-all-start) | async-done | bytes 262176 | tf_op jit(solution)/shard_map/all_to_all | solution.py:50
  40.0 0.2 copy.58
  40.2 0.3 copy.33
  40.5 0.6 copy.34
  41.1 1.0 %convolution_bitcast_fusion.1 = f32[32,2,2,64,4]{3,0,4,2,1:T(8,128)S(1)} fusion(f32[16,32,2,2,4,4]{1,0,4,2,5,3:T(8,128)S(1)} %copy.34, f32[1,16,4,1,64]{4,1,2,0,3:T(8,128)S(1)} %get-tuple-element.19, f32[1,16,4,1,64]{4,1,2,0,3:T(8,128)S(1)} %get-tuple-element.18, f32[1,16,4,1,64]{4,1,2,0,3:T(8,128)S(1)} %get-tuple-element.17), kind=kOutput, calls=%fused_computation.1 | convolution fusion | flops 50380800 | bytes 311296 | tf_op jit(solution)/shard_map/jnrxyc,rjysk->nsxkc/dot_general | solution.py:171
  42.2 0.2 copy.35
  42.4 0.5 copy.36
  43.0 0.2 copy.37
  43.2 1.0 %all_to_all.19 = f32[32,1,3072]{2,1,0:T(1,128)} reshape(f32[32,3072]{1,0:T(8,128)S(1)} %pad_maximum_fusion) | data formatting | bytes 786432 | tf_op jit(solution)/shard_map/all_to_all | solution.py:50
  44.2 17.4 %all-to-all-start.1 = ((f32[32,1,3072]{2,1,0:T(1,128)}), f32[32,1,3072]{2,1,0:T(1,128)S(1)}, u32[]{:S(2)}, u32[]{:S(2)}) async-start(f32[32,1,3072]{2,1,0:T(1,128)} %all_to_all.19), calls=%async_computation.1 | async-start | bytes 786432 | tf_op jit(solution)/shard_map/all_to_all | solution.py:50
  61.6 0.6 and_select_fusion.3
  62.2 0.2 fusion.53
  62.4 23.5 %all-to-all-done.1 = f32[32,1,3072]{2,1,0:T(1,128)S(1)} async-done(((f32[32,1,3072]{2,1,0:T(1,128)}), f32[32,1,3072]{2,1,0:T(1,128)S(1)}, u32[]{:S(2)}, u32[]{:S(2)}) %all-to-all-start.1) | async-done | bytes 393248 | tf_op jit(solution)/shard_map/all_to_all | solution.py:50
  85.8 0.6 copy.38
  86.5 0.3 slice_reduce_fusion
  86.9 1.0 %convolution_bitcast_fusion = f32[32,2,2,4,64]{4,0,3,2,1:T(8,128)S(1)} fusion(f32[32,32,2,2,2,4]{0,5,4,3,2,1:T(4,128)S(1)} %bitcast.104, f32[1,32,2,1,64]{4,1,2,0,3:T(8,128)S(1)} %get-tuple-element.25, f32[1,32,2,1,64]{4,1,2,0,3:T(8,128)S(1)} %get-tuple-element.24, f32[1,32,2,1,64]{4,1,2,0,3:T(8,128)S(1)} %get-tuple-element.23), kind=kOutput, calls=%fused_computation | convolution fusion | flops 50380800 | bytes 311296 | tf_op jit(solution)/shard_map/inrxbc,rixsk->nsbck/dot_general | solution.py:178
  87.9 0.2 copy.40
  88.1 0.9 reshape.764
  88.9 0.7 reshape_reshape.4
  (32 shorter events, 1.4 us)
Async XLA Ops:
  0.6 9.0 %copy-start = (bf16[2,2,12,12,2,256]{5,4,3,2,1,0:T(2,128)(2,1)S(1)}, bf16[2,2,12,12,2,256]{5,4,3,2,1,0:T(2,128)(2,1)}, u32[]{:S(2)}) copy-start(bf16[2,2,12,12,2,256]{5,4,3,2,1,0:T(2,128)(2,1)} %param.5) | copy-start | bytes 1769476
  0.6 10.0 %copy-start.1 = (bf16[2,2,12,12,2,256]{5,4,3,2,1,0:T(2,128)(2,1)S(1)}, bf16[2,2,12,12,2,256]{5,4,3,2,1,0:T(2,128)(2,1)}, u32[]{:S(2)}) copy-start(bf16[2,2,12,12,2,256]{5,4,3,2,1,0:T(2,128)(2,1)} %param.6) | copy-start | bytes 1769476
  21.4 18.6 %all-to-all-start = ((f32[16,1,4096]{2,1,0:T(1,128)}), f32[16,1,4096]{2,1,0:T(1,128)S(1)}, u32[]{:S(2)}, u32[]{:S(2)}) async-start(f32[16,1,4096]{2,1,0:T(1,128)} %all_to_all.16), calls=%async_computation | async-start | bytes 524288 | tf_op jit(solution)/shard_map/all_to_all | solution.py:50
  44.2 41.7 %all-to-all-start.1 = ((f32[32,1,3072]{2,1,0:T(1,128)}), f32[32,1,3072]{2,1,0:T(1,128)S(1)}, u32[]{:S(2)}, u32[]{:S(2)}) async-start(f32[32,1,3072]{2,1,0:T(1,128)} %all_to_all.19), calls=%async_computation.1 | async-start | bytes 786432 | tf_op jit(solution)/shard_map/all_to_all | solution.py:50

commit v4 on v3

--- a/solution.py
+++ b/solution.py
@@ -1,3 +1,4 @@
+import functools
 import math
 
 import jax
@@ -43,11 +44,74 @@
     return jnp.stack([rows_re, rows_im], 0)
 
 
-def exchange(blocks, shared, axis):
+def swap_kernel(axis, blocks_ref, out_ref, send_sem, recv_sem):
+    parts = blocks_ref.shape[0]
+    me = lax.axis_index(axis)
+    mesh_ids = pl.DeviceIdType.MESH
+    barrier = pltpu.get_barrier_semaphore()
+    for step in range(1, parts):
+        pl.semaphore_signal(
+            barrier, 1, device_id={axis: lax.rem(me + step, parts)}, device_id_type=mesh_ids
+        )
+    pl.semaphore_wait(barrier, parts - 1)
+
+    def copy_to(step):
+        peer = lax.rem(me + step, parts)
+        return pltpu.make_async_remote_copy(
+            src_ref=blocks_ref.at[peer],
+            dst_ref=out_ref.at[me],
+            send_sem=send_sem.at[step],
+            recv_sem=recv_sem.at[step],
+            device_id={axis: peer},
+            device_id_type=mesh_ids,
+        )
+
+    def copy_from(step):
+        source = lax.rem(me + parts - step, parts)
+        return pltpu.make_async_remote_copy(
+            src_ref=blocks_ref.at[source],
+            dst_ref=out_ref.at[source],
+            send_sem=send_sem.at[step],
+            recv_sem=recv_sem.at[step],
+            device_id={axis: source},
+            device_id_type=mesh_ids,
+        )
+
+    @pl.loop(1, parts)
+    def _(step):
+        copy_to(step).start()
+
+    out_ref[me] = blocks_ref[me]
+
+    @pl.loop(1, parts)
+    def _(step):
+        copy_to(step).wait_send()
+
+    @pl.loop(1, parts)
+    def _(step):
+        copy_from(step).wait_recv()
+
+
+def swap(blocks, axis, ident):
+    parts = blocks.shape[0]
+    lanes = 128
+    shaped = blocks.reshape(parts, -1, lanes)
+    out = pl.pallas_call(
+        functools.partial(swap_kernel, axis),
+        out_shape=jax.ShapeDtypeStruct(shaped.shape, shaped.dtype),
+        in_specs=[pl.BlockSpec(memory_space=pltpu.VMEM)],
+        out_specs=pl.BlockSpec(memory_space=pltpu.VMEM),
+        scratch_shapes=[pltpu.SemaphoreType.DMA((parts,)), pltpu.SemaphoreType.DMA((parts,))],
+        compiler_params=pltpu.CompilerParams(collective_id=ident, has_side_effects=True),
+    )(shaped)
+    return out.reshape(blocks.shape)
+
+
+def exchange(blocks, shared, axis, ident):
     parts = blocks.shape[0]
     width = blocks.shape[1]
     extra = jnp.broadcast_to(shared.reshape(1, -1), (parts, shared.size))
-    got = lax.all_to_all(jnp.concatenate([blocks, extra], 1), axis, 0, 0, tiled=True)
+    got = swap(jnp.concatenate([blocks, extra], 1), axis, ident)
     return got[:, :width], got[:, width:].sum(0).reshape(shared.shape)
 
 
@@ -165,14 +229,14 @@
     share_z = LZ // groups_y
     blocks = along_z.reshape(count, 2, rows_x, rows_y, groups_y, share_z)
     blocks = blocks.transpose(4, 0, 1, 2, 3, 5).reshape(groups_y, -1)
-    blocks, partial = exchange(blocks, partial, "sy")
+    blocks, partial = exchange(blocks, partial, "sy", 0)
     blocks = blocks.reshape(groups_y, count, 2, rows_x, rows_y, share_z)
     table_y = dft_matrix(rows_y * groups_y, source_site[1]).reshape(2, groups_y, rows_y, 2, -1)
     along_y = jnp.einsum("jnrxyc,rjysk->nsxkc", blocks, table_y, precision=HIGHEST)
     share_y = along_y.shape[3] // groups_x
     blocks = along_y.reshape(count, 2, rows_x, groups_x, share_y, share_z)
     blocks = blocks.transpose(3, 0, 1, 2, 4, 5).reshape(groups_x, -1)
-    blocks, partial = exchange(blocks, partial, "sx")
+    blocks, partial = exchange(blocks, partial, "sx", 1)
     blocks = blocks.reshape(groups_x, count, 2, rows_x, share_y, share_z)
     table_x = dft_matrix(rows_x * groups_x, source_site[0]).reshape(2, groups_x, rows_x, 2, -1)
     spectrum = jnp.einsum("inrxbc,rixsk->nsbck", blocks, table_x, precision=HIGHEST)

time: 91 us -> 84.7 us (0.931)
  Pallas kernels: 4.11 us -> 56.7 us
  waiting for transfers between devices: 32.2 us -> 0 us
  starting transfers between devices: 26.4 us -> 0 us
    pallas_call x0 -> x2, Pallas kernels: none -> 52.6 us  [swap(): pl.pallas_call(functools.partial(swap_kernel, axis), out_shape=jax.ShapeD...]
    all_to_all x2 -> x0, waiting for transfers between devices: 32.2 us -> none  [exchange(): lax.all_to_all(jnp.concatenate([blocks, extra], 1), axis, 0, 0, tiled=True)]
    all_to_all x2 -> x0, starting transfers between devices: 26.4 us -> none  [exchange(): lax.all_to_all(jnp.concatenate([blocks, extra], 1), axis, 0, 0, tiled=True)]
    unnamed x5 -> x13, local copies, waits for them, and re-layouts: 0.16 us -> 4.1 us
    all_to_all x3 -> x0, local copies, waits for them, and re-layouts: 2.59 us -> none  [exchange(): lax.all_to_all(jnp.concatenate([blocks, extra], 1), axis, 0, 0, tiled=True)]
  transfers between devices with their start and end apart: 2 -> 0, of which waited for: 2 -> 0; matrix products, arithmetic and copies ran while one was open for 2% -> 0% of each run, Pallas kernels for 0% -> 0%
where the time goes in v4:
time: 84.7 us; the launch traced here: 83.5 us
  Pallas kernels  56.7 us (67%)
  local copies, waits for them, and re-layouts  15.6 us (18%)
  other arithmetic  7.09 us (8%)
  matrix products  3.25 us (4%)
  between operations  0.96 us (1%)
    pallas_call x2, Pallas kernels, swap(): pl.pallas_call(functools.partial(swap_kernel, axis), out_shape=jax.ShapeD...  52.6 us
    pallas_call x1, Pallas kernels, contract(): pl.pallas_call(contract_kernel, out_shape=jax.ShapeDtypeStruct((slices, r...  4.11 us
    unnamed x13, local copies, waits for them, and re-layouts  4.1 us
    select_n x3, other arithmetic, dft_table(): offsets = jnp.mod(wavenum - anchor, length)  1.97 us

profile of v4, /device:TPU:1, one launch (start us, length us, event | category | flops | bytes accessed | tf_op | source)
XLA Modules:
  0.0 83.5 jit_solution(4729447672512168987)
XLA Ops:
  0.6 0.8 fusion.56
  1.4 0.7 slice.50
  2.3 0.3 copy.16
  2.7 0.8 reshape.765.mix_ref
  3.4 1.0 %reshape.766.forward_ref = bf16[2,2,12,24,256]{4,3,2,1,0:T(8,128)(2,1)} reshape(bf16[2,2,12,12,2,256]{5,4,3,2,1,0:T(2,128)(2,1)S(1)} %copy-done) | data formatting | bytes 1179648 | tf_op jit(solution)/shard_map/reshape | solution.py:199
  4.5 1.0 %reshape.767.backward_ref = bf16[2,2,12,24,256]{4,3,2,1,0:T(8,128)(2,1)} reshape(bf16[2,2,12,12,2,256]{5,4,3,2,1,0:T(2,128)(2,1)S(1)} %copy-done.1) | data formatting | bytes 1179648 | tf_op jit(solution)/shard_map/reshape | solution.py:200
  5.5 4.1 %shard_map.68 = f32[2,2,32,256]{3,2,1,0:T(8,128)} custom-call(f32[32,32]{1,0:T(8,128)} %reshape.765.mix_ref, bf16[2,2,12,24,256]{4,3,2,1,0:T(8,128)(2,1)} %reshape.766.forward_ref, bf16[2,2,12,24,256]{4,3,2,1,0:T(8,128)(2,1)} %reshape.767.backward_ref), custom_call_target="tpu_custom_call" | custom-call | tf_op jit(solution)/shard_map/pallas_call | solution.py:204
  9.6 1.0 %reshape.768 = f32[2,2,16,2,256]{4,3,2,1,0:T(2,128)S(1)} reshape(f32[2,2,32,256]{3,2,1,0:T(8,128)} %shard_map.68) | data formatting | bytes 262144 | tf_op jit(solution)/shard_map/reshape | solution.py:211
  10.7 0.2 reshape.769
  11.0 0.1 reshape_squeeze.6
  11.1 0.5 copy-done.2
  11.6 0.6 fusion.66
  12.3 0.7 add_subtract_fusion.1
  13.1 0.6 add_subtract_fusion
  13.8 0.1 fusion.32
  14.0 0.7 and_select_fusion.2
  14.7 1.1 %add_sine_fusion = (f32[32,2,4,64]{3,2,1,0:T(4,128)S(1)}, f32[32,2,4,64]{3,2,1,0:T(4,128)S(1)}) fusion(f32[32,64]{1,0:T(8,128)S(1)} %fusion.43, f32[32,2,4]{2,1,0:T(2,128)S(1)} %fusion.32), kind=kLoop, calls=%fused_computation.17 | loop fusion | flops 16384 | bytes 140288 | tf_op jit(solution)/shard_map/sin | solution.py:145
  15.8 0.1 cos.54
  16.0 0.2 fusion.67
  16.4 0.2 fusion.1
  16.6 0.2 fusion.68
  16.8 0.2 fusion
  17.1 0.2 fusion.52
  17.3 0.4 convolution_bitcast_fusion.2
  17.8 0.2 copy.19
  18.0 1.1 %copy.20 = f32[16,32,2,2,4,4]{0,5,4,3,2,1:T(4,128)S(1)} copy(f32[16,32,2,2,4,4]{1,5,0,4,3,2:T(4,128)S(1)} %bitcast.109) | data formatting | bytes 262144 | tf_op jit(solution)/shard_map/transpose | solution.py:231
  19.1 0.3 copy.22
  19.4 0.7 pad_maximum_fusion.blocks_ref
  20.2 16.5 %shard_map.69 = f32[16,32,128]{2,1,0:T(8,128)} custom-call(f32[16,32,128]{2,1,0:T(8,128)} %pad_maximum_fusion.blocks_ref), custom_call_target="tpu_custom_call" | custom-call | tf_op jit(solution)/shard_map/pallas_call | solution.py:99
  36.6 1.1 %copy.54 = f32[2,8,32,128]{3,1,2,0:T(8,128)S(1)} copy(f32[2,8,32,128]{3,2,1,0:T(8,128)} %bitcast.117) | data formatting | bytes 524288
  37.8 0.3 copy.37
  38.1 0.6 copy.24
  38.7 0.6 add_select_fusion.5
  39.4 0.2 fusion.54
  39.6 1.0 %convolution_bitcast_fusion.1 = f32[32,2,2,64,4]{3,0,4,2,1:T(8,128)S(1)} fusion(f32[16,32,2,2,4,4]{1,0,4,2,5,3:T(8,128)S(1)} %copy.24, f32[1,16,4,1,64]{4,1,2,0,3:T(8,128)S(1)} %get-tuple-element.19, f32[1,16,4,1,64]{4,1,2,0,3:T(8,128)S(1)} %get-tuple-element.18, f32[1,16,4,1,64]{4,1,2,0,3:T(8,128)S(1)} %get-tuple-element.17), kind=kOutput, calls=%fused_computation.1 | convolution fusion | flops 50380800 | bytes 311296 | tf_op jit(solution)/shard_map/jnrxyc,rjysk->nsxkc/dot_general | solution.py:235
  40.6 0.2 copy.25
  40.8 0.5 copy.26
  41.4 0.2 copy.27
  41.6 0.8 copy.40
  42.4 36.1 %shard_map.70 = f32[32,24,128]{2,1,0:T(8,128)} custom-call(f32[32,24,128]{2,1,0:T(8,128)} %bitcast.114), custom_call_target="tpu_custom_call" | custom-call | tf_op jit(solution)/shard_map/pallas_call | solution.py:99
  78.5 1.1 %copy.53 = f32[4,8,24,128]{3,1,2,0:T(8,128)S(1)} copy(f32[4,8,24,128]{3,2,1,0:T(8,128)} %bitcast.115) | data formatting | bytes 786432
  79.6 0.2 copy.38
  79.8 0.7 and_select_fusion.3
  80.5 0.2 fusion.53
  80.7 1.0 %convolution_bitcast_fusion = f32[32,2,2,4,64]{4,0,3,2,1:T(8,128)S(1)} fusion(f32[32,32,2,2,2,4]{0,5,4,3,2,1:T(4,128)S(1)} %bitcast.108, f32[1,32,2,1,64]{4,1,2,0,3:T(8,128)S(1)} %get-tuple-element.25, f32[1,32,2,1,64]{4,1,2,0,3:T(8,128)S(1)} %get-tuple-element.24, f32[1,32,2,1,64]{4,1,2,0,3:T(8,128)S(1)} %get-tuple-element.23), kind=kOutput, calls=%fused_computation | convolution fusion | flops 50380800 | bytes 311296 | tf_op jit(solution)/shard_map/inrxbc,rixsk->nsbck/dot_general | solution.py:242
  81.7 0.2 copy.30
  81.9 0.9 %reshape.778 = f32[16,2,2,2,256]{4,3,2,1,0:T(2,128)} reshape(f32[32,2,2,4,64]{4,3,2,1,0:T(4,128)S(1)} %copy.30) | data formatting | bytes 262144 | tf_op jit(solution)/shard_map/reshape | solution.py:243
  82.8 0.7 reshape_reshape.4
  (34 shorter events, 1.2 us)
Async XLA Ops:
  0.6 2.8 %copy-start = (bf16[2,2,12,12,2,256]{5,4,3,2,1,0:T(2,128)(2,1)S(1)}, bf16[2,2,12,12,2,256]{5,4,3,2,1,0:T(2,128)(2,1)}, u32[]{:S(2)}) copy-start(bf16[2,2,12,12,2,256]{5,4,3,2,1,0:T(2,128)(2,1)} %param.5) | copy-start | bytes 1769476
  3.4 1.1 %copy-start.1 = (bf16[2,2,12,12,2,256]{5,4,3,2,1,0:T(2,128)(2,1)S(1)}, bf16[2,2,12,12,2,256]{5,4,3,2,1,0:T(2,128)(2,1)}, u32[]{:S(2)}) copy-start(bf16[2,2,12,12,2,256]{5,4,3,2,1,0:T(2,128)(2,1)} %param.6) | copy-start | bytes 1769476
  11.0 0.7 copy-start.2
  12.3 0.7 copy-start.3

commit v5 on v4

--- a/solution.py
+++ b/solution.py
@@ -107,12 +107,10 @@
     return out.reshape(blocks.shape)
 
 
-def exchange(blocks, shared, axis, ident):
-    parts = blocks.shape[0]
+def exchange(blocks, extra, axis, ident):
     width = blocks.shape[1]
-    extra = jnp.broadcast_to(shared.reshape(1, -1), (parts, shared.size))
     got = swap(jnp.concatenate([blocks, extra], 1), axis, ident)
-    return got[:, :width], got[:, width:].sum(0).reshape(shared.shape)
+    return got[:, :width], got[:, width:].sum(0)
 
 
 def apply_gammas(mat_re, mat_im, real_part, imag_part):
@@ -229,19 +227,22 @@
     share_z = LZ // groups_y
     blocks = along_z.reshape(count, 2, rows_x, rows_y, groups_y, share_z)
     blocks = blocks.transpose(4, 0, 1, 2, 3, 5).reshape(groups_y, -1)
-    blocks, partial = exchange(blocks, partial, "sy", 0)
+    shares = partial.reshape(groups_y, -1)
+    blocks, share = exchange(blocks, shares, "sy", 0)
     blocks = blocks.reshape(groups_y, count, 2, rows_x, rows_y, share_z)
     table_y = dft_matrix(rows_y * groups_y, source_site[1]).reshape(2, groups_y, rows_y, 2, -1)
     along_y = jnp.einsum("jnrxyc,rjysk->nsxkc", blocks, table_y, precision=HIGHEST)
     share_y = along_y.shape[3] // groups_x
     blocks = along_y.reshape(count, 2, rows_x, groups_x, share_y, share_z)
     blocks = blocks.transpose(3, 0, 1, 2, 4, 5).reshape(groups_x, -1)
-    blocks, partial = exchange(blocks, partial, "sx", 1)
+    spread = jnp.broadcast_to(share[None], (groups_x, share.size))
+    blocks, share = exchange(blocks, spread, "sx", 1)
     blocks = blocks.reshape(groups_x, count, 2, rows_x, share_y, share_z)
     table_x = dft_matrix(rows_x * groups_x, source_site[0]).reshape(2, groups_x, rows_x, 2, -1)
     spectrum = jnp.einsum("inrxbc,rixsk->nsbck", blocks, table_x, precision=HIGHEST)
     corr = spectrum.reshape(inserts, slices, 2, share_y, -1)
-    listed = partial.reshape(2, inserts, slices, -1)
+    spread = jnp.broadcast_to(share[None], (groups_y, share.size))
+    listed = swap(spread, "sy", 2).reshape(2, inserts, slices, -1)
     return (corr, listed)
 
 

time: 84.7 us -> 83.6 us (0.987)
  Pallas kernels: 56.7 us -> 53 us
  local copies, waits for them, and re-layouts: 15.6 us -> 17.1 us
    pallas_call x2 -> x3, Pallas kernels: 52.6 us -> 48.9 us  [swap(): pl.pallas_call(functools.partial(swap_kernel, axis), out_shape=jax.ShapeD...]
    reshape x0 -> x5, local copies, waits for them, and re-layouts: none -> 2.4 us  [the longest x3 2.03 us: swap(): shaped = blocks.reshape(parts, -1, lanes)]
    unnamed x13 -> x10, local copies, waits for them, and re-layouts: 4.1 us -> 2.54 us
    pallas_call x0 -> x1, other arithmetic: none -> 1.36 us  [swap(): pl.pallas_call(functools.partial(swap_kernel, axis), out_shape=jax.ShapeD...]
where the time goes in v5:
time: 83.6 us; the launch traced here: 82.2 us
  Pallas kernels  53 us (63%)
  local copies, waits for them, and re-layouts  17.1 us (20%)
  other arithmetic  7.81 us (9%)
  matrix products  3.26 us (4%)
  between operations  0.97 us (1%)
    pallas_call x3, Pallas kernels, swap(): pl.pallas_call(functools.partial(swap_kernel, axis), out_shape=jax.ShapeD...  48.9 us
    pallas_call x1, Pallas kernels, contract(): pl.pallas_call(contract_kernel, out_shape=jax.ShapeDtypeStruct((slices, r...  4.11 us
    unnamed x10, local copies, waits for them, and re-layouts  2.54 us
    reshape x3, local copies, waits for them, and re-layouts, swap(): shaped = blocks.reshape(parts, -1, lanes)  2.03 us
    select_n x3, other arithmetic, dft_table(): offsets = jnp.mod(wavenum - anchor, length)  2.03 us

profile of v5, /device:TPU:1, one launch (start us, length us, event | category | flops | bytes accessed | tf_op | source)
XLA Modules:
  0.0 82.2 jit_solution(2077222076336402127)
XLA Ops:
  0.6 0.8 fusion.56
  1.4 0.7 slice.50
  2.3 0.3 copy.33
  2.7 0.8 reshape.766.mix_ref
  3.4 1.0 %reshape.767.forward_ref = bf16[2,2,12,24,256]{4,3,2,1,0:T(8,128)(2,1)} reshape(bf16[2,2,12,12,2,256]{5,4,3,2,1,0:T(2,128)(2,1)S(1)} %copy-done) | data formatting | bytes 1179648 | tf_op jit(solution)/shard_map/reshape | solution.py:197
  4.5 1.0 %reshape.768.backward_ref = bf16[2,2,12,24,256]{4,3,2,1,0:T(8,128)(2,1)} reshape(bf16[2,2,12,12,2,256]{5,4,3,2,1,0:T(2,128)(2,1)S(1)} %copy-done.1) | data formatting | bytes 1179648 | tf_op jit(solution)/shard_map/reshape | solution.py:198
  5.5 4.1 %shard_map.68 = f32[2,2,32,256]{3,2,1,0:T(8,128)} custom-call(f32[32,32]{1,0:T(8,128)} %reshape.766.mix_ref, bf16[2,2,12,24,256]{4,3,2,1,0:T(8,128)(2,1)} %reshape.767.forward_ref, bf16[2,2,12,24,256]{4,3,2,1,0:T(8,128)(2,1)} %reshape.768.backward_ref), custom_call_target="tpu_custom_call" | custom-call | tf_op jit(solution)/shard_map/pallas_call | solution.py:202
  9.6 1.0 %reshape.769 = f32[2,2,16,2,256]{4,3,2,1,0:T(2,128)S(1)} reshape(f32[2,2,32,256]{3,2,1,0:T(8,128)} %shard_map.68) | data formatting | bytes 262144 | tf_op jit(solution)/shard_map/reshape | solution.py:209
  10.7 0.2 reshape.770
  11.1 0.5 copy-done.2
  11.6 0.7 fusion.66
  12.3 0.7 add_subtract_fusion.1
  13.2 0.7 add_subtract_fusion
  14.1 0.7 and_select_fusion.2
  14.8 1.1 %add_sine_fusion = (f32[32,2,4,64]{3,2,1,0:T(4,128)S(1)}, f32[32,2,4,64]{3,2,1,0:T(4,128)S(1)}) fusion(f32[32,64]{1,0:T(8,128)S(1)} %fusion.43, f32[32,2,4]{2,1,0:T(2,128)S(1)} %fusion.32), kind=kLoop, calls=%fused_computation.12 | loop fusion | flops 16384 | bytes 140288 | tf_op jit(solution)/shard_map/sin | solution.py:143
  16.1 0.2 fusion.67
  16.5 0.2 fusion.1
  16.7 0.2 fusion.68
  16.9 0.2 fusion
  17.2 0.2 fusion.52
  17.4 0.4 convolution_bitcast_fusion.2
  17.9 0.2 copy.36
  18.1 1.1 %copy.37 = f32[16,32,2,2,4,4]{0,5,4,3,2,1:T(4,128)S(1)} copy(f32[16,32,2,2,4,4]{1,5,0,4,3,2:T(4,128)S(1)} %bitcast.106) | data formatting | bytes 262144 | tf_op jit(solution)/shard_map/transpose | solution.py:229
  19.2 0.3 copy.39
  19.5 0.7 reshape.774.blocks_ref
  20.2 12.9 %shard_map.69 = f32[16,17,128]{2,1,0:T(8,128)} custom-call(f32[16,17,128]{2,1,0:T(8,128)} %reshape.774.blocks_ref), custom_call_target="tpu_custom_call" | custom-call | tf_op jit(solution)/shard_map/pallas_call | solution.py:99
  33.2 1.0 %copy.68 = f32[2,8,17,128]{3,1,2,0:T(8,128)S(1)} copy(f32[2,8,17,128]{3,2,1,0:T(8,128)} %bitcast.110) | data formatting | bytes 278528
  34.1 0.3 copy.40
  34.5 0.6 copy.41
  35.1 0.7 add_select_fusion.5
  35.8 0.2 fusion.54
  36.0 1.0 %convolution_bitcast_fusion.1 = f32[32,2,2,64,4]{3,0,4,2,1:T(8,128)S(1)} fusion(f32[16,32,2,2,4,4]{1,0,4,2,5,3:T(8,128)S(1)} %copy.41, f32[1,16,4,1,64]{4,1,2,0,3:T(8,128)S(1)} %get-tuple-element.17, f32[1,16,4,1,64]{4,1,2,0,3:T(8,128)S(1)} %get-tuple-element.16, f32[1,16,4,1,64]{4,1,2,0,3:T(8,128)S(1)} %get-tuple-element.15), kind=kOutput, calls=%fused_computation.1 | convolution fusion | flops 50380800 | bytes 311296 | tf_op jit(solution)/shard_map/jnrxyc,rjysk->nsxkc/dot_general | solution.py:234
  37.1 0.2 copy.42
  37.3 0.5 copy.43
  38.0 0.7 reshape.779.blocks_ref
  38.8 26.8 %shard_map.70 = f32[32,9,128]{2,1,0:T(8,128)} custom-call(f32[32,9,128]{2,1,0:T(8,128)} %reshape.779.blocks_ref), custom_call_target="tpu_custom_call" | custom-call | tf_op jit(solution)/shard_map/pallas_call | solution.py:99
  65.5 1.0 %copy.67 = f32[4,8,9,128]{3,1,2,0:T(8,128)S(1)} copy(f32[4,8,9,128]{3,2,1,0:T(8,128)} %bitcast.109) | data formatting | bytes 294912
  66.6 0.2 copy.45
  66.8 0.7 and_select_fusion.3
  67.4 0.2 fusion.53
  67.7 1.0 %convolution_bitcast_fusion = f32[32,2,2,4,64]{4,0,3,2,1:T(8,128)S(1)} fusion(f32[32,32,2,2,2,4]{0,5,4,3,2,1:T(4,128)S(1)} %bitcast.105, f32[1,32,2,1,64]{4,1,2,0,3:T(8,128)S(1)} %get-tuple-element.23, f32[1,32,2,1,64]{4,1,2,0,3:T(8,128)S(1)} %get-tuple-element.22, f32[1,32,2,1,64]{4,1,2,0,3:T(8,128)S(1)} %get-tuple-element.21), kind=kOutput, calls=%fused_computation | convolution fusion | flops 50380800 | bytes 311296 | tf_op jit(solution)/shard_map/inrxbc,rixsk->nsbck/dot_general | solution.py:242
  68.7 0.2 copy.47
  68.9 0.9 %reshape.782 = f32[16,2,2,2,256]{4,3,2,1,0:T(2,128)} reshape(f32[32,2,2,4,64]{4,3,2,1,0:T(4,128)S(1)} %copy.47) | data formatting | bytes 262144 | tf_op jit(solution)/shard_map/reshape | solution.py:243
  69.8 0.6 reshape.783.blocks_ref
  70.4 9.2 %shard_map.71 = f32[16,1,128]{2,1,0:T(1,128)} custom-call(f32[16,1,128]{2,1,0:T(1,128)} %reshape.783.blocks_ref), custom_call_target="tpu_custom_call" | custom-call | tf_op jit(solution)/shard_map/pallas_call | solution.py:99
  79.6 0.5 broadcast.904
  80.1 1.4 %reduce.3 = f32[16,128]{1,0:T(8,128)S(1)} reduce(f32[16,1,128]{2,1,0:T(1,128)} %shard_map.71, f32[]{:T(128)} %broadcast.904), dimensions={1}, to_apply=%pallas_call.15.reduce_sub_computation.3 | reduce | bytes 16388 | tf_op jit(solution)/shard_map/pallas_call | solution.py:99
  81.5 0.7 reshape_reshape.3
  (39 shorter events, 1.7 us)
Async XLA Ops:
  0.6 2.8 %copy-start = (bf16[2,2,12,12,2,256]{5,4,3,2,1,0:T(2,128)(2,1)S(1)}, bf16[2,2,12,12,2,256]{5,4,3,2,1,0:T(2,128)(2,1)}, u32[]{:S(2)}) copy-start(bf16[2,2,12,12,2,256]{5,4,3,2,1,0:T(2,128)(2,1)} %param.5) | copy-start | bytes 1769476
  3.4 1.1 %copy-start.1 = (bf16[2,2,12,12,2,256]{5,4,3,2,1,0:T(2,128)(2,1)S(1)}, bf16[2,2,12,12,2,256]{5,4,3,2,1,0:T(2,128)(2,1)}, u32[]{:S(2)}) copy-start(bf16[2,2,12,12,2,256]{5,4,3,2,1,0:T(2,128)(2,1)} %param.6) | copy-start | bytes 1769476
  11.0 0.7 copy-start.2
  12.3 0.7 copy-start.3

commit v6 on v5

--- a/solution.py
+++ b/solution.py
@@ -209,6 +209,122 @@
     return out.reshape(slices, rows_x, inserts, 2, sites).transpose(2, 0, 3, 1, 4)
 
 
+def spectral_kernel(
+    sent_ref, table_ref, slab_ref, gathered_ref,
+    landed_ref, turned_ref, share_ref, shares_ref, total_ref,
+    a_send, a_recv, b_send, b_recv, s_send, s_recv, c_send, c_recv,
+):
+    parts_y = sent_ref.shape[0]
+    parts_x = slab_ref.shape[0]
+    depth = sent_ref.shape[1] - 1
+    band = slab_ref.shape[1]
+    me_y = lax.axis_index("sy")
+    me_x = lax.axis_index("sx")
+    mesh_ids = pl.DeviceIdType.MESH
+    barrier = pltpu.get_barrier_semaphore()
+    for step in range(1, parts_y):
+        pl.semaphore_signal(
+            barrier, 1, device_id={"sy": lax.rem(me_y + step, parts_y)}, device_id_type=mesh_ids
+        )
+    for step in range(1, parts_x):
+        pl.semaphore_signal(
+            barrier, 1, device_id={"sx": lax.rem(me_x + step, parts_x)}, device_id_type=mesh_ids
+        )
+    pl.semaphore_wait(barrier, parts_y + parts_x - 2)
+
+    def send_y(step, src, dst, send_sem, recv_sem):
+        peer = lax.rem(me_y + step, parts_y)
+        return pltpu.make_async_remote_copy(
+            src_ref=src(peer), dst_ref=dst(me_y), send_sem=send_sem.at[step],
+            recv_sem=recv_sem.at[step], device_id={"sy": peer}, device_id_type=mesh_ids,
+        )
+
+    def recv_y(step, src, dst, send_sem, recv_sem):
+        source = lax.rem(me_y + parts_y - step, parts_y)
+        return pltpu.make_async_remote_copy(
+            src_ref=src(source), dst_ref=dst(source), send_sem=send_sem.at[step],
+            recv_sem=recv_sem.at[step], device_id={"sy": source}, device_id_type=mesh_ids,
+        )
+
+    def send_x(step, src, dst, send_sem, recv_sem):
+        peer = lax.rem(me_x + step, parts_x)
+        return pltpu.make_async_remote_copy(
+            src_ref=src(peer), dst_ref=dst(me_x), send_sem=send_sem.at[step],
+            recv_sem=recv_sem.at[step], device_id={"sx": peer}, device_id_type=mesh_ids,
+        )
+
+    def recv_x(step, src, dst, send_sem, recv_sem):
+        source = lax.rem(me_x + parts_x - step, parts_x)
+        return pltpu.make_async_remote_copy(
+            src_ref=src(source), dst_ref=dst(source), send_sem=send_sem.at[step],
+            recv_sem=recv_sem.at[step], device_id={"sx": source}, device_id_type=mesh_ids,
+        )
+
+    def run(parts, send, recv, src, dst, send_sem, recv_sem):
+        @pl.loop(1, parts)
+        def _(step):
+            send(step, src, dst, send_sem, recv_sem).start()
+
+        @pl.loop(1, parts)
+        def _(step):
+            send(step, src, dst, send_sem, recv_sem).wait_send()
+
+        @pl.loop(1, parts)
+        def _(step):
+            recv(step, src, dst, send_sem, recv_sem).wait_recv()
+
+    run(parts_y, send_y, recv_y, lambda i: sent_ref.at[i], lambda i: landed_ref.at[i], a_send, a_recv)
+    landed_ref[me_y] = sent_ref[me_y]
+
+    block = landed_ref[:, 0:depth, :].reshape(parts_y * depth, -1)
+    turned = jnp.dot(table_ref[...], block, precision=HIGHEST, preferred_element_type=jnp.float32)
+    for peer in range(parts_x):
+        turned_ref[peer] = turned[peer * band : (peer + 1) * band]
+    share = landed_ref[0, depth : depth + 1, :]
+    for source in range(1, parts_y):
+        share = share + landed_ref[source, depth : depth + 1, :]
+    share_ref[...] = share
+
+    run(parts_x, send_x, recv_x, lambda i: turned_ref.at[i], lambda i: slab_ref.at[i], b_send, b_recv)
+    run(parts_x, send_x, recv_x, lambda i: share_ref, lambda i: shares_ref.at[i], s_send, s_recv)
+    slab_ref[me_x] = turned_ref[me_x]
+    shares_ref[me_x] = share_ref[...]
+
+    total = shares_ref[0]
+    for source in range(1, parts_x):
+        total = total + shares_ref[source]
+    total_ref[...] = total
+
+    run(parts_y, send_y, recv_y, lambda i: total_ref, lambda i: gathered_ref.at[i], c_send, c_recv)
+    gathered_ref[me_y] = total_ref[...]
+
+
+def spectral(sent, table, parts_x, band):
+    parts_y, rows, width = sent.shape
+    depth = rows - 1
+    vmem = pl.BlockSpec(memory_space=pltpu.VMEM)
+    return pl.pallas_call(
+        spectral_kernel,
+        out_shape=(
+            jax.ShapeDtypeStruct((parts_x, band, width), jnp.float32),
+            jax.ShapeDtypeStruct((parts_y, 1, width), jnp.float32),
+        ),
+        in_specs=[vmem, vmem],
+        out_specs=(vmem, vmem),
+        scratch_shapes=[
+            pltpu.VMEM((parts_y, rows, width), jnp.float32),
+            pltpu.VMEM((parts_x, band, width), jnp.float32),
+            pltpu.VMEM((1, width), jnp.float32),
+            pltpu.VMEM((parts_x, 1, width), jnp.float32),
+            pltpu.VMEM((1, width), jnp.float32),
+        ]
+        + [pltpu.SemaphoreType.DMA((parts_y,))] * 2
+        + [pltpu.SemaphoreType.DMA((parts_x,))] * 4
+        + [pltpu.SemaphoreType.DMA((parts_y,))] * 2,
+        compiler_params=pltpu.CompilerParams(collective_id=0, has_side_effects=True),
+    )(sent, table)
+
+
 def body(forward_prop, backward_prop, gamma_table, source_site, momenta):
     slices = forward_prop.shape[0]
     rows_x = forward_prop.shape[4]
@@ -221,28 +337,24 @@
     partial = jnp.stack([local_re, local_im], 0)
     groups_y = lax.axis_size("sy")
     groups_x = lax.axis_size("sx")
-    along_z = jnp.einsum(
-        "nrxyz,rzsk->nsxyk", fields, dft_matrix(LZ, source_site[2]), precision=HIGHEST
-    )
     share_z = LZ // groups_y
-    blocks = along_z.reshape(count, 2, rows_x, rows_y, groups_y, share_z)
-    blocks = blocks.transpose(4, 0, 1, 2, 3, 5).reshape(groups_y, -1)
-    shares = partial.reshape(groups_y, -1)
-    blocks, share = exchange(blocks, shares, "sy", 0)
-    blocks = blocks.reshape(groups_y, count, 2, rows_x, rows_y, share_z)
-    table_y = dft_matrix(rows_y * groups_y, source_site[1]).reshape(2, groups_y, rows_y, 2, -1)
-    along_y = jnp.einsum("jnrxyc,rjysk->nsxkc", blocks, table_y, precision=HIGHEST)
-    share_y = along_y.shape[3] // groups_x
-    blocks = along_y.reshape(count, 2, rows_x, groups_x, share_y, share_z)
-    blocks = blocks.transpose(3, 0, 1, 2, 4, 5).reshape(groups_x, -1)
-    spread = jnp.broadcast_to(share[None], (groups_x, share.size))
-    blocks, share = exchange(blocks, spread, "sx", 1)
-    blocks = blocks.reshape(groups_x, count, 2, rows_x, share_y, share_z)
+    length_y = rows_y * groups_y
+    share_y = length_y // groups_x
+    table_z = dft_matrix(LZ, source_site[2]).reshape(2, LZ, 2, groups_y, share_z)
+    sent = jnp.einsum("nrxyz,rzsjc->jsynxc", fields, table_z, precision=HIGHEST)
+    sent = sent.reshape(groups_y, 2 * rows_y, -1)
+    width = sent.shape[2]
+    shares = partial.reshape(groups_y, 1, -1)
+    shares = jnp.pad(shares, ((0, 0), (0, 0), (0, width - shares.shape[2])))
+    sent = jnp.concatenate([sent, shares], 1)
+    table_y = dft_matrix(length_y, source_site[1]).reshape(2, groups_y, rows_y, 2, groups_x, share_y)
+    table_y = table_y.transpose(4, 5, 3, 1, 0, 2).reshape(2 * length_y, 2 * length_y)
+    slab, gathered = spectral(sent, table_y, groups_x, 2 * share_y)
+    slab = slab.reshape(groups_x, share_y, 2, count, rows_x, share_z)
     table_x = dft_matrix(rows_x * groups_x, source_site[0]).reshape(2, groups_x, rows_x, 2, -1)
-    spectrum = jnp.einsum("inrxbc,rixsk->nsbck", blocks, table_x, precision=HIGHEST)
+    spectrum = jnp.einsum("ibsnxc,sixtk->ntbck", slab, table_x, precision=HIGHEST)
     corr = spectrum.reshape(inserts, slices, 2, share_y, -1)
-    spread = jnp.broadcast_to(share[None], (groups_y, share.size))
-    listed = swap(spread, "sy", 2).reshape(2, inserts, slices, -1)
+    listed = gathered[:, 0, : partial.size // groups_y].reshape(2, inserts, slices, -1)
     return (corr, listed)
 
 

time: 83.6 us -> 88.4 us (1.057); the launches traced: 82.2 us -> 88.1 us
  Pallas kernels: 53 us -> 59.4 us
  local copies, waits for them, and re-layouts: 17.1 us -> 18.4 us
    pallas_call x3 -> x1, Pallas kernels: 48.9 us -> 55.3 us  [spectral(): pl.pallas_call(spectral_kernel, out_shape=(jax.ShapeDtypeStruct((parts_x,...]
    unnamed x10 -> x8, local copies, waits for them, and re-layouts: 2.54 us -> 0.02 us
    reshape x1, local copies, waits for them, and re-layouts: 1.03 us -> 2.64 us  [contract(): forward = forward_prop.reshape(slices, 2, 12, 12 * rows_x, sites)]
    transpose x5 -> x3, local copies, waits for them, and re-layouts: 2.24 us -> 3.66 us  [the longest x1 3.03 us: body(): table_y.transpose(4, 5, 3, 1, 0, 2).reshape(2 * length_y, 2 * length_y)]
    pallas_call x1 -> x0, other arithmetic: 1.36 us -> none  [swap(): pl.pallas_call(functools.partial(swap_kernel, axis), out_shape=jax.ShapeD...]
    dot_general x3 -> x2, matrix products: 2.48 us -> 1.6 us  [the longest x1 0.81 us: body(): sent = jnp.einsum('nrxyz,rzsjc->jsynxc', fields, table_z, precision=HIGHEST)]
    reshape x7 -> x3, local copies, waits for them, and re-layouts: 3.19 us -> 3.94 us  [the longest x1 3.54 us: body(): table_y.transpose(4, 5, 3, 1, 0, 2).reshape(2 * length_y, 2 * length_y)]
where the time goes in v6:
time: 88.4 us; the launch traced here: 88.1 us
  Pallas kernels  59.4 us (67%)
  local copies, waits for them, and re-layouts  18.4 us (21%)
  other arithmetic  7.04 us (8%)
  matrix products  2.38 us (3%)
  between operations  0.92 us (1%)
    pallas_call x1, Pallas kernels, spectral(): pl.pallas_call(spectral_kernel, out_shape=(jax.ShapeDtypeStruct((parts_x,...  55.3 us
    pallas_call x1, Pallas kernels, contract(): pl.pallas_call(contract_kernel, out_shape=jax.ShapeDtypeStruct((slices, r...  4.11 us
    reshape x1, local copies, waits for them, and re-layouts, body(): table_y.transpose(4, 5, 3, 1, 0, 2).reshape(2 * length_y, 2 * length_y)  3.54 us
    transpose x1, local copies, waits for them, and re-layouts, body(): table_y.transpose(4, 5, 3, 1, 0, 2).reshape(2 * length_y, 2 * length_y)  3.03 us
    reshape x1, local copies, waits for them, and re-layouts, contract(): forward = forward_prop.reshape(slices, 2, 12, 12 * rows_x, sites)  2.64 us
    select_n x3, other arithmetic, dft_table(): offsets = jnp.mod(wavenum - anchor, length)  1.89 us

profile of v6, /device:TPU:1, one launch (start us, length us, event | category | flops | bytes accessed | tf_op | source)
XLA Modules:
  0.0 88.1 jit_solution(17806605065763661742)
XLA Ops:
  0.6 0.8 fusion.46
  1.4 0.7 slice.40
  2.1 0.1 eq.85
  2.2 0.1 fusion.53
  2.3 0.3 copy.27
  2.7 0.8 reshape.731.mix_ref
  3.4 2.6 %reshape.732.forward_ref = bf16[2,2,12,24,256]{4,3,2,1,0:T(8,128)(2,1)} reshape(bf16[2,2,12,12,2,256]{5,4,3,2,1,0:T(2,128)(2,1)} %param.5) | data formatting | bytes 1179648 | tf_op jit(solution)/shard_map/reshape | solution.py:197
  6.1 1.0 %reshape.733.backward_ref = bf16[2,2,12,24,256]{4,3,2,1,0:T(8,128)(2,1)} reshape(bf16[2,2,12,12,2,256]{5,4,3,2,1,0:T(2,128)(2,1)S(1)} %copy-done) | data formatting | bytes 1179648 | tf_op jit(solution)/shard_map/reshape | solution.py:198
  7.1 4.1 %shard_map.68 = f32[2,2,32,256]{3,2,1,0:T(8,128)} custom-call(f32[32,32]{1,0:T(8,128)} %reshape.731.mix_ref, bf16[2,2,12,24,256]{4,3,2,1,0:T(8,128)(2,1)} %reshape.732.forward_ref, bf16[2,2,12,24,256]{4,3,2,1,0:T(8,128)(2,1)} %reshape.733.backward_ref), custom_call_target="tpu_custom_call" | custom-call | tf_op jit(solution)/shard_map/pallas_call | solution.py:202
  11.2 1.0 %reshape.734 = f32[2,2,16,2,256]{4,3,2,1,0:T(2,128)S(1)} reshape(f32[2,2,32,256]{3,2,1,0:T(8,128)} %shard_map.68) | data formatting | bytes 262144 | tf_op jit(solution)/shard_map/reshape | solution.py:209
  12.2 0.1 copy.51
  12.3 0.2 reshape.735
  12.6 0.1 reshape_squeeze.9
  12.7 0.6 fusion.55
  13.3 0.6 add_subtract_fusion.1
  13.9 0.1 and_select_fusion.1
  14.0 0.1 copy.31
  14.1 0.6 add_subtract_fusion
  14.8 0.1 add_select_fusion.4
  14.9 0.1 fusion.27
  15.0 0.6 and_select_fusion.2
  15.6 0.1 fusion.36
  15.7 1.1 %add_sine_fusion = (f32[32,2,4,64]{3,2,1,0:T(4,128)S(1)}, f32[32,2,4,64]{3,2,1,0:T(4,128)S(1)}) fusion(f32[32,64]{1,0:T(8,128)S(1)} %fusion.36, f32[32,2,4]{2,1,0:T(2,128)S(1)} %fusion.27), kind=kLoop, calls=%fused_computation.12 | loop fusion | flops 16384 | bytes 140288 | tf_op jit(solution)/shard_map/sin | solution.py:143
  16.8 0.1 cos.55
  16.9 0.2 fusion.56
  17.1 0.1 reshape_squeeze.10
  17.2 0.1 sin.67
  17.3 0.2 fusion.1
  17.5 0.2 fusion.57
  17.7 0.2 fusion
  17.9 0.1 reshape.737
  18.0 0.2 fusion.44
  18.3 0.8 convolution_bitcast_fusion
  19.1 0.5 copy.30
  19.5 0.3 copy.32
  19.9 0.7 select_maximum_fusion.sent_ref
  20.6 0.7 add_select_fusion.5
  21.3 0.3 fusion.34
  21.6 3.0 %copy.33 = f32[32,2,2,16,2,4]{5,4,3,2,1,0:T(2,128)S(1)} copy(f32[32,2,2,16,2,4]{0,3,1,2,5,4:T(8,128)S(1)} %maximum_bitcast_fusion) | data formatting | bytes 131072 | tf_op jit(solution)/shard_map/transpose | solution.py:351
  24.7 3.5 %reshape.738.table_ref = f32[128,128]{1,0:T(8,128)} reshape(f32[32,2,2,16,2,4]{5,4,3,2,1,0:T(2,128)S(1)} %copy.33) | data formatting | bytes 131072 | tf_op jit(solution)/shard_map/reshape | solution.py:351
  28.2 55.3 %shard_map.69 = (f32[32,4,256]{2,1,0:T(4,128)}, f32[16,1,256]{2,1,0:T(1,128)}) custom-call(f32[16,9,256]{2,1,0:T(8,128)} %select_maximum_fusion.sent_ref, f32[128,128]{1,0:T(8,128)} %reshape.738.table_ref), custom_call_target="tpu_custom_call" | custom-call | tf_op jit(solution)/shard_map/pallas_call | solution.py:306
  83.5 1.1 %copy.34 = f32[32,4,256]{0,2,1:T(8,128)S(1)} copy(f32[32,4,256]{2,1,0:T(4,128)} %get-tuple-element.4) | data formatting | bytes 262144 | tf_op jit(solution)/shard_map/pallas_call | solution.py:306
  84.6 0.7 and_select_fusion.3
  85.3 0.2 fusion.43
  85.5 0.8 convolution_bitcast_fusion.1
  86.3 0.2 copy.36
  86.5 0.9 reshape.740
  87.4 0.7 reshape_squeeze.11
  (22 shorter events, 0.1 us)
Async XLA Ops:
  0.6 5.4 %copy-start = (bf16[2,2,12,12,2,256]{5,4,3,2,1,0:T(2,128)(2,1)S(1)}, bf16[2,2,12,12,2,256]{5,4,3,2,1,0:T(2,128)(2,1)}, u32[]{:S(2)}) copy-start(bf16[2,2,12,12,2,256]{5,4,3,2,1,0:T(2,128)(2,1)} %param.6) | copy-start | bytes 1769476
  6.1 6.6 %copy-start.1 = (s32[3]{0:T(128)S(1)}, s32[3]{0:T(128)}, u32[]{:S(2)}) copy-start(s32[3]{0:T(128)} %param.8) | copy-start | bytes 40
  6.1 7.9 %copy-start.3 = (s32[32,3]{0,1:T(4,128)S(1)}, s32[32,3]{0,1:T(4,128)}, u32[]{:S(2)}) copy-start(s32[32,3]{0,1:T(4,128)} %param.9) | copy-start | bytes 1156
  83.5 3.9 %copy-start.2 = (f32[16,1,256]{2,1,0:T(1,128)S(1)}, f32[16,1,256]{2,1,0:T(1,128)}, u32[]{:S(2)}) copy-start(f32[16,1,256]{2,1,0:T(1,128)} %get-tuple-element.5) | copy-start | bytes 49156

commit v7 on v5

--- a/solution.py
+++ b/solution.py
@@ -111,6 +111,110 @@
     width = blocks.shape[1]
     got = swap(jnp.concatenate([blocks, extra], 1), axis, ident)
     return got[:, :width], got[:, width:].sum(0)
+
+
+def spread_kernel(blocks_ref, out_ref, gathered_ref, total_ref, b_send, b_recv, c_send, c_recv):
+    parts_x = blocks_ref.shape[0]
+    parts_y = gathered_ref.shape[0]
+    depth = blocks_ref.shape[1] - 1
+    me_x = lax.axis_index("sx")
+    me_y = lax.axis_index("sy")
+    mesh_ids = pl.DeviceIdType.MESH
+    barrier = pltpu.get_barrier_semaphore()
+    for step in range(1, parts_x):
+        pl.semaphore_signal(
+            barrier, 1, device_id={"sx": lax.rem(me_x + step, parts_x)}, device_id_type=mesh_ids
+        )
+    for step in range(1, parts_y):
+        pl.semaphore_signal(
+            barrier, 1, device_id={"sy": lax.rem(me_y + step, parts_y)}, device_id_type=mesh_ids
+        )
+    pl.semaphore_wait(barrier, parts_x + parts_y - 2)
+
+    def copy_x(step, outgoing):
+        peer = lax.rem(me_x + (step if outgoing else parts_x - step), parts_x)
+        return pltpu.make_async_remote_copy(
+            src_ref=blocks_ref.at[peer],
+            dst_ref=out_ref.at[me_x if outgoing else peer],
+            send_sem=b_send.at[step],
+            recv_sem=b_recv.at[step],
+            device_id={"sx": peer},
+            device_id_type=mesh_ids,
+        )
+
+    def copy_y(step, outgoing):
+        peer = lax.rem(me_y + (step if outgoing else parts_y - step), parts_y)
+        return pltpu.make_async_remote_copy(
+            src_ref=total_ref,
+            dst_ref=gathered_ref.at[me_y if outgoing else peer],
+            send_sem=c_send.at[step],
+            recv_sem=c_recv.at[step],
+            device_id={"sy": peer},
+            device_id_type=mesh_ids,
+        )
+
+    @pl.loop(1, parts_x)
+    def _(step):
+        copy_x(step, True).start()
+
+    out_ref[me_x] = blocks_ref[me_x]
+
+    @pl.loop(1, parts_x)
+    def _(step):
+        copy_x(step, True).wait_send()
+
+    @pl.loop(1, parts_x)
+    def _(step):
+        copy_x(step, False).wait_recv()
+
+    total = out_ref[0, depth : depth + 1, :]
+    for source in range(1, parts_x):
+        total = total + out_ref[source, depth : depth + 1, :]
+    total_ref[...] = total
+
+    @pl.loop(1, parts_y)
+    def _(step):
+        copy_y(step, True).start()
+
+    gathered_ref[me_y] = total
+
+    @pl.loop(1, parts_y)
+    def _(step):
+        copy_y(step, True).wait_send()
+
+    @pl.loop(1, parts_y)
+    def _(step):
+        copy_y(step, False).wait_recv()
+
+
+def spread(blocks, share, parts_y):
+    parts_x = blocks.shape[0]
+    lanes = 128
+    width = share.size
+    rows = jnp.pad(share, (0, lanes - width)) if width < lanes else share
+    shaped = blocks.reshape(parts_x, -1, rows.size)
+    shaped = jnp.concatenate(
+        [shaped, jnp.broadcast_to(rows.reshape(1, 1, -1), (parts_x, 1, rows.size))], 1
+    )
+    vmem = pl.BlockSpec(memory_space=pltpu.VMEM)
+    got, gathered = pl.pallas_call(
+        spread_kernel,
+        out_shape=(
+            jax.ShapeDtypeStruct(shaped.shape, shaped.dtype),
+            jax.ShapeDtypeStruct((parts_y, 1, rows.size), shaped.dtype),
+        ),
+        in_specs=[vmem],
+        out_specs=(vmem, vmem),
+        scratch_shapes=[
+            pltpu.VMEM((1, rows.size), jnp.float32),
+            pltpu.SemaphoreType.DMA((parts_x,)),
+            pltpu.SemaphoreType.DMA((parts_x,)),
+            pltpu.SemaphoreType.DMA((parts_y,)),
+            pltpu.SemaphoreType.DMA((parts_y,)),
+        ],
+        compiler_params=pltpu.CompilerParams(collective_id=1, has_side_effects=True),
+    )(shaped)
+    return got[:, :-1].reshape(blocks.shape), gathered[:, 0, :width]
 
 
 def apply_gammas(mat_re, mat_im, real_part, imag_part):
@@ -235,14 +339,12 @@
     share_y = along_y.shape[3] // groups_x
     blocks = along_y.reshape(count, 2, rows_x, groups_x, share_y, share_z)
     blocks = blocks.transpose(3, 0, 1, 2, 4, 5).reshape(groups_x, -1)
-    spread = jnp.broadcast_to(share[None], (groups_x, share.size))
-    blocks, share = exchange(blocks, spread, "sx", 1)
+    blocks, gathered = spread(blocks, share, groups_y)
     blocks = blocks.reshape(groups_x, count, 2, rows_x, share_y, share_z)
     table_x = dft_matrix(rows_x * groups_x, source_site[0]).reshape(2, groups_x, rows_x, 2, -1)
     spectrum = jnp.einsum("inrxbc,rixsk->nsbck", blocks, table_x, precision=HIGHEST)
     corr = spectrum.reshape(inserts, slices, 2, share_y, -1)
-    spread = jnp.broadcast_to(share[None], (groups_y, share.size))
-    listed = swap(spread, "sy", 2).reshape(2, inserts, slices, -1)
+    listed = gathered.reshape(2, inserts, slices, -1)
     return (corr, listed)
 
 

time: 83.6 us -> 77.6 us (0.928); the launches traced: 82.2 us -> 77.2 us
  Pallas kernels: 53 us -> 49.5 us
  local copies, waits for them, and re-layouts: 17.1 us -> 15.7 us
    pallas_call x3 -> x1, Pallas kernels: 48.9 us -> 12.9 us  [swap(): pl.pallas_call(functools.partial(swap_kernel, axis), out_shape=jax.ShapeD...]
    pallas_call x0 -> x1, Pallas kernels: none -> 32.4 us  [spread(): pl.pallas_call(spread_kernel, out_shape=(jax.ShapeDtypeStruct(shaped.shap...]
    reshape x3 -> x1, local copies, waits for them, and re-layouts: 2.03 us -> 0.7 us  [swap(): shaped = blocks.reshape(parts, -1, lanes)]
    slice x0 -> x2, local copies, waits for them, and re-layouts: none -> 1.12 us  [spread(): return (got[:, :-1].reshape(blocks.shape), gathered[:, 0, :width])]
    unnamed x10 -> x11, local copies, waits for them, and re-layouts: 2.54 us -> 1.52 us
where the time goes in v7:
time: 77.6 us; the launch traced here: 77.2 us
  Pallas kernels  49.5 us (64%)
  local copies, waits for them, and re-layouts  15.7 us (20%)
  other arithmetic  7.76 us (10%)
  matrix products  3.25 us (4%)
  between operations  0.98 us (1%)
    pallas_call x1, Pallas kernels, spread(): pl.pallas_call(spread_kernel, out_shape=(jax.ShapeDtypeStruct(shaped.shap...  32.4 us
    pallas_call x1, Pallas kernels, swap(): pl.pallas_call(functools.partial(swap_kernel, axis), out_shape=jax.ShapeD...  12.9 us
    pallas_call x1, Pallas kernels, contract(): pl.pallas_call(contract_kernel, out_shape=jax.ShapeDtypeStruct((slices, r...  4.11 us
    select_n x3, other arithmetic, dft_table(): offsets = jnp.mod(wavenum - anchor, length)  2.02 us

profile of v7, /device:TPU:1, one launch (start us, length us, event | category | flops | bytes accessed | tf_op | source)
XLA Modules:
  0.0 77.2 jit_solution(8336463927393399746)
XLA Ops:
  0.6 0.8 fusion.56
  1.4 0.7 slice.47
  2.3 0.3 copy.34
  2.7 0.8 reshape.753.mix_ref
  3.4 1.0 %reshape.754.forward_ref = bf16[2,2,12,24,256]{4,3,2,1,0:T(8,128)(2,1)} reshape(bf16[2,2,12,12,2,256]{5,4,3,2,1,0:T(2,128)(2,1)S(1)} %copy-done) | data formatting | bytes 1179648 | tf_op jit(solution)/shard_map/reshape | solution.py:301
  4.5 1.0 %reshape.755.backward_ref = bf16[2,2,12,24,256]{4,3,2,1,0:T(8,128)(2,1)} reshape(bf16[2,2,12,12,2,256]{5,4,3,2,1,0:T(2,128)(2,1)S(1)} %copy-done.1) | data formatting | bytes 1179648 | tf_op jit(solution)/shard_map/reshape | solution.py:302
  5.5 4.1 %shard_map.68 = f32[2,2,32,256]{3,2,1,0:T(8,128)} custom-call(f32[32,32]{1,0:T(8,128)} %reshape.753.mix_ref, bf16[2,2,12,24,256]{4,3,2,1,0:T(8,128)(2,1)} %reshape.754.forward_ref, bf16[2,2,12,24,256]{4,3,2,1,0:T(8,128)(2,1)} %reshape.755.backward_ref), custom_call_target="tpu_custom_call" | custom-call | tf_op jit(solution)/shard_map/pallas_call | solution.py:306
  9.6 1.0 %reshape.756 = f32[2,2,16,2,256]{4,3,2,1,0:T(2,128)S(1)} reshape(f32[2,2,32,256]{3,2,1,0:T(8,128)} %shard_map.68) | data formatting | bytes 262144 | tf_op jit(solution)/shard_map/reshape | solution.py:313
  10.7 0.2 reshape.757
  11.1 0.5 copy-done.3
  11.6 0.6 fusion.66
  12.3 0.7 and_select_fusion.2
  13.1 0.7 add_subtract_fusion
  13.8 0.7 add_subtract_fusion.1
  14.7 0.1 fusion.32
  14.8 1.1 %add_sine_fusion = (f32[32,2,4,64]{3,2,1,0:T(4,128)S(1)}, f32[32,2,4,64]{3,2,1,0:T(4,128)S(1)}) fusion(f32[32,64]{1,0:T(8,128)S(1)} %fusion.43, f32[32,2,4]{2,1,0:T(2,128)S(1)} %fusion.32), kind=kLoop, calls=%fused_computation.13 | loop fusion | flops 16384 | bytes 140288 | tf_op jit(solution)/shard_map/sin | solution.py:247
  16.0 0.2 fusion.68
  16.5 0.2 fusion
  16.7 0.2 fusion.67
  16.9 0.2 fusion.1
  17.2 0.2 fusion.52
  17.4 0.4 convolution_bitcast_fusion.2
  17.8 0.2 copy.37
  18.1 1.1 %copy.38 = f32[16,32,2,2,4,4]{0,5,4,3,2,1:T(4,128)S(1)} copy(f32[16,32,2,2,4,4]{1,5,0,4,3,2:T(4,128)S(1)} %bitcast.102) | data formatting | bytes 262144 | tf_op jit(solution)/shard_map/transpose | solution.py:333
  19.2 0.3 copy.40
  19.5 0.7 reshape.761.blocks_ref
  20.2 12.9 %shard_map.69 = f32[16,17,128]{2,1,0:T(8,128)} custom-call(f32[16,17,128]{2,1,0:T(8,128)} %reshape.761.blocks_ref), custom_call_target="tpu_custom_call" | custom-call | tf_op jit(solution)/shard_map/pallas_call | solution.py:99
  33.2 1.0 %copy.66 = f32[2,8,17,128]{3,1,2,0:T(8,128)S(1)} copy(f32[2,8,17,128]{3,2,1,0:T(8,128)} %bitcast.105) | data formatting | bytes 278528
  34.2 0.3 copy.41
  34.5 0.6 copy.42
  35.1 0.7 add_select_fusion.5
  35.8 0.2 fusion.54
  36.0 1.0 %convolution_bitcast_fusion.1 = f32[32,2,2,64,4]{3,0,4,2,1:T(8,128)S(1)} fusion(f32[16,32,2,2,4,4]{1,0,4,2,5,3:T(8,128)S(1)} %copy.42, f32[1,16,4,1,64]{4,1,2,0,3:T(8,128)S(1)} %get-tuple-element.21, f32[1,16,4,1,64]{4,1,2,0,3:T(8,128)S(1)} %get-tuple-element.20, f32[1,16,4,1,64]{4,1,2,0,3:T(8,128)S(1)} %get-tuple-element.19), kind=kOutput, calls=%fused_computation.1 | convolution fusion | flops 50380800 | bytes 311296 | tf_op jit(solution)/shard_map/jnrxyc,rjysk->nsxkc/dot_general | solution.py:338
  37.0 0.2 copy.43
  37.3 0.5 copy.44
  37.8 0.2 copy.45
  38.0 0.7 pad_maximum_fusion.blocks_ref
  38.7 32.4 %shard_map.70 = (f32[32,9,128]{2,1,0:T(8,128)}, f32[16,1,128]{2,1,0:T(1,128)}) custom-call(f32[32,9,128]{2,1,0:T(8,128)} %pad_maximum_fusion.blocks_ref), custom_call_target="tpu_custom_call" | custom-call | tf_op jit(solution)/shard_map/pallas_call | solution.py:200
  71.2 0.9 %slice.57 = f32[32,8,128]{2,1,0:T(8,128)S(1)} slice(f32[32,9,128]{2,1,0:T(8,128)} %get-tuple-element.4), slice={[0:32], [0:8], [0:128]} | slice | bytes 262144 | tf_op jit(solution)/shard_map/slice | solution.py:217
  72.1 0.2 copy.46
  72.3 0.7 and_select_fusion.3
  73.0 0.2 fusion.53
  73.2 1.0 %convolution_bitcast_fusion = f32[32,2,2,4,64]{4,0,3,2,1:T(8,128)S(1)} fusion(f32[32,32,2,2,2,4]{0,5,4,3,2,1:T(4,128)S(1)} %bitcast.101, f32[1,32,2,1,64]{4,1,2,0,3:T(8,128)S(1)} %get-tuple-element.27, f32[1,32,2,1,64]{4,1,2,0,3:T(8,128)S(1)} %get-tuple-element.26, f32[1,32,2,1,64]{4,1,2,0,3:T(8,128)S(1)} %get-tuple-element.25), kind=kOutput, calls=%fused_computation | convolution fusion | flops 50380800 | bytes 311296 | tf_op jit(solution)/shard_map/inrxbc,rixsk->nsbck/dot_general | solution.py:345
  74.2 0.2 copy.48
  74.4 0.9 %reshape.765 = f32[16,2,2,2,256]{4,3,2,1,0:T(2,128)} reshape(f32[32,2,2,4,64]{4,3,2,1,0:T(4,128)S(1)} %copy.48) | data formatting | bytes 262144 | tf_op jit(solution)/shard_map/reshape | solution.py:346
  75.3 0.5 broadcast.901
  75.8 0.7 reduce.3
  76.5 0.7 reshape_squeeze.11
  (36 shorter events, 1.3 us)
Async XLA Ops:
  0.6 2.8 %copy-start = (bf16[2,2,12,12,2,256]{5,4,3,2,1,0:T(2,128)(2,1)S(1)}, bf16[2,2,12,12,2,256]{5,4,3,2,1,0:T(2,128)(2,1)}, u32[]{:S(2)}) copy-start(bf16[2,2,12,12,2,256]{5,4,3,2,1,0:T(2,128)(2,1)} %param.5) | copy-start | bytes 1769476
  3.4 1.1 %copy-start.1 = (bf16[2,2,12,12,2,256]{5,4,3,2,1,0:T(2,128)(2,1)S(1)}, bf16[2,2,12,12,2,256]{5,4,3,2,1,0:T(2,128)(2,1)}, u32[]{:S(2)}) copy-start(bf16[2,2,12,12,2,256]{5,4,3,2,1,0:T(2,128)(2,1)} %param.6) | copy-start | bytes 1769476
  11.0 0.7 copy-start.3
  12.3 0.7 copy-start.4
  74.4 1.4 %copy-start.2 = (f32[16,1,128]{2,1,0:T(1,128)S(1)}, f32[16,1,128]{2,1,0:T(1,128)}, u32[]{:S(2)}) copy-start(f32[16,1,128]{2,1,0:T(1,128)} %get-tuple-element.5) | copy-start | bytes 24580

commit v8 on v7

--- a/solution.py
+++ b/solution.py
@@ -13,6 +13,7 @@
 
 
 HIGHEST = lax.Precision.HIGHEST
+HIGH = lax.Precision.HIGH
 
 
 def gamma_matrices(gamma_table):
@@ -37,11 +38,16 @@
     return (jnp.cos(angles), -jnp.sin(angles))
 
 
-def dft_matrix(length, anchor):
-    table_re, table_im = dft_table(length, anchor)
-    rows_re = jnp.stack([table_re, table_im], 1)
-    rows_im = jnp.stack([-table_im, table_re], 1)
-    return jnp.stack([rows_re, rows_im], 0)
+def dft_matrices(length, anchors):
+    wavenum = jnp.arange(length, dtype=jnp.int32)
+    offsets = jnp.mod(wavenum[None, :] - anchors[:, None], length)
+    phase_index = jnp.mod(offsets[:, :, None] * wavenum[None, None, :], length)
+    angles = 2.0 * math.pi / length * phase_index.astype(jnp.float32)
+    table_re = jnp.cos(angles)
+    table_im = -jnp.sin(angles)
+    rows_re = jnp.stack([table_re, table_im], 2)
+    rows_im = jnp.stack([-table_im, table_re], 2)
+    return jnp.stack([rows_re, rows_im], 1)
 
 
 def swap_kernel(axis, blocks_ref, out_ref, send_sem, recv_sem):
@@ -325,24 +331,23 @@
     partial = jnp.stack([local_re, local_im], 0)
     groups_y = lax.axis_size("sy")
     groups_x = lax.axis_size("sx")
-    along_z = jnp.einsum(
-        "nrxyz,rzsk->nsxyk", fields, dft_matrix(LZ, source_site[2]), precision=HIGHEST
-    )
+    tables = dft_matrices(LZ, source_site)
+    along_z = jnp.einsum("nrxyz,rzsk->nsxyk", fields, tables[2], precision=HIGH)
     share_z = LZ // groups_y
     blocks = along_z.reshape(count, 2, rows_x, rows_y, groups_y, share_z)
     blocks = blocks.transpose(4, 0, 1, 2, 3, 5).reshape(groups_y, -1)
     shares = partial.reshape(groups_y, -1)
     blocks, share = exchange(blocks, shares, "sy", 0)
     blocks = blocks.reshape(groups_y, count, 2, rows_x, rows_y, share_z)
-    table_y = dft_matrix(rows_y * groups_y, source_site[1]).reshape(2, groups_y, rows_y, 2, -1)
-    along_y = jnp.einsum("jnrxyc,rjysk->nsxkc", blocks, table_y, precision=HIGHEST)
+    table_y = tables[1].reshape(2, groups_y, rows_y, 2, -1)
+    along_y = jnp.einsum("jnrxyc,rjysk->nsxkc", blocks, table_y, precision=HIGH)
     share_y = along_y.shape[3] // groups_x
     blocks = along_y.reshape(count, 2, rows_x, groups_x, share_y, share_z)
     blocks = blocks.transpose(3, 0, 1, 2, 4, 5).reshape(groups_x, -1)
     blocks, gathered = spread(blocks, share, groups_y)
     blocks = blocks.reshape(groups_x, count, 2, rows_x, share_y, share_z)
-    table_x = dft_matrix(rows_x * groups_x, source_site[0]).reshape(2, groups_x, rows_x, 2, -1)
-    spectrum = jnp.einsum("inrxbc,rixsk->nsbck", blocks, table_x, precision=HIGHEST)
+    table_x = tables[0].reshape(2, groups_x, rows_x, 2, -1)
+    spectrum = jnp.einsum("inrxbc,rixsk->nsbck", blocks, table_x, precision=HIGH)
     corr = spectrum.reshape(inserts, slices, 2, share_y, -1)
     listed = gathered.reshape(2, inserts, slices, -1)
     return (corr, listed)

time: 77.6 us -> 75.2 us (0.969)
  other arithmetic: 7.76 us -> 6.33 us
  matrix products: 3.25 us -> 2.38 us
    select_n x3 -> x1, other arithmetic: 2.02 us -> 0.08 us  [dft_matrices(): offsets = jnp.mod(wavenum[None, :] - anchors[:, None], length)]
    dot_general x3, matrix products: 2.47 us -> 1.6 us  [the longest x1 0.7 us: body(): jnp.einsum('inrxbc,rixsk->nsbck', blocks, table_x, precision=HIGH)]
where the time goes in v8:
time: 75.2 us; the launch traced here: 74.7 us
  Pallas kernels  49.5 us (66%)
  local copies, waits for them, and re-layouts  15.6 us (21%)
  other arithmetic  6.33 us (8%)
  matrix products  2.38 us (3%)
  between operations  0.97 us (1%)
    pallas_call x1, Pallas kernels, spread(): pl.pallas_call(spread_kernel, out_shape=(jax.ShapeDtypeStruct(shaped.shap...  32.4 us
    pallas_call x1, Pallas kernels, swap(): pl.pallas_call(functools.partial(swap_kernel, axis), out_shape=jax.ShapeD...  12.9 us
    pallas_call x1, Pallas kernels, contract(): pl.pallas_call(contract_kernel, out_shape=jax.ShapeDtypeStruct((slices, r...  4.11 us
    unnamed x11, local copies, waits for them, and re-layouts  1.54 us

profile of v8, /device:TPU:1, one launch (start us, length us, event | category | flops | bytes accessed | tf_op | source)
XLA Modules:
  0.0 74.7 jit_solution(11225771123160902255)
XLA Ops:
  0.6 0.8 %fusion.32 = (f32[16,4,1]{0,2,1:T(1,128)S(1)}, f32[16,4,1]{0,2,1:T(1,128)S(1)}) fusion(s32[16,4,2]{0,2,1:T(2,128)} %param.7), kind=kLoop, calls=%fused_computation.86 | loop fusion | flops 640 | bytes 768 | tf_op jit(solution)/shard_map/sub | solution.py:25
  1.4 0.7 slice.53
  2.3 0.3 copy.36
  2.7 0.8 %reshape.435.mix_ref = f32[32,32]{1,0:T(8,128)} reshape(f32[16,2,16,2]{3,2,1,0:T(8,128)S(1)} %copy.36) | data formatting | bytes 8192 | tf_op jit(solution)/shard_map/reshape | solution.py:311
  3.4 1.0 %reshape.436.forward_ref = bf16[2,2,12,24,256]{4,3,2,1,0:T(8,128)(2,1)} reshape(bf16[2,2,12,12,2,256]{5,4,3,2,1,0:T(2,128)(2,1)S(1)} %copy-done) | data formatting | bytes 1179648 | tf_op jit(solution)/shard_map/reshape | solution.py:307
  4.5 1.0 %reshape.437.backward_ref = bf16[2,2,12,24,256]{4,3,2,1,0:T(8,128)(2,1)} reshape(bf16[2,2,12,12,2,256]{5,4,3,2,1,0:T(2,128)(2,1)S(1)} %copy-done.1) | data formatting | bytes 1179648 | tf_op jit(solution)/shard_map/reshape | solution.py:308
  5.5 4.1 %shard_map.68 = f32[2,2,32,256]{3,2,1,0:T(8,128)} custom-call(f32[32,32]{1,0:T(8,128)} %reshape.435.mix_ref, bf16[2,2,12,24,256]{4,3,2,1,0:T(8,128)(2,1)} %reshape.436.forward_ref, bf16[2,2,12,24,256]{4,3,2,1,0:T(8,128)(2,1)} %reshape.437.backward_ref), custom_call_target="tpu_custom_call" | custom-call | tf_op jit(solution)/shard_map/pallas_call | solution.py:312
  9.6 1.0 %reshape.438 = f32[2,2,16,2,256]{4,3,2,1,0:T(2,128)S(1)} reshape(f32[2,2,32,256]{3,2,1,0:T(8,128)} %shard_map.68) | data formatting | bytes 262144 | tf_op jit(solution)/shard_map/reshape | solution.py:319
  10.7 0.2 reshape.439
  11.0 0.1 reshape_squeeze.18
  11.1 0.5 copy-done.2
  11.6 0.6 fusion.37
  12.3 0.7 iota_subtract_fusion
  13.0 0.6 add_subtract_fusion
  13.8 0.7 add_subtract_fusion.1
  14.5 0.1 fusion.25
  14.6 1.1 %add_sine_fusion = (f32[32,2,4,64]{3,2,1,0:T(4,128)S(1)}, f32[32,2,4,64]{3,2,1,0:T(4,128)S(1)}) fusion(f32[32,64]{1,0:T(8,128)S(1)} %fusion.27, f32[32,2,4]{2,1,0:T(2,128)S(1)} %fusion.25), kind=kLoop, calls=%fused_computation.19 | loop fusion | flops 16384 | bytes 140288 | tf_op jit(solution)/shard_map/sin | solution.py:253
  15.8 0.1 cos.28
  15.9 0.2 fusion.39
  16.1 0.1 reshape_squeeze.17
  16.2 0.1 sin.32
  16.3 0.2 fusion
  16.5 0.2 fusion.38
  16.7 0.2 fusion.1
  17.1 0.5 fusion.22
  17.6 0.3 convolution_bitcast_fusion.2
  17.9 0.2 copy.39
  18.1 1.1 %copy.40 = f32[16,32,2,2,4,4]{0,5,4,3,2,1:T(4,128)S(1)} copy(f32[16,32,2,2,4,4]{1,5,0,4,3,2:T(4,128)S(1)} %bitcast.100) | data formatting | bytes 262144 | tf_op jit(solution)/shard_map/transpose | solution.py:338
  19.3 0.3 copy.41
  19.6 0.7 reshape.443.blocks_ref
  20.3 12.9 %shard_map.69 = f32[16,17,128]{2,1,0:T(8,128)} custom-call(f32[16,17,128]{2,1,0:T(8,128)} %reshape.443.blocks_ref), custom_call_target="tpu_custom_call" | custom-call | tf_op jit(solution)/shard_map/pallas_call | solution.py:105
  33.2 1.0 %copy.77 = f32[2,8,17,128]{3,1,2,0:T(8,128)S(1)} copy(f32[2,8,17,128]{3,2,1,0:T(8,128)} %bitcast.103) | data formatting | bytes 278528
  34.2 0.3 copy.42
  34.6 0.6 copy.44
  35.2 0.6 convolution_bitcast_fusion.1
  35.8 0.2 copy.45
  36.0 0.5 copy.46
  36.6 0.2 copy.47
  36.8 0.7 pad_maximum_fusion.blocks_ref
  37.5 32.4 %shard_map.70 = (f32[32,9,128]{2,1,0:T(8,128)}, f32[16,1,128]{2,1,0:T(1,128)}) custom-call(f32[32,9,128]{2,1,0:T(8,128)} %pad_maximum_fusion.blocks_ref), custom_call_target="tpu_custom_call" | custom-call | tf_op jit(solution)/shard_map/pallas_call | solution.py:206
  69.9 0.9 %slice.66 = f32[32,8,128]{2,1,0:T(8,128)S(1)} slice(f32[32,9,128]{2,1,0:T(8,128)} %get-tuple-element.4), slice={[0:32], [0:8], [0:128]} | slice | bytes 262144 | tf_op jit(solution)/shard_map/slice | solution.py:223
  70.9 0.2 copy.48
  71.1 0.7 convolution_bitcast_fusion
  71.8 0.2 copy.51
  72.0 0.9 %reshape.447 = f32[16,2,2,2,256]{4,3,2,1,0:T(2,128)} reshape(f32[32,2,2,4,64]{4,3,2,1,0:T(4,128)S(1)} %copy.51) | data formatting | bytes 262144 | tf_op jit(solution)/shard_map/reshape | solution.py:351
  72.8 0.5 broadcast.453
  73.4 0.7 reduce.3
  74.0 0.7 reshape_squeeze.19
  (33 shorter events, 0.9 us)
Async XLA Ops:
  0.6 2.8 %copy-start = (bf16[2,2,12,12,2,256]{5,4,3,2,1,0:T(2,128)(2,1)S(1)}, bf16[2,2,12,12,2,256]{5,4,3,2,1,0:T(2,128)(2,1)}, u32[]{:S(2)}) copy-start(bf16[2,2,12,12,2,256]{5,4,3,2,1,0:T(2,128)(2,1)} %param.5) | copy-start | bytes 1769476
  3.4 1.1 %copy-start.1 = (bf16[2,2,12,12,2,256]{5,4,3,2,1,0:T(2,128)(2,1)S(1)}, bf16[2,2,12,12,2,256]{5,4,3,2,1,0:T(2,128)(2,1)}, u32[]{:S(2)}) copy-start(bf16[2,2,12,12,2,256]{5,4,3,2,1,0:T(2,128)(2,1)} %param.6) | copy-start | bytes 1769476
  11.0 0.7 copy-start.2
  12.3 0.7 copy-start.4
  72.0 1.4 %copy-start.3 = (f32[16,1,128]{2,1,0:T(1,128)S(1)}, f32[16,1,128]{2,1,0:T(1,128)}, u32[]{:S(2)}) copy-start(f32[16,1,128]{2,1,0:T(1,128)} %get-tuple-element.5) | copy-start | bytes 24580

commit v9 on v8

--- a/solution.py
+++ b/solution.py
@@ -119,6 +119,82 @@
     return got[:, :width], got[:, width:].sum(0)
 
 
+def turn_kernel(sent_ref, table_ref, ready_ref, landed_ref, send_sem, recv_sem):
+    parts = sent_ref.shape[0]
+    depth = sent_ref.shape[1] - 1
+    band = ready_ref.shape[1] - 1
+    me = lax.axis_index("sy")
+    mesh_ids = pl.DeviceIdType.MESH
+    barrier = pltpu.get_barrier_semaphore()
+    for step in range(1, parts):
+        pl.semaphore_signal(
+            barrier, 1, device_id={"sy": lax.rem(me + step, parts)}, device_id_type=mesh_ids
+        )
+    pl.semaphore_wait(barrier, parts - 1)
+
+    def copy_y(step, outgoing):
+        peer = lax.rem(me + (step if outgoing else parts - step), parts)
+        return pltpu.make_async_remote_copy(
+            src_ref=sent_ref.at[peer],
+            dst_ref=landed_ref.at[me if outgoing else peer],
+            send_sem=send_sem.at[step],
+            recv_sem=recv_sem.at[step],
+            device_id={"sy": peer},
+            device_id_type=mesh_ids,
+        )
+
+    @pl.loop(1, parts)
+    def _(step):
+        copy_y(step, True).start()
+
+    landed_ref[me] = sent_ref[me]
+
+    @pl.loop(1, parts)
+    def _(step):
+        copy_y(step, True).wait_send()
+
+    @pl.loop(1, parts)
+    def _(step):
+        copy_y(step, False).wait_recv()
+
+    block = landed_ref[:, 0:depth, :].reshape(parts * depth, -1)
+    turned = jnp.dot(table_ref[...], block, precision=HIGHEST, preferred_element_type=jnp.float32)
+    share = landed_ref[0, depth : depth + 1, :]
+    for source in range(1, parts):
+        share = share + landed_ref[source, depth : depth + 1, :]
+    for peer in range(ready_ref.shape[0]):
+        ready_ref[peer, 0:band, :] = turned[peer * band : (peer + 1) * band]
+        ready_ref[peer, band : band + 1, :] = share
+
+
+def turn(sent, table, parts_x, band):
+    parts_y, rows, width = sent.shape
+    vmem = pl.BlockSpec(memory_space=pltpu.VMEM)
+    return pl.pallas_call(
+        turn_kernel,
+        out_shape=jax.ShapeDtypeStruct((parts_x, band + 1, width), jnp.float32),
+        in_specs=[vmem, vmem],
+        out_specs=vmem,
+        scratch_shapes=[
+            pltpu.VMEM((parts_y, rows, width), jnp.float32),
+            pltpu.SemaphoreType.DMA((parts_y,)),
+            pltpu.SemaphoreType.DMA((parts_y,)),
+        ],
+        compiler_params=pltpu.CompilerParams(collective_id=0, has_side_effects=True),
+    )(sent, table)
+
+
+def turn_table(length, anchor, rows_y, share_y):
+    line = jnp.arange(2 * length, dtype=jnp.int32)
+    wave = line[:, None] // 2
+    out_part = line[:, None] % 2
+    in_part = (line[None, :] // rows_y) % 2
+    site = (line[None, :] // (2 * rows_y)) * rows_y + line[None, :] % rows_y
+    offset = jnp.mod(site - anchor, length)
+    index = jnp.mod(offset * wave + (length // 4) * (out_part - in_part), length)
+    return jnp.cos(2.0 * math.pi / length * index.astype(jnp.float32))
+
+
 def spread_kernel(blocks_ref, out_ref, gathered_ref, total_ref, b_send, b_recv, c_send, c_recv):
     parts_x = blocks_ref.shape[0]
     parts_y = gathered_ref.shape[0]
@@ -191,6 +267,30 @@
     @pl.loop(1, parts_y)
     def _(step):
         copy_y(step, False).wait_recv()
+
+
+def spread_ready(shaped):
+    parts_x = shaped.shape[0]
+    parts_y = lax.axis_size("sy")
+    vmem = pl.BlockSpec(memory_space=pltpu.VMEM)
+    got, gathered = pl.pallas_call(
+        spread_kernel,
+        out_shape=(
+            jax.ShapeDtypeStruct(shaped.shape, shaped.dtype),
+            jax.ShapeDtypeStruct((parts_y, 1, shaped.shape[2]), shaped.dtype),
+        ),
+        in_specs=[vmem],
+        out_specs=(vmem, vmem),
+        scratch_shapes=[
+            pltpu.VMEM((1, shaped.shape[2]), jnp.float32),
+            pltpu.SemaphoreType.DMA((parts_x,)),
+            pltpu.SemaphoreType.DMA((parts_x,)),
+            pltpu.SemaphoreType.DMA((parts_y,)),
+            pltpu.SemaphoreType.DMA((parts_y,)),
+        ],
+        compiler_params=pltpu.CompilerParams(collective_id=1, has_side_effects=True),
+    )(shaped)
+    return got[:, :-1], gathered[:, 0]
 
 
 def spread(blocks, share, parts_y):
@@ -332,22 +432,21 @@
     groups_y = lax.axis_size("sy")
     groups_x = lax.axis_size("sx")
     tables = dft_matrices(LZ, source_site)
-    along_z = jnp.einsum("nrxyz,rzsk->nsxyk", fields, tables[2], precision=HIGH)
     share_z = LZ // groups_y
-    blocks = along_z.reshape(count, 2, rows_x, rows_y, groups_y, share_z)
-    blocks = blocks.transpose(4, 0, 1, 2, 3, 5).reshape(groups_y, -1)
-    shares = partial.reshape(groups_y, -1)
-    blocks, share = exchange(blocks, shares, "sy", 0)
-    blocks = blocks.reshape(groups_y, count, 2, rows_x, rows_y, share_z)
-    table_y = tables[1].reshape(2, groups_y, rows_y, 2, -1)
-    along_y = jnp.einsum("jnrxyc,rjysk->nsxkc", blocks, table_y, precision=HIGH)
-    share_y = along_y.shape[3] // groups_x
-    blocks = along_y.reshape(count, 2, rows_x, groups_x, share_y, share_z)
-    blocks = blocks.transpose(3, 0, 1, 2, 4, 5).reshape(groups_x, -1)
-    blocks, gathered = spread(blocks, share, groups_y)
-    blocks = blocks.reshape(groups_x, count, 2, rows_x, share_y, share_z)
+    table_z = tables[2].reshape(2, LZ, 2, groups_y, share_z)
+    blocks = jnp.einsum("nrxyz,rzsjc->jsynxc", fields, table_z, precision=HIGH)
+    blocks = blocks.reshape(groups_y, 2 * rows_y, -1)
+    width = blocks.shape[2]
+    shares = partial.reshape(groups_y, 1, -1)
+    shares = jnp.pad(shares, ((0, 0), (0, 0), (0, width - shares.shape[2])))
+    share_y = rows_y * groups_y // groups_x
+    table_y = turn_table(rows_y * groups_y, source_site[1], rows_y, share_y)
+    ready = turn(jnp.concatenate([blocks, shares], 1), table_y, groups_x, 2 * share_y)
+    blocks, gathered = spread_ready(ready)
+    blocks = blocks.reshape(groups_x, share_y, 2, count, rows_x, share_z)
+    gathered = gathered[:, : partial.size // groups_y]
     table_x = tables[0].reshape(2, groups_x, rows_x, 2, -1)
-    spectrum = jnp.einsum("inrxbc,rixsk->nsbck", blocks, table_x, precision=HIGH)
+    spectrum = jnp.einsum("ibsnxc,sixtk->ntbck", blocks, table_x, precision=HIGH)
     corr = spectrum.reshape(inserts, slices, 2, share_y, -1)
     listed = gathered.reshape(2, inserts, slices, -1)
     return (corr, listed)

time: 75.2 us -> 78 us (1.037); the launches traced: 74.7 us -> 76.5 us
  Pallas kernels: 49.5 us -> 55.8 us
  local copies, waits for them, and re-layouts: 15.6 us -> 10.9 us
    pallas_call x2, Pallas kernels: 45.4 us -> 51.7 us  [the longest x1 35 us: spread_ready(): pl.pallas_call(spread_kernel, out_shape=(jax.ShapeDtypeStruct(shaped.shap...]
    transpose x5 -> x2, local copies, waits for them, and re-layouts: 2.26 us -> 0.63 us  [the longest x1 0.45 us: body(): blocks = jnp.einsum('nrxyz,rzsjc->jsynxc', fields, table_z, precision=HIGH)]
    cos x0 -> x1, other arithmetic: none -> 0.97 us  [turn_table(): return jnp.cos(2.0 * math.pi / length * index.astype(jnp.float32))]
    another operation x2 -> x0, local copies, waits for them, and re-layouts: 0.89 us -> none  [the longest x1 0.7 us: body(): listed = gathered.reshape(2, inserts, slices, -1)]
    unnamed x11, local copies, waits for them, and re-layouts: 1.54 us -> 0.67 us
    dot_general x3 -> x2, matrix products: 1.6 us -> 0.99 us  [the longest x1 0.5 us: body(): blocks = jnp.einsum('nrxyz,rzsjc->jsynxc', fields, table_z, precision=HIGH)]
    reshape x4 -> x3, local copies, waits for them, and re-layouts: 1.67 us -> 1.11 us  [the longest x1 0.71 us: body(): listed = gathered.reshape(2, inserts, slices, -1)]
where the time goes in v9:
time: 78 us; the launch traced here: 76.5 us
  Pallas kernels  55.8 us (72%)
  local copies, waits for them, and re-layouts  10.9 us (14%)
  other arithmetic  7.05 us (9%)
  matrix products  1.77 us (2%)
  between operations  0.92 us (1%)
    pallas_call x1, Pallas kernels, spread_ready(): pl.pallas_call(spread_kernel, out_shape=(jax.ShapeDtypeStruct(shaped.shap...  35 us
    pallas_call x1, Pallas kernels, turn(): pl.pallas_call(turn_kernel, out_shape=jax.ShapeDtypeStruct((parts_x, band...  16.7 us
    pallas_call x1, Pallas kernels, contract(): pl.pallas_call(contract_kernel, out_shape=jax.ShapeDtypeStruct((slices, r...  4.11 us

profile of v9, /device:TPU:1, one launch (start us, length us, event | category | flops | bytes accessed | tf_op | source)
XLA Modules:
  0.0 76.5 jit_solution(14966842929001364890)
XLA Ops:
  0.6 0.8 fusion.29
  1.4 0.7 slice.47
  2.1 0.1 eq.89
  2.3 0.3 copy.15
  2.7 0.8 reshape.597.mix_ref
  3.4 1.0 %reshape.598.forward_ref = bf16[2,2,12,24,256]{4,3,2,1,0:T(8,128)(2,1)} reshape(bf16[2,2,12,12,2,256]{5,4,3,2,1,0:T(2,128)(2,1)S(1)} %copy-done) | data formatting | bytes 1179648 | tf_op jit(solution)/shard_map/reshape | solution.py:407
  4.5 1.0 %reshape.599.backward_ref = bf16[2,2,12,24,256]{4,3,2,1,0:T(8,128)(2,1)} reshape(bf16[2,2,12,12,2,256]{5,4,3,2,1,0:T(2,128)(2,1)S(1)} %copy-done.1) | data formatting | bytes 1179648 | tf_op jit(solution)/shard_map/reshape | solution.py:408
  5.5 4.1 %shard_map.68 = f32[2,2,32,256]{3,2,1,0:T(8,128)} custom-call(f32[32,32]{1,0:T(8,128)} %reshape.597.mix_ref, bf16[2,2,12,24,256]{4,3,2,1,0:T(8,128)(2,1)} %reshape.598.forward_ref, bf16[2,2,12,24,256]{4,3,2,1,0:T(8,128)(2,1)} %reshape.599.backward_ref), custom_call_target="tpu_custom_call" | custom-call | tf_op jit(solution)/shard_map/pallas_call | solution.py:412
  9.6 1.0 %reshape.600 = f32[2,2,16,2,256]{4,3,2,1,0:T(2,128)S(1)} reshape(f32[2,2,32,256]{3,2,1,0:T(8,128)} %shard_map.68) | data formatting | bytes 262144 | tf_op jit(solution)/shard_map/reshape | solution.py:419
  10.6 0.1 copy.49
  10.7 0.2 reshape.601
  11.0 0.1 reshape_squeeze.14
  11.1 0.5 copy-done.3
  11.6 0.6 fusion.39
  12.2 0.6 add_subtract_fusion
  12.8 0.1 copy-done.4
  12.9 0.1 add_select_fusion.3
  13.0 0.7 add_subtract_fusion.1
  13.7 0.1 add_select_fusion.4
  13.7 0.1 fusion.22
  13.9 0.7 iota_subtract_fusion
  14.5 0.1 fusion.24
  14.6 1.1 %add_sine_fusion = (f32[32,2,4,64]{3,2,1,0:T(4,128)S(1)}, f32[32,2,4,64]{3,2,1,0:T(4,128)S(1)}) fusion(f32[32,64]{1,0:T(8,128)S(1)} %fusion.24, f32[32,2,4]{2,1,0:T(2,128)S(1)} %fusion.22), kind=kLoop, calls=%fused_computation.13 | loop fusion | flops 16384 | bytes 140288 | tf_op jit(solution)/shard_map/sin | solution.py:353
  15.7 0.1 cos.31
  15.8 0.2 fusion.40
  16.1 0.1 reshape_squeeze.15
  16.2 0.1 sin.32
  16.3 0.2 fusion.1
  16.5 0.2 fusion.41
  16.7 0.2 fusion
  16.9 0.1 reshape.603
  17.0 0.1 add_select_fusion.5
  17.1 0.5 fusion.19
  17.6 0.1 copy.14
  17.7 0.5 convolution_bitcast_fusion
  18.2 0.5 copy.19
  18.7 0.3 copy.20
  19.0 0.7 select_maximum_fusion.sent_ref
  19.7 0.6 and_select_fusion.4
  20.3 1.0 %fusion.16.table_ref = f32[128,128]{1,0:T(8,128)} fusion(s32[128]{0:T(128)S(1)} %get-tuple-element.30, s32[128]{0:T(128)S(1)} %get-tuple-element.31, s32[128]{0:T(128)S(1)} %get-tuple-element.32, s32[128]{0:T(128)S(1)} %get-tuple-element.33), kind=kLoop, calls=%fused_computation.37 | loop fusion | flops 278528 | bytes 67584 | tf_op jit(solution)/shard_map/cos | solution.py:195
  21.3 16.7 %shard_map.69.blocks_ref = f32[32,5,256]{2,1,0:T(8,128)} custom-call(f32[16,9,256]{2,1,0:T(8,128)} %select_maximum_fusion.sent_ref, f32[128,128]{1,0:T(8,128)} %fusion.16.table_ref), custom_call_target="tpu_custom_call" | custom-call | tf_op jit(solution)/shard_map/pallas_call | solution.py:173
  38.0 35.0 %shard_map.70 = (f32[32,5,256]{2,1,0:T(8,128)}, f32[16,1,256]{2,1,0:T(1,128)}) custom-call(f32[32,5,256]{2,1,0:T(8,128)} %shard_map.69.blocks_ref), custom_call_target="tpu_custom_call" | custom-call | tf_op jit(solution)/shard_map/pallas_call | solution.py:276
  73.0 1.0 %slice.58 = f32[32,4,256]{2,1,0:T(4,128)S(1)} slice(f32[32,5,256]{2,1,0:T(8,128)} %get-tuple-element.4), slice={[0:32], [0:4], [0:256]} | slice | bytes 262144 | tf_op jit(solution)/shard_map/slice | solution.py:293
  74.0 0.2 copy.21
  74.2 0.5 convolution_bitcast_fusion.1
  74.7 0.2 copy.24
  74.9 0.9 %reshape.605 = f32[16,2,2,2,256]{4,3,2,1,0:T(2,128)} reshape(f32[32,2,2,4,64]{4,3,2,1,0:T(4,128)S(1)} %copy.24) | data formatting | bytes 262144 | tf_op jit(solution)/shard_map/reshape | solution.py:450
  75.8 0.7 reshape.606
  (24 shorter events, 0.2 us)
Async XLA Ops:
  0.6 2.8 %copy-start = (bf16[2,2,12,12,2,256]{5,4,3,2,1,0:T(2,128)(2,1)S(1)}, bf16[2,2,12,12,2,256]{5,4,3,2,1,0:T(2,128)(2,1)}, u32[]{:S(2)}) copy-start(bf16[2,2,12,12,2,256]{5,4,3,2,1,0:T(2,128)(2,1)} %param.5) | copy-start | bytes 1769476
  3.4 1.1 %copy-start.1 = (bf16[2,2,12,12,2,256]{5,4,3,2,1,0:T(2,128)(2,1)S(1)}, bf16[2,2,12,12,2,256]{5,4,3,2,1,0:T(2,128)(2,1)}, u32[]{:S(2)}) copy-start(bf16[2,2,12,12,2,256]{5,4,3,2,1,0:T(2,128)(2,1)} %param.6) | copy-start | bytes 1769476
  11.0 0.7 copy-start.3
  12.2 0.7 copy-start.4
  74.9 0.9 %copy-start.2 = (f32[16,1,256]{2,1,0:T(1,128)S(1)}, f32[16,1,256]{2,1,0:T(1,128)}, u32[]{:S(2)}) copy-start(f32[16,1,256]{2,1,0:T(1,128)} %get-tuple-element.5) | copy-start | bytes 49156

commit v10 on v9

--- a/solution.py
+++ b/solution.py
@@ -157,13 +157,21 @@
     def _(step):
         copy_y(step, False).wait_recv()
 
+    lanes = ready_ref.shape[2]
+    halves = landed_ref.shape[2] // lanes
+    rows = band // halves
     block = landed_ref[:, 0:depth, :].reshape(parts * depth, -1)
-    turned = jnp.dot(table_ref[...], block, precision=HIGHEST, preferred_element_type=jnp.float32)
-    share = landed_ref[0, depth : depth + 1, :]
+    share = landed_ref[0, depth : depth + 1, 0:lanes]
     for source in range(1, parts):
-        share = share + landed_ref[source, depth : depth + 1, :]
+        share = share + landed_ref[source, depth : depth + 1, 0:lanes]
+    for half in range(halves):
+        turned = jnp.dot(
+            table_ref[...], block[:, half * lanes : (half + 1) * lanes], precision=HIGHEST,
+            preferred_element_type=jnp.float32,
+        )
+        for peer in range(ready_ref.shape[0]):
+            ready_ref[peer, half * rows : (half + 1) * rows, :] = turned[peer * rows : (peer + 1) * rows]
     for peer in range(ready_ref.shape[0]):
-        ready_ref[peer, 0:band, :] = turned[peer * band : (peer + 1) * band]
         ready_ref[peer, band : band + 1, :] = share
 
 
@@ -172,7 +180,7 @@
     vmem = pl.BlockSpec(memory_space=pltpu.VMEM)
     return pl.pallas_call(
         turn_kernel,
-        out_shape=jax.ShapeDtypeStruct((parts_x, band + 1, width), jnp.float32),
+        out_shape=jax.ShapeDtypeStruct((parts_x, band * width // 128 + 1, 128), jnp.float32),
         in_specs=[vmem, vmem],
         out_specs=vmem,
         scratch_shapes=[
@@ -443,6 +451,7 @@
     table_y = turn_table(rows_y * groups_y, source_site[1], rows_y, share_y)
     ready = turn(jnp.concatenate([blocks, shares], 1), table_y, groups_x, 2 * share_y)
     blocks, gathered = spread_ready(ready)
+    blocks = blocks.reshape(groups_x, width // 128, share_y, 2, 128).transpose(0, 2, 3, 1, 4)
     blocks = blocks.reshape(groups_x, share_y, 2, count, rows_x, share_z)
     gathered = gathered[:, : partial.size // groups_y]
     table_x = tables[0].reshape(2, groups_x, rows_x, 2, -1)

time: 78 us -> 74.5 us (0.955); the launches traced: 76.5 us -> 74 us
  Pallas kernels: 55.8 us -> 52.1 us
  other arithmetic: 7.05 us -> 7.88 us
    pallas_call x1, Pallas kernels: 35 us -> 31.3 us  [spread_ready(): pl.pallas_call(spread_kernel, out_shape=(jax.ShapeDtypeStruct(shaped.shap...]
where the time goes in v10:
time: 74.5 us; the launch traced here: 74 us
  Pallas kernels  52.1 us (70%)
  local copies, waits for them, and re-layouts  11.3 us (15%)
  other arithmetic  7.88 us (11%)
  matrix products  1.77 us (2%)
  between operations  0.92 us (1%)
    pallas_call x1, Pallas kernels, spread_ready(): pl.pallas_call(spread_kernel, out_shape=(jax.ShapeDtypeStruct(shaped.shap...  31.3 us
    pallas_call x1, Pallas kernels, turn(): pl.pallas_call(turn_kernel, out_shape=jax.ShapeDtypeStruct((parts_x, band...  16.7 us
    pallas_call x1, Pallas kernels, contract(): pl.pallas_call(contract_kernel, out_shape=jax.ShapeDtypeStruct((slices, r...  4.11 us

profile of v10, /device:TPU:1, one launch (start us, length us, event | category | flops | bytes accessed | tf_op | source)
XLA Modules:
  0.0 74.0 jit_solution(3589787787257919438)
XLA Ops:
  0.6 0.8 %fusion.29 = (f32[16,4,1]{0,2,1:T(1,128)S(1)}, f32[16,4,1]{0,2,1:T(1,128)S(1)}) fusion(s32[16,4,2]{0,2,1:T(2,128)} %param.7), kind=kLoop, calls=%fused_computation.85 | loop fusion | flops 640 | bytes 768 | tf_op jit(solution)/shard_map/sub | solution.py:25
  1.4 0.7 slice.44
  2.1 0.1 eq.89
  2.3 0.3 copy.14
  2.7 0.8 %reshape.597.mix_ref = f32[32,32]{1,0:T(8,128)} reshape(f32[16,2,16,2]{3,2,1,0:T(8,128)S(1)} %copy.14) | data formatting | bytes 8192 | tf_op jit(solution)/shard_map/reshape | solution.py:419
  3.4 1.0 %reshape.598.forward_ref = bf16[2,2,12,24,256]{4,3,2,1,0:T(8,128)(2,1)} reshape(bf16[2,2,12,12,2,256]{5,4,3,2,1,0:T(2,128)(2,1)S(1)} %copy-done) | data formatting | bytes 1179648 | tf_op jit(solution)/shard_map/reshape | solution.py:415
  4.5 1.0 %reshape.599.backward_ref = bf16[2,2,12,24,256]{4,3,2,1,0:T(8,128)(2,1)} reshape(bf16[2,2,12,12,2,256]{5,4,3,2,1,0:T(2,128)(2,1)S(1)} %copy-done.1) | data formatting | bytes 1179648 | tf_op jit(solution)/shard_map/reshape | solution.py:416
  5.5 4.1 %shard_map.68 = f32[2,2,32,256]{3,2,1,0:T(8,128)} custom-call(f32[32,32]{1,0:T(8,128)} %reshape.597.mix_ref, bf16[2,2,12,24,256]{4,3,2,1,0:T(8,128)(2,1)} %reshape.598.forward_ref, bf16[2,2,12,24,256]{4,3,2,1,0:T(8,128)(2,1)} %reshape.599.backward_ref), custom_call_target="tpu_custom_call" | custom-call | tf_op jit(solution)/shard_map/pallas_call | solution.py:420
  9.6 1.0 %reshape.600 = f32[2,2,16,2,256]{4,3,2,1,0:T(2,128)S(1)} reshape(f32[2,2,32,256]{3,2,1,0:T(8,128)} %shard_map.68) | data formatting | bytes 262144 | tf_op jit(solution)/shard_map/reshape | solution.py:427
  10.6 0.1 copy.46
  10.7 0.2 reshape.601
  11.0 0.1 reshape_squeeze.17
  11.1 0.5 copy-done.2
  11.6 0.6 fusion.39
  12.3 0.6 add_subtract_fusion
  13.0 0.1 add_select_fusion.3
  13.1 0.7 add_subtract_fusion.1
  13.7 0.1 add_select_fusion.4
  13.8 0.1 fusion.22
  13.9 0.7 iota_subtract_fusion
  14.6 0.1 fusion.24
  14.7 1.1 %add_sine_fusion = (f32[32,2,4,64]{3,2,1,0:T(4,128)S(1)}, f32[32,2,4,64]{3,2,1,0:T(4,128)S(1)}) fusion(f32[32,64]{1,0:T(8,128)S(1)} %fusion.24, f32[32,2,4]{2,1,0:T(2,128)S(1)} %fusion.22), kind=kLoop, calls=%fused_computation.13 | loop fusion | flops 16384 | bytes 140288 | tf_op jit(solution)/shard_map/sin | solution.py:361
  15.8 0.1 cos.31
  15.9 0.2 fusion.40
  16.1 0.1 reshape_squeeze.18
  16.2 0.1 sin.32
  16.3 0.2 fusion.1
  16.5 0.2 fusion.41
  16.7 0.2 fusion
  17.0 0.1 reshape.603
  17.1 0.5 fusion.19
  17.7 0.1 copy.13
  17.8 0.5 convolution_bitcast_fusion
  18.3 0.5 copy.18
  18.7 0.3 copy.19
  19.1 0.7 select_maximum_fusion.sent_ref
  19.8 0.6 and_select_fusion.4
  20.4 1.0 %fusion.16.table_ref = f32[128,128]{1,0:T(8,128)} fusion(s32[128]{0:T(128)S(1)} %get-tuple-element.30, s32[128]{0:T(128)S(1)} %get-tuple-element.31, s32[128]{0:T(128)S(1)} %get-tuple-element.32, s32[128]{0:T(128)S(1)} %get-tuple-element.33), kind=kLoop, calls=%fused_computation.37 | loop fusion | flops 278528 | bytes 67584 | tf_op jit(solution)/shard_map/cos | solution.py:203
  21.4 16.7 %shard_map.69.blocks_ref = f32[32,9,128]{2,1,0:T(8,128)} custom-call(f32[16,9,256]{2,1,0:T(8,128)} %select_maximum_fusion.sent_ref, f32[128,128]{1,0:T(8,128)} %fusion.16.table_ref), custom_call_target="tpu_custom_call" | custom-call | tf_op jit(solution)/shard_map/pallas_call | solution.py:181
  38.2 31.3 %shard_map.70 = (f32[32,9,128]{2,1,0:T(8,128)}, f32[16,1,128]{2,1,0:T(1,128)}) custom-call(f32[32,9,128]{2,1,0:T(8,128)} %shard_map.69.blocks_ref), custom_call_target="tpu_custom_call" | custom-call | tf_op jit(solution)/shard_map/pallas_call | solution.py:284
  69.5 0.9 %slice.55 = f32[32,8,128]{2,1,0:T(8,128)S(1)} slice(f32[32,9,128]{2,1,0:T(8,128)} %get-tuple-element.4), slice={[0:32], [0:8], [0:128]} | slice | bytes 262144 | tf_op jit(solution)/shard_map/slice | solution.py:301
  70.4 0.2 copy.20
  70.6 0.5 convolution_bitcast_fusion.1
  71.1 0.2 copy.23
  71.3 0.9 %reshape.606 = f32[16,2,2,2,256]{4,3,2,1,0:T(2,128)} reshape(f32[32,2,2,4,64]{4,3,2,1,0:T(4,128)S(1)} %copy.23) | data formatting | bytes 262144 | tf_op jit(solution)/shard_map/reshape | solution.py:459
  72.2 0.5 broadcast.690
  72.7 0.7 reduce.3
  73.3 0.7 reshape_squeeze.19
  (24 shorter events, 0.4 us)
Async XLA Ops:
  0.6 2.8 %copy-start = (bf16[2,2,12,12,2,256]{5,4,3,2,1,0:T(2,128)(2,1)S(1)}, bf16[2,2,12,12,2,256]{5,4,3,2,1,0:T(2,128)(2,1)}, u32[]{:S(2)}) copy-start(bf16[2,2,12,12,2,256]{5,4,3,2,1,0:T(2,128)(2,1)} %param.5) | copy-start | bytes 1769476
  3.4 1.1 %copy-start.1 = (bf16[2,2,12,12,2,256]{5,4,3,2,1,0:T(2,128)(2,1)S(1)}, bf16[2,2,12,12,2,256]{5,4,3,2,1,0:T(2,128)(2,1)}, u32[]{:S(2)}) copy-start(bf16[2,2,12,12,2,256]{5,4,3,2,1,0:T(2,128)(2,1)} %param.6) | copy-start | bytes 1769476
  11.0 0.7 copy-start.2
  12.3 0.7 copy-start.4
  71.3 1.4 %copy-start.3 = (f32[16,1,128]{2,1,0:T(1,128)S(1)}, f32[16,1,128]{2,1,0:T(1,128)}, u32[]{:S(2)}) copy-start(f32[16,1,128]{2,1,0:T(1,128)} %get-tuple-element.5) | copy-start | bytes 24580

commit v11 on v10

--- a/solution.py
+++ b/solution.py
@@ -119,7 +119,7 @@
     return got[:, :width], got[:, width:].sum(0)
 
 
-def turn_kernel(sent_ref, table_ref, ready_ref, landed_ref, send_sem, recv_sem):
+def turn_kernel(anchor_ref, sent_ref, ready_ref, landed_ref, table_ref, send_sem, recv_sem):
     parts = sent_ref.shape[0]
     depth = sent_ref.shape[1] - 1
     band = ready_ref.shape[1] - 1
@@ -130,6 +130,9 @@
         pl.semaphore_signal(
             barrier, 1, device_id={"sy": lax.rem(me + step, parts)}, device_id_type=mesh_ids
         )
+    table_ref[...] = turn_table(
+        parts * depth // 2, anchor_ref[0], depth // 2, ready_ref.shape[1] // 2, table_ref.shape
+    )
     pl.semaphore_wait(barrier, parts - 1)
 
     def copy_y(step, outgoing):
@@ -175,32 +178,34 @@
         ready_ref[peer, band : band + 1, :] = share
 
 
-def turn(sent, table, parts_x, band):
+def turn(sent, anchor, parts_x, band):
     parts_y, rows, width = sent.shape
     vmem = pl.BlockSpec(memory_space=pltpu.VMEM)
     return pl.pallas_call(
         turn_kernel,
         out_shape=jax.ShapeDtypeStruct((parts_x, band * width // 128 + 1, 128), jnp.float32),
-        in_specs=[vmem, vmem],
+        in_specs=[pl.BlockSpec(memory_space=pltpu.SMEM), vmem],
         out_specs=vmem,
         scratch_shapes=[
             pltpu.VMEM((parts_y, rows, width), jnp.float32),
+            pltpu.VMEM((parts_y * (rows - 1), parts_y * (rows - 1)), jnp.float32),
             pltpu.SemaphoreType.DMA((parts_y,)),
             pltpu.SemaphoreType.DMA((parts_y,)),
         ],
         compiler_params=pltpu.CompilerParams(collective_id=0, has_side_effects=True),
-    )(sent, table)
-
-
-def turn_table(length, anchor, rows_y, share_y):
-    line = jnp.arange(2 * length, dtype=jnp.int32)
-    wave = line[:, None] // 2
-    out_part = line[:, None] % 2
-    in_part = (line[None, :] // rows_y) % 2
-    site = (line[None, :] // (2 * rows_y)) * rows_y + line[None, :] % rows_y
-    offset = jnp.mod(site - anchor, length)
-    index = jnp.mod(offset * wave + (length // 4) * (out_part - in_part), length)
-    return jnp.cos(2.0 * math.pi / length * index.astype(jnp.float32))
+    )(anchor, sent)
+
+
+def turn_table(length, anchor, rows_y, share_y, shape):
+    line = lax.broadcasted_iota(jnp.int32, shape, 0)
+    column = lax.broadcasted_iota(jnp.int32, shape, 1)
+    wave = line // 2
+    out_part = line % 2
+    in_part = (column // rows_y) % 2
+    site = (column // (2 * rows_y)) * rows_y + column % rows_y
+    offset = (site - anchor + length) % length
+    index = (offset * wave + (length // 4) * (out_part - in_part) + length) % length
+    return jnp.cos((2.0 * math.pi / length) * index.astype(jnp.float32))
 
 
 def spread_kernel(blocks_ref, out_ref, gathered_ref, total_ref, b_send, b_recv, c_send, c_recv):
@@ -448,8 +453,7 @@
     shares = partial.reshape(groups_y, 1, -1)
     shares = jnp.pad(shares, ((0, 0), (0, 0), (0, width - shares.shape[2])))
     share_y = rows_y * groups_y // groups_x
-    table_y = turn_table(rows_y * groups_y, source_site[1], rows_y, share_y)
-    ready = turn(jnp.concatenate([blocks, shares], 1), table_y, groups_x, 2 * share_y)
+    ready = turn(jnp.concatenate([blocks, shares], 1), source_site[1:2], groups_x, 2 * share_y)
     blocks, gathered = spread_ready(ready)
     blocks = blocks.reshape(groups_x, width // 128, share_y, 2, 128).transpose(0, 2, 3, 1, 4)
     blocks = blocks.reshape(groups_x, share_y, 2, count, rows_x, share_z)

time: 74.5 us -> 73.3 us (0.984)
  other arithmetic: 7.88 us -> 6.21 us
    cos x1 -> x0, other arithmetic: 0.97 us -> none  [turn_table(): return jnp.cos(2.0 * math.pi / length * index.astype(jnp.float32))]
where the time goes in v11:
time: 73.3 us; the launch traced here: 72.9 us
  Pallas kernels  52.8 us (72%)
  local copies, waits for them, and re-layouts  11.3 us (15%)
  other arithmetic  6.21 us (8%)
  matrix products  1.77 us (2%)
  between operations  0.91 us (1%)
    pallas_call x1, Pallas kernels, spread_ready(): pl.pallas_call(spread_kernel, out_shape=(jax.ShapeDtypeStruct(shaped.shap...  31.3 us
    pallas_call x1, Pallas kernels, turn(): pl.pallas_call(turn_kernel, out_shape=jax.ShapeDtypeStruct((parts_x, band...  17.4 us
    pallas_call x1, Pallas kernels, contract(): pl.pallas_call(contract_kernel, out_shape=jax.ShapeDtypeStruct((slices, r...  4.11 us

profile of v11, /device:TPU:1, one launch (start us, length us, event | category | flops | bytes accessed | tf_op | source)
XLA Modules:
  0.0 72.9 jit_solution(5044221593826254805)
XLA Ops:
  0.6 0.8 %fusion.25 = (f32[16,4,1]{0,2,1:T(1,128)S(1)}, f32[16,4,1]{0,2,1:T(1,128)S(1)}) fusion(s32[16,4,2]{0,2,1:T(2,128)} %param.7), kind=kLoop, calls=%fused_computation.74 | loop fusion | flops 640 | bytes 768 | tf_op jit(solution)/shard_map/sub | solution.py:25
  1.4 0.7 slice.45
  2.1 0.1 eq.81
  2.2 0.1 fusion.27
  2.3 0.3 copy.14
  2.7 0.8 %reshape.422.mix_ref = f32[32,32]{1,0:T(8,128)} reshape(f32[16,2,16,2]{3,2,1,0:T(8,128)S(1)} %copy.14) | data formatting | bytes 8192 | tf_op jit(solution)/shard_map/reshape | solution.py:424
  3.4 1.0 %reshape.423.forward_ref = bf16[2,2,12,24,256]{4,3,2,1,0:T(8,128)(2,1)} reshape(bf16[2,2,12,12,2,256]{5,4,3,2,1,0:T(2,128)(2,1)S(1)} %copy-done) | data formatting | bytes 1179648 | tf_op jit(solution)/shard_map/reshape | solution.py:420
  4.5 1.0 %reshape.424.backward_ref = bf16[2,2,12,24,256]{4,3,2,1,0:T(8,128)(2,1)} reshape(bf16[2,2,12,12,2,256]{5,4,3,2,1,0:T(2,128)(2,1)S(1)} %copy-done.1) | data formatting | bytes 1179648 | tf_op jit(solution)/shard_map/reshape | solution.py:421
  5.5 4.1 %shard_map.68 = f32[2,2,32,256]{3,2,1,0:T(8,128)} custom-call(f32[32,32]{1,0:T(8,128)} %reshape.422.mix_ref, bf16[2,2,12,24,256]{4,3,2,1,0:T(8,128)(2,1)} %reshape.423.forward_ref, bf16[2,2,12,24,256]{4,3,2,1,0:T(8,128)(2,1)} %reshape.424.backward_ref), custom_call_target="tpu_custom_call" | custom-call | tf_op jit(solution)/shard_map/pallas_call | solution.py:425
  9.6 1.0 %reshape.425 = f32[2,2,16,2,256]{4,3,2,1,0:T(2,128)S(1)} reshape(f32[2,2,32,256]{3,2,1,0:T(8,128)} %shard_map.68) | data formatting | bytes 262144 | tf_op jit(solution)/shard_map/reshape | solution.py:432
  10.6 0.1 copy.46
  10.7 0.2 reshape.426
  11.0 0.1 reshape_squeeze.17
  11.1 0.5 copy-done.2
  11.6 0.6 fusion.29
  12.2 0.7 add_subtract_fusion
  12.9 0.1 add_select_fusion.2
  13.0 0.7 add_subtract_fusion.1
  13.7 0.1 add_select_fusion.3
  13.7 0.1 fusion.18
  13.9 0.6 iota_subtract_fusion
  14.4 0.1 fusion.20
  14.5 1.1 %add_sine_fusion = (f32[32,2,4,64]{3,2,1,0:T(4,128)S(1)}, f32[32,2,4,64]{3,2,1,0:T(4,128)S(1)}) fusion(f32[32,64]{1,0:T(8,128)S(1)} %fusion.20, f32[32,2,4]{2,1,0:T(2,128)S(1)} %fusion.18), kind=kLoop, calls=%fused_computation.13 | loop fusion | flops 16384 | bytes 140288 | tf_op jit(solution)/shard_map/sin | solution.py:366
  15.6 0.1 cos.28
  15.8 0.2 fusion.30
  16.0 0.1 reshape_squeeze.18
  16.1 0.1 sin.32
  16.2 0.2 fusion.1
  16.4 0.2 fusion.31
  16.6 0.2 fusion
  16.8 0.1 reshape.428
  16.9 0.1 add_select_fusion.4
  17.0 0.5 fusion.15
  17.5 0.1 copy.13
  17.6 0.5 convolution_bitcast_fusion
  18.1 0.5 copy.18
  18.6 0.3 copy.19
  18.9 0.7 select_maximum_fusion.sent_ref
  19.7 17.4 %shard_map.69.blocks_ref = f32[32,9,128]{2,1,0:T(8,128)} custom-call(s32[1]{0:T(128)} %get-tuple-element.28.anchor_ref, f32[16,9,256]{2,1,0:T(8,128)} %select_maximum_fusion.sent_ref), custom_call_target="tpu_custom_call" | custom-call | tf_op jit(solution)/shard_map/pallas_call | solution.py:184
  37.0 31.3 %shard_map.70 = (f32[32,9,128]{2,1,0:T(8,128)}, f32[16,1,128]{2,1,0:T(1,128)}) custom-call(f32[32,9,128]{2,1,0:T(8,128)} %shard_map.69.blocks_ref), custom_call_target="tpu_custom_call" | custom-call | tf_op jit(solution)/shard_map/pallas_call | solution.py:289
  68.3 0.9 %slice.55 = f32[32,8,128]{2,1,0:T(8,128)S(1)} slice(f32[32,9,128]{2,1,0:T(8,128)} %get-tuple-element.4), slice={[0:32], [0:8], [0:128]} | slice | bytes 262144 | tf_op jit(solution)/shard_map/slice | solution.py:306
  69.2 0.2 copy.20
  69.5 0.5 convolution_bitcast_fusion.1
  70.0 0.2 copy.23
  70.2 0.9 %reshape.431 = f32[16,2,2,2,256]{4,3,2,1,0:T(2,128)} reshape(f32[32,2,2,4,64]{4,3,2,1,0:T(4,128)S(1)} %copy.23) | data formatting | bytes 262144 | tf_op jit(solution)/shard_map/reshape | solution.py:463
  71.0 0.5 broadcast.457
  71.5 0.7 reduce.3
  72.2 0.7 reshape_squeeze.19
  (21 shorter events, 0.2 us)
Async XLA Ops:
  0.6 2.8 %copy-start = (bf16[2,2,12,12,2,256]{5,4,3,2,1,0:T(2,128)(2,1)S(1)}, bf16[2,2,12,12,2,256]{5,4,3,2,1,0:T(2,128)(2,1)}, u32[]{:S(2)}) copy-start(bf16[2,2,12,12,2,256]{5,4,3,2,1,0:T(2,128)(2,1)} %param.5) | copy-start | bytes 1769476
  3.4 1.1 %copy-start.1 = (bf16[2,2,12,12,2,256]{5,4,3,2,1,0:T(2,128)(2,1)S(1)}, bf16[2,2,12,12,2,256]{5,4,3,2,1,0:T(2,128)(2,1)}, u32[]{:S(2)}) copy-start(bf16[2,2,12,12,2,256]{5,4,3,2,1,0:T(2,128)(2,1)} %param.6) | copy-start | bytes 1769476
  11.0 0.7 copy-start.2
  12.2 0.7 copy-start.4
  70.1 1.4 %copy-start.3 = (f32[16,1,128]{2,1,0:T(1,128)S(1)}, f32[16,1,128]{2,1,0:T(1,128)}, u32[]{:S(2)}) copy-start(f32[16,1,128]{2,1,0:T(1,128)} %get-tuple-element.5) | copy-start | bytes 24580

commit v12 on v11

--- a/solution.py
+++ b/solution.py
@@ -375,9 +375,30 @@
     return (local_re, local_im)
 
 
-def contract_kernel(mix_ref, forward_ref, backward_ref, out_ref, pair_ref):
+def gamma_mix(table_ref, inserts):
+    shape = (inserts * 2, 32)
+    line = lax.broadcasted_iota(jnp.int32, shape, 0)
+    column = lax.broadcasted_iota(jnp.int32, shape, 1)
+    out_part = line % 2
+    in_part = column % 2
+    same = out_part == in_part
+    sign = 2 * out_part - 1
+    mix = jnp.zeros(shape, jnp.int32)
+    for g in range(inserts):
+        for s in range(4):
+            target = table_ref[g * 8 + s * 2]
+            power = table_ref[g * 8 + s * 2 + 1]
+            unit_re = jnp.where(power == 0, 1, 0) - jnp.where(power == 2, 1, 0)
+            unit_im = jnp.where(power == 1, 1, 0) - jnp.where(power == 3, 1, 0)
+            hit = (line // 2 == g) & (column // 2 == s * 4 + target)
+            mix = jnp.where(hit, jnp.where(same, unit_re, sign * unit_im), mix)
+    return mix.astype(jnp.float32)
+
+
+def contract_kernel(gamma_ref, forward_ref, backward_ref, out_ref, pair_ref):
     slices = forward_ref.shape[0]
     rows = forward_ref.shape[3]
+    mix = gamma_mix(gamma_ref, out_ref.shape[2] // 2)
     for t in range(slices):
         for u in range(4):
             f_re = [forward_ref[t, 0, 3 * u + c].astype(jnp.float32) for c in range(3)]
@@ -396,7 +417,7 @@
                 pair_ref[base : base + rows, :] = acc_re
                 pair_ref[base + rows : base + 2 * rows, :] = acc_im
         width = pair_ref.shape[0]
-        kinds = mix_ref.shape[1]
+        kinds = mix.shape[1]
         lines = out_ref.shape[1] * kinds
         row = lax.broadcasted_iota(jnp.int32, (lines, width), 0)
         col = lax.broadcasted_iota(jnp.int32, (lines, width), 1)
@@ -407,7 +428,7 @@
         )
         for x in range(out_ref.shape[1]):
             out_ref[t, x] = jnp.dot(
-                mix_ref[...], summed[x * kinds : (x + 1) * kinds], precision=HIGHEST,
+                mix, summed[x * kinds : (x + 1) * kinds], precision=HIGHEST,
                 preferred_element_type=jnp.float32,
             )
 
@@ -419,16 +440,14 @@
     inserts = gamma_table.shape[0]
     forward = forward_prop.reshape(slices, 2, 12, 12 * rows_x, sites)
     backward = backward_prop.reshape(slices, 2, 12, 12 * rows_x, sites)
-    mat_re, mat_im = gamma_matrices(gamma_table)
-    mix = jnp.stack([jnp.stack([mat_re, -mat_im], 2), jnp.stack([mat_im, mat_re], 2)], 1)
-    mix = mix.reshape(inserts * 2, 16 * 2)
     out = pl.pallas_call(
         contract_kernel,
         out_shape=jax.ShapeDtypeStruct((slices, rows_x, inserts * 2, sites), jnp.float32),
-        in_specs=[pl.BlockSpec(memory_space=pltpu.VMEM)] * 3,
+        in_specs=[pl.BlockSpec(memory_space=pltpu.SMEM)]
+        + [pl.BlockSpec(memory_space=pltpu.VMEM)] * 2,
         out_specs=pl.BlockSpec(memory_space=pltpu.VMEM),
         scratch_shapes=[pltpu.VMEM((16 * 2 * 12 * rows_x, sites), jnp.float32)],
-    )(mix, forward, backward)
+    )(gamma_table.reshape(-1), forward, backward)
     return out.reshape(slices, rows_x, inserts, 2, sites).transpose(2, 0, 3, 1, 4)
 
 

time: 73.3 us -> 73 us (level)
  other arithmetic: 6.21 us -> 5.35 us
    slice x1, local copies, waits for them, and re-layouts: 0.01 us -> 0.8 us  [project_sites(): part_x = jnp.mod(momenta[:, 0:1] * coord_x[None, :], length)]
    slice x1, local copies, waits for them, and re-layouts: 0.59 us -> 1.36 us  [project_sites(): source_site[0]]
    sub x1 -> x0, other arithmetic: 0.76 us -> none  [gamma_matrices(): (powers == 0).astype(jnp.float32) - (powers == 2).astype(jnp.float32)]
where the time goes in v12:
time: 73 us; the launch traced here: 72.6 us
  Pallas kernels  52.8 us (72%)
  local copies, waits for them, and re-layouts  11.7 us (16%)
  other arithmetic  5.35 us (7%)
  matrix products  1.77 us (2%)
  between operations  0.88 us (1%)
    pallas_call x1, Pallas kernels, spread_ready(): pl.pallas_call(spread_kernel, out_shape=(jax.ShapeDtypeStruct(shaped.shap...  31.3 us
    pallas_call x1, Pallas kernels, turn(): pl.pallas_call(turn_kernel, out_shape=jax.ShapeDtypeStruct((parts_x, band...  17.3 us
    pallas_call x1, Pallas kernels, contract(): pl.pallas_call(contract_kernel, out_shape=jax.ShapeDtypeStruct((slices, r...  4.21 us

profile of v12, /device:TPU:1, one launch (start us, length us, event | category | flops | bytes accessed | tf_op | source)
XLA Modules:
  0.0 72.6 jit_solution(756504638717263378)
XLA Ops:
  0.6 1.4 %fusion.26 = (s32[1]{0:T(128)}, s32[1]{0:T(128)}, s32[1]{0:T(128)}) fusion(s32[3]{0:T(128)} %param.8), kind=kLoop, calls=%fused_computation.71 | loop fusion | bytes 24 | tf_op jit(solution)/shard_map/slice | solution.py:353
  2.0 0.6 add_subtract_fusion
  2.6 0.8 %slice_bitcast_fusion.2 = (s32[32]{0:T(128)S(1)}, s32[32]{0:T(128)S(1)}, s32[32]{0:T(128)S(1)}) fusion(s32[32,3]{0,1:T(4,128)} %param.9), kind=kLoop, calls=%fused_computation.69 | loop fusion | bytes 768 | tf_op jit(solution)/shard_map/slice | solution.py:356
  3.4 0.1 add_select_fusion.2
  3.5 0.7 add_subtract_fusion.1
  4.1 0.1 add_select_fusion.3
  4.2 0.1 fusion.18
  4.3 0.7 iota_subtract_fusion
  5.0 0.1 fusion.20
  5.1 1.1 %add_sine_fusion = (f32[32,2,4,64]{3,2,1,0:T(4,128)S(1)}, f32[32,2,4,64]{3,2,1,0:T(4,128)S(1)}) fusion(f32[32,64]{1,0:T(8,128)S(1)} %fusion.20, f32[32,2,4]{2,1,0:T(2,128)S(1)} %fusion.18), kind=kLoop, calls=%fused_computation.13 | loop fusion | flops 16384 | bytes 140288 | tf_op jit(solution)/shard_map/sin | solution.py:366
  6.2 0.1 cos.28
  6.3 1.0 %reshape.294.forward_ref = bf16[2,2,12,24,256]{4,3,2,1,0:T(8,128)(2,1)} reshape(bf16[2,2,12,12,2,256]{5,4,3,2,1,0:T(2,128)(2,1)S(1)} %copy-done) | data formatting | bytes 1179648 | tf_op jit(solution)/shard_map/reshape | solution.py:441
  7.4 0.0 copy-done.1
  7.4 1.0 %reshape.295.backward_ref = bf16[2,2,12,24,256]{4,3,2,1,0:T(8,128)(2,1)} reshape(bf16[2,2,12,12,2,256]{5,4,3,2,1,0:T(2,128)(2,1)S(1)} %copy-done.1) | data formatting | bytes 1179648 | tf_op jit(solution)/shard_map/reshape | solution.py:442
  8.4 0.1 copy.11
  8.5 0.7 reshape.293.gamma_ref
  9.2 4.2 %shard_map.68 = f32[2,2,32,256]{3,2,1,0:T(8,128)} custom-call(s32[128]{0:T(128)} %reshape.293.gamma_ref, bf16[2,2,12,24,256]{4,3,2,1,0:T(8,128)(2,1)} %reshape.294.forward_ref, bf16[2,2,12,24,256]{4,3,2,1,0:T(8,128)(2,1)} %reshape.295.backward_ref), custom_call_target="tpu_custom_call" | custom-call | tf_op jit(solution)/shard_map/pallas_call | solution.py:443
  13.4 1.0 %reshape.296 = f32[2,2,16,2,256]{4,3,2,1,0:T(2,128)S(1)} reshape(f32[2,2,32,256]{3,2,1,0:T(8,128)} %shard_map.68) | data formatting | bytes 262144 | tf_op jit(solution)/shard_map/reshape | solution.py:451
  14.4 0.1 copy.43
  14.5 0.2 reshape.297
  14.8 0.1 reshape_squeeze.17
  14.9 0.2 fusion.27
  15.1 0.1 sin.32
  15.2 0.1 reshape_squeeze.18
  15.3 0.2 fusion.1
  15.5 0.2 fusion.28
  15.7 0.2 fusion
  15.9 0.0 copy-start.2
  15.9 0.1 reshape.299
  16.0 0.6 copy-done.2
  16.6 0.1 add_select_fusion.4
  16.7 0.5 fusion.15
  17.2 0.1 copy.10
  17.3 0.5 convolution_bitcast_fusion
  17.8 0.5 copy.15
  18.3 0.3 copy.16
  18.6 0.7 %select_maximum_fusion.sent_ref = f32[16,9,256]{2,1,0:T(8,128)} fusion(f32[16,1,128]{2,1,0:T(1,128)S(1)} %reshape.299, f32[16,8,256]{2,1,0:T(8,128)S(1)} %copy.16), kind=kLoop, calls=%fused_computation.8 | loop fusion | flops 110592 | bytes 286720 | tf_op jit(solution)/shard_map/concatenate | solution.py:475
  19.3 17.3 %shard_map.69.blocks_ref = f32[32,9,128]{2,1,0:T(8,128)} custom-call(s32[1]{0:T(128)} %get-tuple-element.21.anchor_ref, f32[16,9,256]{2,1,0:T(8,128)} %select_maximum_fusion.sent_ref), custom_call_target="tpu_custom_call" | custom-call | tf_op jit(solution)/shard_map/pallas_call | solution.py:184
  36.7 31.3 %shard_map.70 = (f32[32,9,128]{2,1,0:T(8,128)}, f32[16,1,128]{2,1,0:T(1,128)}) custom-call(f32[32,9,128]{2,1,0:T(8,128)} %shard_map.69.blocks_ref), custom_call_target="tpu_custom_call" | custom-call | tf_op jit(solution)/shard_map/pallas_call | solution.py:289
  68.0 0.9 %slice.47 = f32[32,8,128]{2,1,0:T(8,128)S(1)} slice(f32[32,9,128]{2,1,0:T(8,128)} %get-tuple-element.4), slice={[0:32], [0:8], [0:128]} | slice | bytes 262144 | tf_op jit(solution)/shard_map/slice | solution.py:306
  68.9 0.2 copy.17
  69.1 0.5 convolution_bitcast_fusion.1
  69.6 0.2 copy.20
  69.8 0.9 %reshape.302 = f32[16,2,2,2,256]{4,3,2,1,0:T(2,128)} reshape(f32[32,2,2,4,64]{4,3,2,1,0:T(4,128)S(1)} %copy.20) | data formatting | bytes 262144 | tf_op jit(solution)/shard_map/reshape | solution.py:482
  70.7 0.5 broadcast.378
  71.2 0.0 copy-done.3
  71.2 0.7 reduce.3
  71.8 0.7 reshape_squeeze.19
  (10 shorter events, 0.1 us)
Async XLA Ops:
  0.6 5.7 %copy-start = (bf16[2,2,12,12,2,256]{5,4,3,2,1,0:T(2,128)(2,1)S(1)}, bf16[2,2,12,12,2,256]{5,4,3,2,1,0:T(2,128)(2,1)}, u32[]{:S(2)}) copy-start(bf16[2,2,12,12,2,256]{5,4,3,2,1,0:T(2,128)(2,1)} %param.5) | copy-start | bytes 1769476
  6.3 1.1 %copy-start.1 = (bf16[2,2,12,12,2,256]{5,4,3,2,1,0:T(2,128)(2,1)S(1)}, bf16[2,2,12,12,2,256]{5,4,3,2,1,0:T(2,128)(2,1)}, u32[]{:S(2)}) copy-start(bf16[2,2,12,12,2,256]{5,4,3,2,1,0:T(2,128)(2,1)} %param.6) | copy-start | bytes 1769476
  7.4 1.0 %copy-start.4 = (s32[16,4,2]{0,2,1:T(2,128)S(1)}, s32[16,4,2]{0,2,1:T(2,128)}, u32[]{:S(2)}) copy-start(s32[16,4,2]{0,2,1:T(2,128)} %param.7) | copy-start | bytes 1540
  15.9 0.7 copy-start.2
  69.8 1.4 %copy-start.3 = (f32[16,1,128]{2,1,0:T(1,128)S(1)}, f32[16,1,128]{2,1,0:T(1,128)}, u32[]{:S(2)}) copy-start(f32[16,1,128]{2,1,0:T(1,128)} %get-tuple-element.5) | copy-start | bytes 24580

commit v13 on v12

--- a/solution.py
+++ b/solution.py
@@ -379,7 +379,7 @@
     shape = (inserts * 2, 32)
     line = lax.broadcasted_iota(jnp.int32, shape, 0)
     column = lax.broadcasted_iota(jnp.int32, shape, 1)
-    out_part = line % 2
+    out_part = line // inserts
     in_part = column % 2
     same = out_part == in_part
     sign = 2 * out_part - 1
@@ -390,15 +390,43 @@
             power = table_ref[g * 8 + s * 2 + 1]
             unit_re = jnp.where(power == 0, 1, 0) - jnp.where(power == 2, 1, 0)
             unit_im = jnp.where(power == 1, 1, 0) - jnp.where(power == 3, 1, 0)
-            hit = (line // 2 == g) & (column // 2 == s * 4 + target)
+            hit = (line % inserts == g) & (column // 2 == s * 4 + target)
             mix = jnp.where(hit, jnp.where(same, unit_re, sign * unit_im), mix)
     return mix.astype(jnp.float32)
 
 
-def contract_kernel(gamma_ref, forward_ref, backward_ref, out_ref, pair_ref):
+def phase_tables(moment_ref, site_ref, x, sites, count):
+    span = lax.broadcasted_iota(jnp.int32, (1, count), 1)
+    wave = [jnp.zeros((1, count), jnp.int32) for _ in range(3)]
+    for m in range(count):
+        for axis in range(3):
+            wave[axis] = jnp.where(span == m, moment_ref[m * 3 + axis], wave[axis])
+    rows_y = sites // LZ
+    place = lax.broadcasted_iota(jnp.int32, (sites, 1), 0)
+    coord_x = x - site_ref[0]
+    coord_y = lax.axis_index("sy") * rows_y + place // LZ - site_ref[1]
+    coord_z = place % LZ - site_ref[2]
+    phase = wave[0] * coord_x + wave[1] * coord_y + wave[2] * coord_z
+    phase = (phase % L + L) % L
+    angle = (2.0 * math.pi / L) * phase.astype(jnp.float32)
+    return jnp.cos(angle), jnp.sin(angle)
+
+
+def contract_kernel(
+    gamma_ref, moment_ref, site_ref, forward_ref, backward_ref, out_ref, local_ref, pair_ref
+):
     slices = forward_ref.shape[0]
     rows = forward_ref.shape[3]
-    mix = gamma_mix(gamma_ref, out_ref.shape[2] // 2)
+    inserts = out_ref.shape[2] // 2
+    mix = gamma_mix(gamma_ref, inserts)
+    rows_x = out_ref.shape[1]
+    tables = [
+        phase_tables(
+            moment_ref, site_ref, lax.axis_index("sx") * rows_x + x, out_ref.shape[3],
+            local_ref.shape[3],
+        )
+        for x in range(rows_x)
+    ]
     for t in range(slices):
         for u in range(4):
             f_re = [forward_ref[t, 0, 3 * u + c].astype(jnp.float32) for c in range(3)]
@@ -426,29 +454,46 @@
             pick.astype(jnp.float32), pair_ref[...], precision=HIGHEST,
             preferred_element_type=jnp.float32,
         )
+        local_re = None
+        local_im = None
         for x in range(out_ref.shape[1]):
-            out_ref[t, x] = jnp.dot(
+            field = jnp.dot(
                 mix, summed[x * kinds : (x + 1) * kinds], precision=HIGHEST,
                 preferred_element_type=jnp.float32,
             )
-
-
-def contract(forward_prop, backward_prop, gamma_table):
+            out_ref[t, x] = field
+            cosine, sine = tables[x]
+            with_cos = jnp.dot(field, cosine, precision=HIGHEST, preferred_element_type=jnp.float32)
+            with_sin = jnp.dot(field, sine, precision=HIGHEST, preferred_element_type=jnp.float32)
+            part_re = with_cos[0:inserts] + with_sin[inserts:]
+            part_im = with_cos[inserts:] - with_sin[0:inserts]
+            local_re = part_re if local_re is None else local_re + part_re
+            local_im = part_im if local_im is None else local_im + part_im
+        local_ref[0, t] = local_re
+        local_ref[1, t] = local_im
+
+
+def contract(forward_prop, backward_prop, gamma_table, momenta, source_site):
     slices = forward_prop.shape[0]
     rows_x = forward_prop.shape[4]
     sites = forward_prop.shape[5]
     inserts = gamma_table.shape[0]
     forward = forward_prop.reshape(slices, 2, 12, 12 * rows_x, sites)
     backward = backward_prop.reshape(slices, 2, 12, 12 * rows_x, sites)
-    out = pl.pallas_call(
+    smem = pl.BlockSpec(memory_space=pltpu.SMEM)
+    vmem = pl.BlockSpec(memory_space=pltpu.VMEM)
+    out, local = pl.pallas_call(
         contract_kernel,
-        out_shape=jax.ShapeDtypeStruct((slices, rows_x, inserts * 2, sites), jnp.float32),
-        in_specs=[pl.BlockSpec(memory_space=pltpu.SMEM)]
-        + [pl.BlockSpec(memory_space=pltpu.VMEM)] * 2,
-        out_specs=pl.BlockSpec(memory_space=pltpu.VMEM),
+        out_shape=(
+            jax.ShapeDtypeStruct((slices, rows_x, inserts * 2, sites), jnp.float32),
+            jax.ShapeDtypeStruct((2, slices, inserts, momenta.shape[0]), jnp.float32),
+        ),
+        in_specs=[smem, smem, smem, vmem, vmem],
+        out_specs=(vmem, vmem),
         scratch_shapes=[pltpu.VMEM((16 * 2 * 12 * rows_x, sites), jnp.float32)],
-    )(gamma_table.reshape(-1), forward, backward)
-    return out.reshape(slices, rows_x, inserts, 2, sites).transpose(2, 0, 3, 1, 4)
+    )(gamma_table.reshape(-1), momenta.reshape(-1), source_site, forward, backward)
+    fields = out.reshape(slices, rows_x, 2, inserts, sites).transpose(3, 0, 2, 1, 4)
+    return fields, local
 
 
 def body(forward_prop, backward_prop, gamma_table, source_site, momenta):
@@ -456,11 +501,9 @@
     rows_x = forward_prop.shape[4]
     rows_y = backward_prop.shape[5] // LZ
     inserts = gamma_table.shape[0]
-    fields = contract(forward_prop, backward_prop, gamma_table)
+    fields, partial = contract(forward_prop, backward_prop, gamma_table, momenta, source_site)
     fields = fields.reshape(inserts * slices, 2, rows_x, rows_y, LZ)
     count = fields.shape[0]
-    local_re, local_im = project_sites(fields, source_site, momenta, rows_x, rows_y, L, LZ)
-    partial = jnp.stack([local_re, local_im], 0)
     groups_y = lax.axis_size("sy")
     groups_x = lax.axis_size("sx")
     tables = dft_matrices(LZ, source_site)
@@ -480,7 +523,7 @@
     table_x = tables[0].reshape(2, groups_x, rows_x, 2, -1)
     spectrum = jnp.einsum("ibsnxc,sixtk->ntbck", blocks, table_x, precision=HIGH)
     corr = spectrum.reshape(inserts, slices, 2, share_y, -1)
-    listed = gathered.reshape(2, inserts, slices, -1)
+    listed = gathered.reshape(2, slices, inserts, -1).transpose(0, 2, 1, 3)
     return (corr, listed)
 
 

time: 73 us -> 73.6 us (level)
  other arithmetic: 5.35 us -> 1.99 us
  local copies, waits for them, and re-layouts: 11.7 us -> 14.3 us
  Pallas kernels: 52.8 us -> 55.2 us
  matrix products: 1.77 us -> 0.99 us
    pallas_call x1, Pallas kernels: 4.21 us -> 6.45 us  [contract(): pl.pallas_call(contract_kernel, out_shape=(jax.ShapeDtypeStruct((slices,...]
    sub x3 -> x0, other arithmetic: 1.88 us -> none  [the longest x1 0.65 us: project_sites(): lax.axis_index('sx') * rows_x + jnp.arange(rows_x, dtype=jnp.int32)]
    reshape x1, local copies, waits for them, and re-layouts: 1.03 us -> 2.71 us  [contract(): forward = forward_prop.reshape(slices, 2, 12, 12 * rows_x, sites)]
    sin x1 -> x0, other arithmetic: 1.1 us -> none  [project_sites(): sine = jnp.sin(angles)]
    slice x3 -> x1, local copies, waits for them, and re-layouts: 2.17 us -> 1.32 us  [body(): source_site[1:2]]
    unnamed x11 -> x10, local copies, waits for them, and re-layouts: 0.71 us -> 1.54 us
    dot_general x4 -> x0, matrix products: 0.78 us -> none  [the longest x1 0.2 us: project_sites(): jnp.dot(field_im, sine.T, precision=HIGHEST)]
    reshape x1, local copies, waits for them, and re-layouts: 0.08 us -> 0.84 us  [body(): shares = partial.reshape(groups_y, 1, -1)]
where the time goes in v13:
time: 73.6 us; the launch traced here: 73.2 us
  Pallas kernels  55.2 us (75%)
  local copies, waits for them, and re-layouts  14.3 us (19%)
  other arithmetic  1.99 us (3%)
  matrix products  0.99 us (1%)
  between operations  0.76 us (1%)
    pallas_call x1, Pallas kernels, spread_ready(): pl.pallas_call(spread_kernel, out_shape=(jax.ShapeDtypeStruct(shaped.shap...  31.3 us
    pallas_call x1, Pallas kernels, turn(): pl.pallas_call(turn_kernel, out_shape=jax.ShapeDtypeStruct((parts_x, band...  17.4 us
    pallas_call x1, Pallas kernels, contract(): pl.pallas_call(contract_kernel, out_shape=(jax.ShapeDtypeStruct((slices,...  6.45 us
    reshape x1, local copies, waits for them, and re-layouts, contract(): forward = forward_prop.reshape(slices, 2, 12, 12 * rows_x, sites)  2.71 us
    unnamed x10, local copies, waits for them, and re-layouts  1.54 us

profile of v13, /device:TPU:1, one launch (start us, length us, event | category | flops | bytes accessed | tf_op | source)
XLA Modules:
  0.0 73.2 jit_solution(17693351612655627905)
XLA Ops:
  0.6 1.3 %slice.13.anchor_ref = s32[1]{0:T(128)} slice(s32[3]{0:T(128)} %site_ref.1), slice={[1:2]} | slice | bytes 8 | tf_op jit(solution)/shard_map/slice | solution.py:518
  1.9 0.8 %copy.13 = s32[16,4,2]{2,1,0:T(4,128)S(1)} copy(s32[16,4,2]{0,2,1:T(2,128)} %param.7) | data formatting | bytes 1024 | tf_op args[2]
  2.7 0.0 copy-start.3
  2.7 0.7 reshape.123.gamma_ref
  3.4 0.0 copy-done.3
  3.4 0.1 copy.14
  3.5 0.6 reshape.124.moment_ref
  4.2 0.0 copy-start
  4.2 2.7 %reshape.125.forward_ref = bf16[2,2,12,24,256]{4,3,2,1,0:T(8,128)(2,1)} reshape(bf16[2,2,12,12,2,256]{5,4,3,2,1,0:T(2,128)(2,1)} %param.5) | data formatting | bytes 1179648 | tf_op jit(solution)/shard_map/reshape | solution.py:481
  6.9 0.0 copy-done
  6.9 1.1 %reshape.126.backward_ref = bf16[2,2,12,24,256]{4,3,2,1,0:T(8,128)(2,1)} reshape(bf16[2,2,12,12,2,256]{5,4,3,2,1,0:T(2,128)(2,1)S(1)} %copy-done) | data formatting | bytes 1179648 | tf_op jit(solution)/shard_map/reshape | solution.py:482
  7.9 6.4 %shard_map.68 = (f32[2,2,32,256]{3,2,1,0:T(8,128)}, f32[2,2,16,32]{3,2,1,0:T(8,128)}) custom-call(s32[128]{0:T(128)} %reshape.123.gamma_ref, s32[96]{0:T(128)} %reshape.124.moment_ref, s32[3]{0:T(128)} %site_ref.1, bf16[2,2,12,24,256]{4,3,2,1,0:T(8,128)(2,1)} %reshape.125.forward_ref, bf16[2,2,12,24,256]{4,3,2,1,0:T(8,128)(2,1)} %reshape.126.backward_ref), custom_call_target="tpu_custom_call" | custom-call | tf_op jit(solution)/shard_map/pallas_call | solution.py:485
  14.4 0.8 %reshape.130 = f32[16,1,128]{2,1,0:T(1,128)S(1)} reshape(f32[2,2,16,32]{3,2,1,0:T(8,128)} %get-tuple-element.7) | data formatting | bytes 16384 | tf_op jit(solution)/shard_map/reshape | solution.py:515
  15.2 1.0 %copy.48 = f32[2,2,2,16,256]{4,1,2,0,3:T(2,128)S(1)} copy(f32[2,2,2,16,256]{4,3,2,1,0:T(8,128)} %bitcast.48) | data formatting | bytes 262144 | tf_op jit(solution)/shard_map/reshape | solution.py:495
  16.2 0.2 reshape.128
  16.4 0.0 copy-start.2
  16.5 0.6 copy-done.2
  17.1 0.1 add_select_fusion.1
  17.2 0.5 fusion.13
  17.7 0.1 copy.12
  17.8 0.5 convolution_bitcast_fusion
  18.3 0.5 copy.18
  18.8 0.3 copy.19
  19.1 0.7 select_maximum_fusion.sent_ref
  19.8 17.4 %shard_map.69.blocks_ref = f32[32,9,128]{2,1,0:T(8,128)} custom-call(s32[1]{0:T(128)} %slice.13.anchor_ref, f32[16,9,256]{2,1,0:T(8,128)} %select_maximum_fusion.sent_ref), custom_call_target="tpu_custom_call" | custom-call | tf_op jit(solution)/shard_map/pallas_call | solution.py:184
  37.3 31.3 %shard_map.70 = (f32[32,9,128]{2,1,0:T(8,128)}, f32[16,1,128]{2,1,0:T(1,128)}) custom-call(f32[32,9,128]{2,1,0:T(8,128)} %shard_map.69.blocks_ref), custom_call_target="tpu_custom_call" | custom-call | tf_op jit(solution)/shard_map/pallas_call | solution.py:289
  68.6 0.9 %slice.15 = f32[32,8,128]{2,1,0:T(8,128)S(1)} slice(f32[32,9,128]{2,1,0:T(8,128)} %get-tuple-element.8), slice={[0:32], [0:8], [0:128]} | slice | bytes 262144 | tf_op jit(solution)/shard_map/slice | solution.py:306
  69.5 0.2 copy.20
  69.7 0.5 convolution_bitcast_fusion.1
  70.2 0.2 copy.23
  70.4 0.0 copy-start.1
  70.4 0.9 %reshape.133 = f32[16,2,2,2,256]{4,3,2,1,0:T(2,128)} reshape(f32[32,2,2,4,64]{4,3,2,1,0:T(4,128)S(1)} %copy.23) | data formatting | bytes 262144 | tf_op jit(solution)/shard_map/reshape | solution.py:525
  71.3 0.5 broadcast.169
  71.8 0.0 copy-done.1
  71.8 0.7 reduce.3
  72.5 0.1 reshape_squeeze.11
  72.5 0.6 copy.49
  (2 shorter events, 0.1 us)
Async XLA Ops:
  2.7 0.7 copy-start.3
  4.2 2.7 %copy-start = (bf16[2,2,12,12,2,256]{5,4,3,2,1,0:T(2,128)(2,1)S(1)}, bf16[2,2,12,12,2,256]{5,4,3,2,1,0:T(2,128)(2,1)}, u32[]{:S(2)}) copy-start(bf16[2,2,12,12,2,256]{5,4,3,2,1,0:T(2,128)(2,1)} %param.6) | copy-start | bytes 1769476
  16.4 0.7 copy-start.2
  70.4 1.4 %copy-start.1 = (f32[16,1,128]{2,1,0:T(1,128)S(1)}, f32[16,1,128]{2,1,0:T(1,128)}, u32[]{:S(2)}) copy-start(f32[16,1,128]{2,1,0:T(1,128)} %get-tuple-element.9) | copy-start | bytes 24580

commit v14 on v12

--- a/solution.py
+++ b/solution.py
@@ -154,10 +154,6 @@
 
     @pl.loop(1, parts)
     def _(step):
-        copy_y(step, True).wait_send()
-
-    @pl.loop(1, parts)
-    def _(step):
         copy_y(step, False).wait_recv()
 
     lanes = ready_ref.shape[2]
@@ -176,6 +172,10 @@
             ready_ref[peer, half * rows : (half + 1) * rows, :] = turned[peer * rows : (peer + 1) * rows]
     for peer in range(ready_ref.shape[0]):
         ready_ref[peer, band : band + 1, :] = share
+
+    @pl.loop(1, parts)
+    def _(step):
+        copy_y(step, True).wait_send()
 
 
 def turn(sent, anchor, parts_x, band):
@@ -256,10 +256,6 @@
 
     @pl.loop(1, parts_x)
     def _(step):
-        copy_x(step, True).wait_send()
-
-    @pl.loop(1, parts_x)
-    def _(step):
         copy_x(step, False).wait_recv()
 
     total = out_ref[0, depth : depth + 1, :]
@@ -272,6 +268,10 @@
         copy_y(step, True).start()
 
     gathered_ref[me_y] = total
+
+    @pl.loop(1, parts_x)
+    def _(step):
+        copy_x(step, True).wait_send()
 
     @pl.loop(1, parts_y)
     def _(step):

time: 73 us -> 73 us (level)
  no operation moved by 1% of the time
where the time goes in v14:
time: 73 us; the launch traced here: 72.6 us
  Pallas kernels  52.9 us (72%)
  local copies, waits for them, and re-layouts  11.7 us (16%)
  other arithmetic  5.35 us (7%)
  matrix products  1.77 us (2%)
  between operations  0.88 us (1%)
    pallas_call x1, Pallas kernels, spread_ready(): pl.pallas_call(spread_kernel, out_shape=(jax.ShapeDtypeStruct(shaped.shap...  31.3 us
    pallas_call x1, Pallas kernels, turn(): pl.pallas_call(turn_kernel, out_shape=jax.ShapeDtypeStruct((parts_x, band...  17.4 us
    pallas_call x1, Pallas kernels, contract(): pl.pallas_call(contract_kernel, out_shape=jax.ShapeDtypeStruct((slices, r...  4.21 us

profile of v14, /device:TPU:1, one launch (start us, length us, event | category | flops | bytes accessed | tf_op | source)
XLA Modules:
  0.0 72.6 jit_solution(4569757024260403044)
XLA Ops:
  0.6 0.0 copy-start
  0.6 1.4 %fusion.26 = (s32[1]{0:T(128)}, s32[1]{0:T(128)}, s32[1]{0:T(128)}) fusion(s32[3]{0:T(128)} %param.8), kind=kLoop, calls=%fused_computation.71 | loop fusion | bytes 24 | tf_op jit(solution)/shard_map/slice | solution.py:353
  2.0 0.6 add_subtract_fusion
  2.6 0.8 %slice_bitcast_fusion.2 = (s32[32]{0:T(128)S(1)}, s32[32]{0:T(128)S(1)}, s32[32]{0:T(128)S(1)}) fusion(s32[32,3]{0,1:T(4,128)} %param.9), kind=kLoop, calls=%fused_computation.69 | loop fusion | bytes 768 | tf_op jit(solution)/shard_map/slice | solution.py:356
  3.4 0.1 add_select_fusion.2
  3.5 0.7 add_subtract_fusion.1
  4.1 0.1 add_select_fusion.3
  4.2 0.1 fusion.18
  4.3 0.7 iota_subtract_fusion
  5.0 0.1 fusion.20
  5.1 1.1 %add_sine_fusion = (f32[32,2,4,64]{3,2,1,0:T(4,128)S(1)}, f32[32,2,4,64]{3,2,1,0:T(4,128)S(1)}) fusion(f32[32,64]{1,0:T(8,128)S(1)} %fusion.20, f32[32,2,4]{2,1,0:T(2,128)S(1)} %fusion.18), kind=kLoop, calls=%fused_computation.13 | loop fusion | flops 16384 | bytes 140288 | tf_op jit(solution)/shard_map/sin | solution.py:366
  6.2 0.1 cos.28
  6.3 1.0 %reshape.294.forward_ref = bf16[2,2,12,24,256]{4,3,2,1,0:T(8,128)(2,1)} reshape(bf16[2,2,12,12,2,256]{5,4,3,2,1,0:T(2,128)(2,1)S(1)} %copy-done) | data formatting | bytes 1179648 | tf_op jit(solution)/shard_map/reshape | solution.py:441
  7.4 0.0 copy-done.1
  7.4 1.0 %reshape.295.backward_ref = bf16[2,2,12,24,256]{4,3,2,1,0:T(8,128)(2,1)} reshape(bf16[2,2,12,12,2,256]{5,4,3,2,1,0:T(2,128)(2,1)S(1)} %copy-done.1) | data formatting | bytes 1179648 | tf_op jit(solution)/shard_map/reshape | solution.py:442
  8.4 0.1 copy.11
  8.5 0.7 reshape.293.gamma_ref
  9.2 4.2 %shard_map.68 = f32[2,2,32,256]{3,2,1,0:T(8,128)} custom-call(s32[128]{0:T(128)} %reshape.293.gamma_ref, bf16[2,2,12,24,256]{4,3,2,1,0:T(8,128)(2,1)} %reshape.294.forward_ref, bf16[2,2,12,24,256]{4,3,2,1,0:T(8,128)(2,1)} %reshape.295.backward_ref), custom_call_target="tpu_custom_call" | custom-call | tf_op jit(solution)/shard_map/pallas_call | solution.py:443
  13.4 1.0 %reshape.296 = f32[2,2,16,2,256]{4,3,2,1,0:T(2,128)S(1)} reshape(f32[2,2,32,256]{3,2,1,0:T(8,128)} %shard_map.68) | data formatting | bytes 262144 | tf_op jit(solution)/shard_map/reshape | solution.py:451
  14.4 0.1 copy.43
  14.5 0.2 reshape.297
  14.8 0.1 reshape_squeeze.17
  14.9 0.2 fusion.27
  15.1 0.1 sin.32
  15.2 0.1 reshape_squeeze.18
  15.3 0.2 fusion.1
  15.5 0.2 fusion.28
  15.7 0.2 fusion
  15.9 0.0 copy-start.2
  15.9 0.1 reshape.299
  16.0 0.6 copy-done.2
  16.6 0.1 add_select_fusion.4
  16.7 0.5 fusion.15
  17.2 0.1 copy.10
  17.3 0.5 convolution_bitcast_fusion
  17.8 0.5 copy.15
  18.3 0.3 copy.16
  18.6 0.7 %select_maximum_fusion.sent_ref = f32[16,9,256]{2,1,0:T(8,128)} fusion(f32[16,1,128]{2,1,0:T(1,128)S(1)} %reshape.299, f32[16,8,256]{2,1,0:T(8,128)S(1)} %copy.16), kind=kLoop, calls=%fused_computation.8 | loop fusion | flops 110592 | bytes 286720 | tf_op jit(solution)/shard_map/concatenate | solution.py:475
  19.3 17.4 %shard_map.69.blocks_ref = f32[32,9,128]{2,1,0:T(8,128)} custom-call(s32[1]{0:T(128)} %get-tuple-element.21.anchor_ref, f32[16,9,256]{2,1,0:T(8,128)} %select_maximum_fusion.sent_ref), custom_call_target="tpu_custom_call" | custom-call | tf_op jit(solution)/shard_map/pallas_call | solution.py:184
  36.7 31.3 %shard_map.70 = (f32[32,9,128]{2,1,0:T(8,128)}, f32[16,1,128]{2,1,0:T(1,128)}) custom-call(f32[32,9,128]{2,1,0:T(8,128)} %shard_map.69.blocks_ref), custom_call_target="tpu_custom_call" | custom-call | tf_op jit(solution)/shard_map/pallas_call | solution.py:289
  68.1 0.9 %slice.47 = f32[32,8,128]{2,1,0:T(8,128)S(1)} slice(f32[32,9,128]{2,1,0:T(8,128)} %get-tuple-element.4), slice={[0:32], [0:8], [0:128]} | slice | bytes 262144 | tf_op jit(solution)/shard_map/slice | solution.py:306
  69.0 0.2 copy.17
  69.2 0.5 convolution_bitcast_fusion.1
  69.7 0.2 copy.20
  69.9 0.9 %reshape.302 = f32[16,2,2,2,256]{4,3,2,1,0:T(2,128)} reshape(f32[32,2,2,4,64]{4,3,2,1,0:T(4,128)S(1)} %copy.20) | data formatting | bytes 262144 | tf_op jit(solution)/shard_map/reshape | solution.py:482
  70.8 0.5 broadcast.378
  71.3 0.7 reduce.3
  71.9 0.7 reshape_squeeze.19
  (10 shorter events, 0.1 us)
Async XLA Ops:
  0.6 5.7 %copy-start = (bf16[2,2,12,12,2,256]{5,4,3,2,1,0:T(2,128)(2,1)S(1)}, bf16[2,2,12,12,2,256]{5,4,3,2,1,0:T(2,128)(2,1)}, u32[]{:S(2)}) copy-start(bf16[2,2,12,12,2,256]{5,4,3,2,1,0:T(2,128)(2,1)} %param.5) | copy-start | bytes 1769476
  6.3 1.1 %copy-start.1 = (bf16[2,2,12,12,2,256]{5,4,3,2,1,0:T(2,128)(2,1)S(1)}, bf16[2,2,12,12,2,256]{5,4,3,2,1,0:T(2,128)(2,1)}, u32[]{:S(2)}) copy-start(bf16[2,2,12,12,2,256]{5,4,3,2,1,0:T(2,128)(2,1)} %param.6) | copy-start | bytes 1769476
  7.4 1.0 %copy-start.4 = (s32[16,4,2]{0,2,1:T(2,128)S(1)}, s32[16,4,2]{0,2,1:T(2,128)}, u32[]{:S(2)}) copy-start(s32[16,4,2]{0,2,1:T(2,128)} %param.7) | copy-start | bytes 1540
  15.9 0.7 copy-start.2
  69.9 1.4 %copy-start.3 = (f32[16,1,128]{2,1,0:T(1,128)S(1)}, f32[16,1,128]{2,1,0:T(1,128)}, u32[]{:S(2)}) copy-start(f32[16,1,128]{2,1,0:T(1,128)} %get-tuple-element.5) | copy-start | bytes 24580

commit v15 on v12

--- a/solution.py
+++ b/solution.py
@@ -169,7 +169,7 @@
         share = share + landed_ref[source, depth : depth + 1, 0:lanes]
     for half in range(halves):
         turned = jnp.dot(
-            table_ref[...], block[:, half * lanes : (half + 1) * lanes], precision=HIGHEST,
+            table_ref[...], block[:, half * lanes : (half + 1) * lanes], precision=HIGH,
             preferred_element_type=jnp.float32,
         )
         for peer in range(ready_ref.shape[0]):
@@ -423,12 +423,12 @@
         col = lax.broadcasted_iota(jnp.int32, (lines, width), 1)
         pick = jnp.logical_and(row % kinds == col // rows, row // kinds == col % out_ref.shape[1])
         summed = jnp.dot(
-            pick.astype(jnp.float32), pair_ref[...], precision=HIGHEST,
+            pick.astype(jnp.float32), pair_ref[...], precision=HIGH,
             preferred_element_type=jnp.float32,
         )
         for x in range(out_ref.shape[1]):
             out_ref[t, x] = jnp.dot(
-                mix, summed[x * kinds : (x + 1) * kinds], precision=HIGHEST,
+                mix, summed[x * kinds : (x + 1) * kinds], precision=HIGH,
                 preferred_element_type=jnp.float32,
             )
 

time: 73 us -> 72.2 us (0.989)
  Pallas kernels: 52.8 us -> 52 us
where the time goes in v15:
time: 72.2 us; the launch traced here: 71.8 us
  Pallas kernels  52 us (72%)
  local copies, waits for them, and re-layouts  11.7 us (16%)
  other arithmetic  5.35 us (7%)
  matrix products  1.77 us (2%)
  between operations  0.88 us (1%)
    pallas_call x1, Pallas kernels, spread_ready(): pl.pallas_call(spread_kernel, out_shape=(jax.ShapeDtypeStruct(shaped.shap...  31.3 us
    pallas_call x1, Pallas kernels, turn(): pl.pallas_call(turn_kernel, out_shape=jax.ShapeDtypeStruct((parts_x, band...  17.3 us
    pallas_call x1, Pallas kernels, contract(): pl.pallas_call(contract_kernel, out_shape=jax.ShapeDtypeStruct((slices, r...  3.5 us

profile of v15, /device:TPU:1, one launch (start us, length us, event | category | flops | bytes accessed | tf_op | source)
XLA Modules:
  0.0 71.8 jit_solution(16089951143469522772)
XLA Ops:
  0.6 1.4 %fusion.26 = (s32[1]{0:T(128)}, s32[1]{0:T(128)}, s32[1]{0:T(128)}) fusion(s32[3]{0:T(128)} %param.8), kind=kLoop, calls=%fused_computation.71 | loop fusion | bytes 24 | tf_op jit(solution)/shard_map/slice | solution.py:353
  2.0 0.6 add_subtract_fusion
  2.6 0.8 %slice_bitcast_fusion.2 = (s32[32]{0:T(128)S(1)}, s32[32]{0:T(128)S(1)}, s32[32]{0:T(128)S(1)}) fusion(s32[32,3]{0,1:T(4,128)} %param.9), kind=kLoop, calls=%fused_computation.69 | loop fusion | bytes 768 | tf_op jit(solution)/shard_map/slice | solution.py:356
  3.4 0.1 add_select_fusion.2
  3.5 0.7 add_subtract_fusion.1
  4.1 0.1 add_select_fusion.3
  4.2 0.1 fusion.18
  4.3 0.7 iota_subtract_fusion
  5.0 0.1 fusion.20
  5.1 1.1 %add_sine_fusion = (f32[32,2,4,64]{3,2,1,0:T(4,128)S(1)}, f32[32,2,4,64]{3,2,1,0:T(4,128)S(1)}) fusion(f32[32,64]{1,0:T(8,128)S(1)} %fusion.20, f32[32,2,4]{2,1,0:T(2,128)S(1)} %fusion.18), kind=kLoop, calls=%fused_computation.13 | loop fusion | flops 16384 | bytes 140288 | tf_op jit(solution)/shard_map/sin | solution.py:366
  6.2 0.1 cos.28
  6.3 1.0 %reshape.294.forward_ref = bf16[2,2,12,24,256]{4,3,2,1,0:T(8,128)(2,1)} reshape(bf16[2,2,12,12,2,256]{5,4,3,2,1,0:T(2,128)(2,1)S(1)} %copy-done) | data formatting | bytes 1179648 | tf_op jit(solution)/shard_map/reshape | solution.py:441
  7.4 0.0 copy-done.1
  7.4 1.0 %reshape.295.backward_ref = bf16[2,2,12,24,256]{4,3,2,1,0:T(8,128)(2,1)} reshape(bf16[2,2,12,12,2,256]{5,4,3,2,1,0:T(2,128)(2,1)S(1)} %copy-done.1) | data formatting | bytes 1179648 | tf_op jit(solution)/shard_map/reshape | solution.py:442
  8.4 0.1 copy.11
  8.5 0.7 reshape.293.gamma_ref
  9.2 3.5 %shard_map.68 = f32[2,2,32,256]{3,2,1,0:T(8,128)} custom-call(s32[128]{0:T(128)} %reshape.293.gamma_ref, bf16[2,2,12,24,256]{4,3,2,1,0:T(8,128)(2,1)} %reshape.294.forward_ref, bf16[2,2,12,24,256]{4,3,2,1,0:T(8,128)(2,1)} %reshape.295.backward_ref), custom_call_target="tpu_custom_call" | custom-call | tf_op jit(solution)/shard_map/pallas_call | solution.py:443
  12.7 1.0 %reshape.296 = f32[2,2,16,2,256]{4,3,2,1,0:T(2,128)S(1)} reshape(f32[2,2,32,256]{3,2,1,0:T(8,128)} %shard_map.68) | data formatting | bytes 262144 | tf_op jit(solution)/shard_map/reshape | solution.py:451
  13.7 0.1 copy.43
  13.8 0.2 reshape.297
  14.0 0.1 reshape_squeeze.17
  14.2 0.2 fusion.27
  14.4 0.1 sin.32
  14.5 0.1 reshape_squeeze.18
  14.6 0.2 fusion.1
  14.8 0.2 fusion.28
  15.0 0.2 fusion
  15.2 0.0 copy-start.2
  15.2 0.1 reshape.299
  15.3 0.6 copy-done.2
  15.9 0.1 add_select_fusion.4
  16.0 0.5 fusion.15
  16.5 0.1 copy.10
  16.6 0.5 convolution_bitcast_fusion
  17.1 0.5 copy.15
  17.6 0.3 copy.16
  17.9 0.7 %select_maximum_fusion.sent_ref = f32[16,9,256]{2,1,0:T(8,128)} fusion(f32[16,1,128]{2,1,0:T(1,128)S(1)} %reshape.299, f32[16,8,256]{2,1,0:T(8,128)S(1)} %copy.16), kind=kLoop, calls=%fused_computation.8 | loop fusion | flops 110592 | bytes 286720 | tf_op jit(solution)/shard_map/concatenate | solution.py:475
  18.6 17.3 %shard_map.69.blocks_ref = f32[32,9,128]{2,1,0:T(8,128)} custom-call(s32[1]{0:T(128)} %get-tuple-element.21.anchor_ref, f32[16,9,256]{2,1,0:T(8,128)} %select_maximum_fusion.sent_ref), custom_call_target="tpu_custom_call" | custom-call | tf_op jit(solution)/shard_map/pallas_call | solution.py:184
  35.9 31.3 %shard_map.70 = (f32[32,9,128]{2,1,0:T(8,128)}, f32[16,1,128]{2,1,0:T(1,128)}) custom-call(f32[32,9,128]{2,1,0:T(8,128)} %shard_map.69.blocks_ref), custom_call_target="tpu_custom_call" | custom-call | tf_op jit(solution)/shard_map/pallas_call | solution.py:289
  67.2 0.9 %slice.47 = f32[32,8,128]{2,1,0:T(8,128)S(1)} slice(f32[32,9,128]{2,1,0:T(8,128)} %get-tuple-element.4), slice={[0:32], [0:8], [0:128]} | slice | bytes 262144 | tf_op jit(solution)/shard_map/slice | solution.py:306
  68.1 0.2 copy.17
  68.3 0.5 convolution_bitcast_fusion.1
  68.8 0.2 copy.20
  69.0 0.9 %reshape.302 = f32[16,2,2,2,256]{4,3,2,1,0:T(2,128)} reshape(f32[32,2,2,4,64]{4,3,2,1,0:T(4,128)S(1)} %copy.20) | data formatting | bytes 262144 | tf_op jit(solution)/shard_map/reshape | solution.py:482
  69.9 0.5 broadcast.378
  70.4 0.0 copy-done.3
  70.4 0.7 reduce.3
  71.1 0.7 reshape_squeeze.19
  (10 shorter events, 0.1 us)
Async XLA Ops:
  0.6 5.7 %copy-start = (bf16[2,2,12,12,2,256]{5,4,3,2,1,0:T(2,128)(2,1)S(1)}, bf16[2,2,12,12,2,256]{5,4,3,2,1,0:T(2,128)(2,1)}, u32[]{:S(2)}) copy-start(bf16[2,2,12,12,2,256]{5,4,3,2,1,0:T(2,128)(2,1)} %param.5) | copy-start | bytes 1769476
  6.3 1.1 %copy-start.1 = (bf16[2,2,12,12,2,256]{5,4,3,2,1,0:T(2,128)(2,1)S(1)}, bf16[2,2,12,12,2,256]{5,4,3,2,1,0:T(2,128)(2,1)}, u32[]{:S(2)}) copy-start(bf16[2,2,12,12,2,256]{5,4,3,2,1,0:T(2,128)(2,1)} %param.6) | copy-start | bytes 1769476
  7.4 1.0 %copy-start.4 = (s32[16,4,2]{0,2,1:T(2,128)S(1)}, s32[16,4,2]{0,2,1:T(2,128)}, u32[]{:S(2)}) copy-start(s32[16,4,2]{0,2,1:T(2,128)} %param.7) | copy-start | bytes 1540
  15.2 0.7 copy-start.2
  69.0 1.4 %copy-start.3 = (f32[16,1,128]{2,1,0:T(1,128)S(1)}, f32[16,1,128]{2,1,0:T(1,128)}, u32[]{:S(2)}) copy-start(f32[16,1,128]{2,1,0:T(1,128)} %get-tuple-element.5) | copy-start | bytes 24580

commit v16 on v15

--- a/solution.py
+++ b/solution.py
@@ -240,7 +240,7 @@
     def copy_y(step, outgoing):
         peer = lax.rem(me_y + (step if outgoing else parts_y - step), parts_y)
         return pltpu.make_async_remote_copy(
-            src_ref=total_ref,
+            src_ref=total_ref.at[0],
             dst_ref=gathered_ref.at[me_y if outgoing else peer],
             send_sem=c_send.at[step],
             recv_sem=c_recv.at[step],
@@ -271,7 +271,7 @@
     def _(step):
         copy_y(step, True).start()
 
-    gathered_ref[me_y] = total
+    gathered_ref[pl.ds(me_y, 1), :] = total
 
     @pl.loop(1, parts_y)
     def _(step):
@@ -290,7 +290,7 @@
         spread_kernel,
         out_shape=(
             jax.ShapeDtypeStruct(shaped.shape, shaped.dtype),
-            jax.ShapeDtypeStruct((parts_y, 1, shaped.shape[2]), shaped.dtype),
+            jax.ShapeDtypeStruct((parts_y, shaped.shape[2]), shaped.dtype),
         ),
         in_specs=[vmem],
         out_specs=(vmem, vmem),
@@ -303,7 +303,7 @@
         ],
         compiler_params=pltpu.CompilerParams(collective_id=1, has_side_effects=True),
     )(shaped)
-    return got[:, :-1], gathered[:, 0]
+    return got[:, :-1], gathered
 
 
 def spread(blocks, share, parts_y):

time: 72.2 us -> 71.6 us (level)
    unnamed x11 -> x13, local copies, waits for them, and re-layouts: 0.71 us -> 2.94 us
    slice x1, local copies, waits for them, and re-layouts: 0.8 us -> 0.01 us  [project_sites(): part_x = jnp.mod(momenta[:, 0:1] * coord_x[None, :], length)]
    slice x1, local copies, waits for them, and re-layouts: 1.36 us -> 0.59 us  [project_sites(): source_site[0]]
where the time goes in v16:
time: 71.6 us; the launch traced here: 71.2 us
  Pallas kernels  52 us (73%)
  local copies, waits for them, and re-layouts  11.9 us (17%)
  other arithmetic  4.63 us (6%)
  matrix products  1.76 us (2%)
  between operations  0.88 us (1%)
    pallas_call x1, Pallas kernels, spread_ready(): pl.pallas_call(spread_kernel, out_shape=(jax.ShapeDtypeStruct(shaped.shap...  31.3 us
    pallas_call x1, Pallas kernels, turn(): pl.pallas_call(turn_kernel, out_shape=jax.ShapeDtypeStruct((parts_x, band...  17.2 us
    pallas_call x1, Pallas kernels, contract(): pl.pallas_call(contract_kernel, out_shape=jax.ShapeDtypeStruct((slices, r...  3.5 us
    unnamed x13, local copies, waits for them, and re-layouts  2.94 us

profile of v16, /device:TPU:1, one launch (start us, length us, event | category | flops | bytes accessed | tf_op | source)
XLA Modules:
  0.0 71.2 jit_solution(11103708845624816061)
XLA Ops:
  0.6 0.7 copy-done.5
  1.3 0.7 copy-done.3
  2.0 0.6 fusion.26
  2.6 0.6 add_subtract_fusion.1
  3.2 0.5 add_subtract_fusion
  3.8 0.7 iota_subtract_fusion
  4.4 0.1 add_select_fusion.4
  4.5 0.1 fusion.20
  4.6 0.1 add_select_fusion.2
  4.7 0.1 add_select_fusion.3
  4.8 0.0 copy-start.4
  4.8 0.1 fusion.18
  4.9 0.5 copy-done.4
  5.5 0.1 copy.11
  5.6 0.7 reshape.296.gamma_ref
  6.2 1.1 %add_sine_fusion = (f32[32,2,4,64]{3,2,1,0:T(4,128)S(1)}, f32[32,2,4,64]{3,2,1,0:T(4,128)S(1)}) fusion(f32[32,64]{1,0:T(8,128)S(1)} %fusion.20, f32[32,2,4]{2,1,0:T(2,128)S(1)} %fusion.18), kind=kLoop, calls=%fused_computation.13 | loop fusion | flops 16384 | bytes 140288 | tf_op jit(solution)/shard_map/sin | solution.py:366
  7.3 0.1 sin.32
  7.4 0.1 cos.28
  7.5 0.5 fusion.15
  8.1 0.0 copy-start
  8.1 0.1 copy.10
  8.2 0.9 %copy-done = bf16[2,2,12,12,2,256]{5,4,3,2,1,0:T(2,128)(2,1)S(1)} copy-done((bf16[2,2,12,12,2,256]{5,4,3,2,1,0:T(2,128)(2,1)S(1)}, bf16[2,2,12,12,2,256]{5,4,3,2,1,0:T(2,128)(2,1)}, u32[]{:S(2)}) %copy-start) | copy-done | bytes 589848
  9.1 1.0 %reshape.297.forward_ref = bf16[2,2,12,24,256]{4,3,2,1,0:T(8,128)(2,1)} reshape(bf16[2,2,12,12,2,256]{5,4,3,2,1,0:T(2,128)(2,1)S(1)} %copy-done) | data formatting | bytes 1179648 | tf_op jit(solution)/shard_map/reshape | solution.py:441
  10.2 0.0 copy-done.1
  10.2 1.0 %reshape.298.backward_ref = bf16[2,2,12,24,256]{4,3,2,1,0:T(8,128)(2,1)} reshape(bf16[2,2,12,12,2,256]{5,4,3,2,1,0:T(2,128)(2,1)S(1)} %copy-done.1) | data formatting | bytes 1179648 | tf_op jit(solution)/shard_map/reshape | solution.py:442
  11.2 3.5 %shard_map.68 = f32[2,2,32,256]{3,2,1,0:T(8,128)} custom-call(s32[128]{0:T(128)} %reshape.296.gamma_ref, bf16[2,2,12,24,256]{4,3,2,1,0:T(8,128)(2,1)} %reshape.297.forward_ref, bf16[2,2,12,24,256]{4,3,2,1,0:T(8,128)(2,1)} %reshape.298.backward_ref), custom_call_target="tpu_custom_call" | custom-call | tf_op jit(solution)/shard_map/pallas_call | solution.py:443
  14.7 1.0 %reshape.299 = f32[2,2,16,2,256]{4,3,2,1,0:T(2,128)S(1)} reshape(f32[2,2,32,256]{3,2,1,0:T(8,128)} %shard_map.68) | data formatting | bytes 262144 | tf_op jit(solution)/shard_map/reshape | solution.py:451
  15.7 0.1 copy.43
  15.8 0.2 reshape.300
  16.1 0.1 reshape_squeeze.14
  16.2 0.2 fusion.27
  16.4 0.1 reshape_squeeze.15
  16.5 0.2 fusion.28
  16.7 0.2 fusion.1
  16.9 0.2 fusion
  17.1 0.1 reshape.302
  17.2 0.5 convolution_bitcast_fusion
  17.7 0.5 copy.15
  18.2 0.3 copy.16
  18.5 0.7 %select_maximum_fusion.sent_ref = f32[16,9,256]{2,1,0:T(8,128)} fusion(f32[16,1,128]{2,1,0:T(1,128)S(1)} %reshape.302, f32[16,8,256]{2,1,0:T(8,128)S(1)} %copy.16), kind=kLoop, calls=%fused_computation.8 | loop fusion | flops 110592 | bytes 286720 | tf_op jit(solution)/shard_map/concatenate | solution.py:475
  19.2 17.2 %shard_map.69.blocks_ref = f32[32,9,128]{2,1,0:T(8,128)} custom-call(s32[1]{0:T(128)} %get-tuple-element.21.anchor_ref, f32[16,9,256]{2,1,0:T(8,128)} %select_maximum_fusion.sent_ref), custom_call_target="tpu_custom_call" | custom-call | tf_op jit(solution)/shard_map/pallas_call | solution.py:184
  36.4 31.3 %shard_map.70 = (f32[32,9,128]{2,1,0:T(8,128)}, f32[16,128]{1,0:T(8,128)}) custom-call(f32[32,9,128]{2,1,0:T(8,128)} %shard_map.69.blocks_ref), custom_call_target="tpu_custom_call" | custom-call | tf_op jit(solution)/shard_map/pallas_call | solution.py:289
  67.8 0.9 %slice.47 = f32[32,8,128]{2,1,0:T(8,128)S(1)} slice(f32[32,9,128]{2,1,0:T(8,128)} %get-tuple-element.4), slice={[0:32], [0:8], [0:128]} | slice | bytes 262144 | tf_op jit(solution)/shard_map/slice | solution.py:306
  68.7 0.7 reshape.306
  69.4 0.2 copy.17
  69.6 0.5 convolution_bitcast_fusion.1
  70.1 0.2 copy.20
  70.3 0.9 %reshape.305 = f32[16,2,2,2,256]{4,3,2,1,0:T(2,128)} reshape(f32[32,2,2,4,64]{4,3,2,1,0:T(4,128)S(1)} %copy.20) | data formatting | bytes 262144 | tf_op jit(solution)/shard_map/reshape | solution.py:482
  (10 shorter events, 0.1 us)
Async XLA Ops:
  0.6 0.7 copy-start.5
  1.3 0.7 copy-start.3
  4.8 0.7 copy-start.4
  8.1 1.1 %copy-start = (bf16[2,2,12,12,2,256]{5,4,3,2,1,0:T(2,128)(2,1)S(1)}, bf16[2,2,12,12,2,256]{5,4,3,2,1,0:T(2,128)(2,1)}, u32[]{:S(2)}) copy-start(bf16[2,2,12,12,2,256]{5,4,3,2,1,0:T(2,128)(2,1)} %param.5) | copy-start | bytes 1769476
  9.1 1.1 %copy-start.1 = (bf16[2,2,12,12,2,256]{5,4,3,2,1,0:T(2,128)(2,1)S(1)}, bf16[2,2,12,12,2,256]{5,4,3,2,1,0:T(2,128)(2,1)}, u32[]{:S(2)}) copy-start(bf16[2,2,12,12,2,256]{5,4,3,2,1,0:T(2,128)(2,1)} %param.6) | copy-start | bytes 1769476
  67.7 0.9 %copy-start.2 = (f32[16,128]{1,0:T(8,128)S(1)}, f32[16,128]{1,0:T(8,128)}, u32[]{:S(2)}) copy-start(f32[16,128]{1,0:T(8,128)} %get-tuple-element.5) | copy-start | bytes 24580

commit v17 on v16

--- a/solution.py
+++ b/solution.py
@@ -361,18 +361,19 @@
         2.0 * math.pi / length * plane[:, :, :, None]
         + 2.0 * math.pi / depth * part_z.astype(jnp.float32)[:, None, None, :]
     )
-    angles = angles.reshape(momenta.shape[0], -1)
     cosine = jnp.cos(angles)
     sine = jnp.sin(angles)
-    field_re = fields[:, 0].reshape(fields.shape[0], -1)
-    field_im = fields[:, 1].reshape(fields.shape[0], -1)
-    local_re = jnp.dot(field_re, cosine.T, precision=HIGHEST) + jnp.dot(
-        field_im, sine.T, precision=HIGHEST
-    )
-    local_im = jnp.dot(field_im, cosine.T, precision=HIGHEST) - jnp.dot(
-        field_re, sine.T, precision=HIGHEST
-    )
-    return (local_re, local_im)
+    field_re = fields[:, :, :, 0]
+    field_im = fields[:, :, :, 1]
+    pattern = "txgyz,mxyz->gtm"
+    local_re = jnp.einsum(pattern, field_re, cosine, precision=HIGHEST) + jnp.einsum(
+        pattern, field_im, sine, precision=HIGHEST
+    )
+    local_im = jnp.einsum(pattern, field_im, cosine, precision=HIGHEST) - jnp.einsum(
+        pattern, field_re, sine, precision=HIGHEST
+    )
+    count = local_re.shape[0] * local_re.shape[1]
+    return (local_re.reshape(count, -1), local_im.reshape(count, -1))
 
 
 def gamma_mix(table_ref, inserts):
@@ -448,7 +449,7 @@
         out_specs=pl.BlockSpec(memory_space=pltpu.VMEM),
         scratch_shapes=[pltpu.VMEM((16 * 2 * 12 * rows_x, sites), jnp.float32)],
     )(gamma_table.reshape(-1), forward, backward)
-    return out.reshape(slices, rows_x, inserts, 2, sites).transpose(2, 0, 3, 1, 4)
+    return out.reshape(slices, rows_x, inserts, 2, sites)
 
 
 def body(forward_prop, backward_prop, gamma_table, source_site, momenta):
@@ -457,8 +458,8 @@
     rows_y = backward_prop.shape[5] // LZ
     inserts = gamma_table.shape[0]
     fields = contract(forward_prop, backward_prop, gamma_table)
-    fields = fields.reshape(inserts * slices, 2, rows_x, rows_y, LZ)
-    count = fields.shape[0]
+    fields = fields.reshape(slices, rows_x, inserts, 2, rows_y, LZ)
+    count = inserts * slices
     local_re, local_im = project_sites(fields, source_site, momenta, rows_x, rows_y, L, LZ)
     partial = jnp.stack([local_re, local_im], 0)
     groups_y = lax.axis_size("sy")
@@ -466,7 +467,7 @@
     tables = dft_matrices(LZ, source_site)
     share_z = LZ // groups_y
     table_z = tables[2].reshape(2, LZ, 2, groups_y, share_z)
-    blocks = jnp.einsum("nrxyz,rzsjc->jsynxc", fields, table_z, precision=HIGH)
+    blocks = jnp.einsum("txgryz,rzsjc->jsygtxc", fields, table_z, precision=HIGH)
     blocks = blocks.reshape(groups_y, 2 * rows_y, -1)
     width = blocks.shape[2]
     shares = partial.reshape(groups_y, 1, -1)

time: 71.6 us -> 72.5 us (1.013)
  matrix products: 1.76 us -> 4.05 us
  other arithmetic: 4.63 us -> 3.53 us
    dot_general x5, matrix products: 1.27 us -> 3.56 us  [the longest x1 0.73 us: project_sites(): jnp.einsum(pattern, field_im, sine, precision=HIGHEST)]
    reshape x3 -> x0, local copies, waits for them, and re-layouts: 1.3 us -> none  [the longest x2 1.08 us: contract(): out.reshape(slices, rows_x, inserts, 2, sites).transpose(2, 0, 3, 1, 4)]
    sin x1 -> x0, other arithmetic: 1.08 us -> none  [project_sites(): sine = jnp.sin(angles)]
    another operation x2 -> x1, local copies, waits for them, and re-layouts: 0.24 us -> 1.05 us  [body(): fields = fields.reshape(slices, rows_x, inserts, 2, rows_y, LZ)]
where the time goes in v17:
time: 72.5 us; the launch traced here: 72 us
  Pallas kernels  52.1 us (72%)
  local copies, waits for them, and re-layouts  11.5 us (16%)
  matrix products  4.05 us (6%)
  other arithmetic  3.53 us (5%)
  between operations  0.86 us (1%)
    pallas_call x1, Pallas kernels, spread_ready(): pl.pallas_call(spread_kernel, out_shape=(jax.ShapeDtypeStruct(shaped.shap...  31.3 us
    pallas_call x1, Pallas kernels, turn(): pl.pallas_call(turn_kernel, out_shape=jax.ShapeDtypeStruct((parts_x, band...  17.3 us
    pallas_call x1, Pallas kernels, contract(): pl.pallas_call(contract_kernel, out_shape=jax.ShapeDtypeStruct((slices, r...  3.5 us
    unnamed x13, local copies, waits for them, and re-layouts  2.99 us

profile of v17, /device:TPU:1, one launch (start us, length us, event | category | flops | bytes accessed | tf_op | source)
XLA Modules:
  0.0 72.0 jit_solution(1778807281551387674)
XLA Ops:
  0.6 0.0 copy-start.5
  0.6 0.7 copy-done.5
  1.3 0.0 copy-start.3
  1.3 0.7 copy-done.3
  2.0 0.6 fusion.50
  2.6 0.6 add_subtract_fusion.1
  3.3 0.1 and_select_fusion
  3.4 0.6 add_subtract_fusion
  4.0 0.7 iota_subtract_fusion
  4.7 0.1 add_select_fusion.4
  4.8 0.1 add_select_fusion.5
  4.8 0.0 copy-start.4
  4.8 0.1 fusion.41
  4.9 0.6 copy-done.4
  5.5 0.1 copy.14
  5.6 0.7 reshape.259.gamma_ref
  6.3 0.5 fusion.39
  6.8 0.0 copy-start
  6.8 0.1 copy.13
  6.9 0.9 %copy-done = bf16[2,2,12,12,2,256]{5,4,3,2,1,0:T(2,128)(2,1)S(1)} copy-done((bf16[2,2,12,12,2,256]{5,4,3,2,1,0:T(2,128)(2,1)S(1)}, bf16[2,2,12,12,2,256]{5,4,3,2,1,0:T(2,128)(2,1)}, u32[]{:S(2)}) %copy-start) | copy-done | bytes 589848
  7.9 0.0 copy-start.1
  7.9 1.0 %reshape.260.forward_ref = bf16[2,2,12,24,256]{4,3,2,1,0:T(8,128)(2,1)} reshape(bf16[2,2,12,12,2,256]{5,4,3,2,1,0:T(2,128)(2,1)S(1)} %copy-done) | data formatting | bytes 1179648 | tf_op jit(solution)/shard_map/reshape | solution.py:442
  8.9 0.0 copy-done.1
  8.9 1.0 %reshape.261.backward_ref = bf16[2,2,12,24,256]{4,3,2,1,0:T(8,128)(2,1)} reshape(bf16[2,2,12,12,2,256]{5,4,3,2,1,0:T(2,128)(2,1)S(1)} %copy-done.1) | data formatting | bytes 1179648 | tf_op jit(solution)/shard_map/reshape | solution.py:443
  10.0 3.5 %shard_map.68 = f32[2,2,32,256]{3,2,1,0:T(8,128)} custom-call(s32[128]{0:T(128)} %reshape.259.gamma_ref, bf16[2,2,12,24,256]{4,3,2,1,0:T(8,128)(2,1)} %reshape.260.forward_ref, bf16[2,2,12,24,256]{4,3,2,1,0:T(8,128)(2,1)} %reshape.261.backward_ref), custom_call_target="tpu_custom_call" | custom-call | tf_op jit(solution)/shard_map/pallas_call | solution.py:444
  13.5 1.1 %reshape_reshape.3 = f32[2,2,16,2,4,64]{5,4,3,2,1,0:T(4,128)S(1)} reshape(f32[2,2,32,256]{3,2,1,0:T(8,128)} %shard_map.68) | data formatting | bytes 262144 | tf_op jit(solution)/shard_map/reshape;reshape | solution.py:461
  14.6 0.7 %convolution_bitcast_fusion.4 = f32[32,2,16]{0,2,1:T(8,128)S(1)} fusion(f32[2,2,16,1,4,64]{5,4,3,2,1,0:T(4,128)S(1)} %get-tuple-element.8, f32[32,64]{1,0:T(8,128)S(1)} %fusion.41, f32[32,2,4]{0,2,1:T(4,128)S(1)} %fusion.44), kind=kOutput, calls=%fused_computation.4 | convolution fusion | flops 6307840 | bytes 78848 | tf_op jit(solution)/shard_map/txgyz,mxyz->gtm/dot_general | solution.py:369
  15.3 0.7 %fusion.1 = f32[16,2,32]{2,0,1:T(8,128)S(1)} fusion(f32[32,2,16]{0,2,1:T(8,128)S(1)} %convolution_bitcast_fusion.4, f32[2,2,16,1,4,64]{5,4,3,2,1,0:T(4,128)S(1)} %get-tuple-element.9, f32[32,64]{1,0:T(8,128)S(1)} %fusion.41, f32[32,2,4]{0,2,1:T(4,128)S(1)} %fusion.44), kind=kOutput, calls=%fused_computation.7 | convolution fusion | flops 6308864 | bytes 82944 | tf_op jit(solution)/shard_map/txgyz,mxyz->gtm/dot_general | solution.py:369
  16.1 0.7 %convolution_bitcast_fusion.2 = f32[32,2,16]{0,2,1:T(8,128)S(1)} fusion(f32[2,2,16,1,4,64]{5,4,3,2,1,0:T(4,128)S(1)} %get-tuple-element.9, f32[32,64]{1,0:T(8,128)S(1)} %fusion.41, f32[32,2,4]{0,2,1:T(4,128)S(1)} %fusion.44), kind=kOutput, calls=%fused_computation.2 | convolution fusion | flops 6307840 | bytes 78848 | tf_op jit(solution)/shard_map/txgyz,mxyz->gtm/dot_general | solution.py:372
  16.8 0.7 %fusion.3 = f32[16,2,32]{2,0,1:T(8,128)S(1)} fusion(f32[32,2,16]{0,2,1:T(8,128)S(1)} %convolution_bitcast_fusion.2, f32[2,2,16,1,4,64]{5,4,3,2,1,0:T(4,128)S(1)} %get-tuple-element.8, f32[32,64]{1,0:T(8,128)S(1)} %fusion.41, f32[32,2,4]{0,2,1:T(4,128)S(1)} %fusion.44), kind=kOutput, calls=%fused_computation.9 | convolution fusion | flops 6308864 | bytes 82944 | tf_op jit(solution)/shard_map/txgyz,mxyz->gtm/dot_general | solution.py:372
  17.6 0.1 reshape.263
  17.7 0.6 convolution_bitcast_fusion
  18.3 0.6 copy.17
  18.9 0.3 copy.22
  19.3 0.7 %select_maximum_fusion.sent_ref = f32[16,9,256]{2,1,0:T(8,128)} fusion(f32[16,1,128]{2,1,0:T(1,128)S(1)} %reshape.263, f32[16,8,256]{2,1,0:T(8,128)S(1)} %copy.22), kind=kLoop, calls=%fused_computation.12 | loop fusion | flops 110592 | bytes 286720 | tf_op jit(solution)/shard_map/concatenate | solution.py:476
  20.0 17.3 %shard_map.69.blocks_ref = f32[32,9,128]{2,1,0:T(8,128)} custom-call(s32[1]{0:T(128)} %get-tuple-element.19.anchor_ref, f32[16,9,256]{2,1,0:T(8,128)} %select_maximum_fusion.sent_ref), custom_call_target="tpu_custom_call" | custom-call | tf_op jit(solution)/shard_map/pallas_call | solution.py:184
  37.3 31.3 %shard_map.70 = (f32[32,9,128]{2,1,0:T(8,128)}, f32[16,128]{1,0:T(8,128)}) custom-call(f32[32,9,128]{2,1,0:T(8,128)} %shard_map.69.blocks_ref), custom_call_target="tpu_custom_call" | custom-call | tf_op jit(solution)/shard_map/pallas_call | solution.py:289
  68.6 0.0 copy-start.2
  68.6 0.9 %slice.47 = f32[32,8,128]{2,1,0:T(8,128)S(1)} slice(f32[32,9,128]{2,1,0:T(8,128)} %get-tuple-element.4), slice={[0:32], [0:8], [0:128]} | slice | bytes 262144 | tf_op jit(solution)/shard_map/slice | solution.py:306
  69.6 0.0 copy-done.2
  69.6 0.7 reshape.267
  70.3 0.2 copy.23
  70.5 0.5 convolution_bitcast_fusion.1
  71.0 0.2 copy.26
  71.2 0.9 %reshape.266 = f32[16,2,2,2,256]{4,3,2,1,0:T(2,128)} reshape(f32[32,2,2,4,64]{4,3,2,1,0:T(4,128)S(1)} %copy.26) | data formatting | bytes 262144 | tf_op jit(solution)/shard_map/reshape | solution.py:483
  (8 shorter events, 0.1 us)
Async XLA Ops:
  0.6 0.7 copy-start.5
  1.3 0.7 copy-start.3
  4.8 0.7 copy-start.4
  6.8 1.1 %copy-start = (bf16[2,2,12,12,2,256]{5,4,3,2,1,0:T(2,128)(2,1)S(1)}, bf16[2,2,12,12,2,256]{5,4,3,2,1,0:T(2,128)(2,1)}, u32[]{:S(2)}) copy-start(bf16[2,2,12,12,2,256]{5,4,3,2,1,0:T(2,128)(2,1)} %param.5) | copy-start | bytes 1769476
  7.9 1.1 %copy-start.1 = (bf16[2,2,12,12,2,256]{5,4,3,2,1,0:T(2,128)(2,1)S(1)}, bf16[2,2,12,12,2,256]{5,4,3,2,1,0:T(2,128)(2,1)}, u32[]{:S(2)}) copy-start(bf16[2,2,12,12,2,256]{5,4,3,2,1,0:T(2,128)(2,1)} %param.6) | copy-start | bytes 1769476
  68.6 0.9 %copy-start.2 = (f32[16,128]{1,0:T(8,128)S(1)}, f32[16,128]{1,0:T(8,128)}, u32[]{:S(2)}) copy-start(f32[16,128]{1,0:T(8,128)} %get-tuple-element.5) | copy-start | bytes 24580

commit v18 on v16

--- a/solution.py
+++ b/solution.py
@@ -366,11 +366,11 @@
     sine = jnp.sin(angles)
     field_re = fields[:, 0].reshape(fields.shape[0], -1)
     field_im = fields[:, 1].reshape(fields.shape[0], -1)
-    local_re = jnp.dot(field_re, cosine.T, precision=HIGHEST) + jnp.dot(
-        field_im, sine.T, precision=HIGHEST
-    )
-    local_im = jnp.dot(field_im, cosine.T, precision=HIGHEST) - jnp.dot(
-        field_re, sine.T, precision=HIGHEST
+    local_re = jnp.dot(field_re, cosine.T, precision=HIGH) + jnp.dot(
+        field_im, sine.T, precision=HIGH
+    )
+    local_im = jnp.dot(field_im, cosine.T, precision=HIGH) - jnp.dot(
+        field_re, sine.T, precision=HIGH
     )
     return (local_re, local_im)
 

time: 71.6 us -> 71.5 us (level)
  no operation moved by 1% of the time
where the time goes in v18:
time: 71.5 us; the launch traced here: 71 us
  Pallas kernels  52 us (73%)
  local copies, waits for them, and re-layouts  11.9 us (17%)
  other arithmetic  4.63 us (6%)
  matrix products  1.63 us (2%)
  between operations  0.88 us (1%)
    pallas_call x1, Pallas kernels, spread_ready(): pl.pallas_call(spread_kernel, out_shape=(jax.ShapeDtypeStruct(shaped.shap...  31.3 us
    pallas_call x1, Pallas kernels, turn(): pl.pallas_call(turn_kernel, out_shape=jax.ShapeDtypeStruct((parts_x, band...  17.2 us
    pallas_call x1, Pallas kernels, contract(): pl.pallas_call(contract_kernel, out_shape=jax.ShapeDtypeStruct((slices, r...  3.5 us
    unnamed x13, local copies, waits for them, and re-layouts  2.94 us

profile of v18, /device:TPU:1, one launch (start us, length us, event | category | flops | bytes accessed | tf_op | source)
XLA Modules:
  0.0 71.0 jit_solution(11246815368630269965)
XLA Ops:
  0.6 0.7 copy-done.5
  1.3 0.7 copy-done.3
  2.0 0.6 fusion.26
  2.6 0.6 add_subtract_fusion.1
  3.2 0.5 add_subtract_fusion
  3.8 0.7 iota_subtract_fusion
  4.4 0.1 add_select_fusion.4
  4.5 0.1 fusion.20
  4.6 0.1 add_select_fusion.2
  4.7 0.1 add_select_fusion.3
  4.8 0.0 copy-start.4
  4.8 0.1 fusion.18
  4.9 0.5 copy-done.4
  5.5 0.1 copy.11
  5.6 0.7 reshape.296.gamma_ref
  6.2 1.1 %add_sine_fusion = (f32[32,2,4,64]{3,2,1,0:T(4,128)S(1)}, f32[32,2,4,64]{3,2,1,0:T(4,128)S(1)}) fusion(f32[32,64]{1,0:T(8,128)S(1)} %fusion.20, f32[32,2,4]{2,1,0:T(2,128)S(1)} %fusion.18), kind=kLoop, calls=%fused_computation.13 | loop fusion | flops 16384 | bytes 140288 | tf_op jit(solution)/shard_map/sin | solution.py:366
  7.3 0.1 sin.32
  7.4 0.1 cos.28
  7.5 0.5 fusion.15
  8.1 0.0 copy-start
  8.1 0.1 copy.10
  8.2 0.9 %copy-done = bf16[2,2,12,12,2,256]{5,4,3,2,1,0:T(2,128)(2,1)S(1)} copy-done((bf16[2,2,12,12,2,256]{5,4,3,2,1,0:T(2,128)(2,1)S(1)}, bf16[2,2,12,12,2,256]{5,4,3,2,1,0:T(2,128)(2,1)}, u32[]{:S(2)}) %copy-start) | copy-done | bytes 589848
  9.1 1.0 %reshape.297.forward_ref = bf16[2,2,12,24,256]{4,3,2,1,0:T(8,128)(2,1)} reshape(bf16[2,2,12,12,2,256]{5,4,3,2,1,0:T(2,128)(2,1)S(1)} %copy-done) | data formatting | bytes 1179648 | tf_op jit(solution)/shard_map/reshape | solution.py:441
  10.2 0.0 copy-done.1
  10.2 1.0 %reshape.298.backward_ref = bf16[2,2,12,24,256]{4,3,2,1,0:T(8,128)(2,1)} reshape(bf16[2,2,12,12,2,256]{5,4,3,2,1,0:T(2,128)(2,1)S(1)} %copy-done.1) | data formatting | bytes 1179648 | tf_op jit(solution)/shard_map/reshape | solution.py:442
  11.2 3.5 %shard_map.68 = f32[2,2,32,256]{3,2,1,0:T(8,128)} custom-call(s32[128]{0:T(128)} %reshape.296.gamma_ref, bf16[2,2,12,24,256]{4,3,2,1,0:T(8,128)(2,1)} %reshape.297.forward_ref, bf16[2,2,12,24,256]{4,3,2,1,0:T(8,128)(2,1)} %reshape.298.backward_ref), custom_call_target="tpu_custom_call" | custom-call | tf_op jit(solution)/shard_map/pallas_call | solution.py:443
  14.7 1.0 %reshape.299 = f32[2,2,16,2,256]{4,3,2,1,0:T(2,128)S(1)} reshape(f32[2,2,32,256]{3,2,1,0:T(8,128)} %shard_map.68) | data formatting | bytes 262144 | tf_op jit(solution)/shard_map/reshape | solution.py:451
  15.7 0.1 copy.43
  15.8 0.2 reshape.300
  16.1 0.1 reshape_squeeze.14
  16.2 0.2 fusion.27
  16.4 0.1 reshape_squeeze.15
  16.5 0.2 fusion.28
  16.6 0.2 fusion.1
  16.8 0.2 fusion
  17.0 0.1 reshape.302
  17.1 0.5 convolution_bitcast_fusion
  17.6 0.5 copy.15
  18.0 0.3 copy.16
  18.4 0.7 %select_maximum_fusion.sent_ref = f32[16,9,256]{2,1,0:T(8,128)} fusion(f32[16,1,128]{2,1,0:T(1,128)S(1)} %reshape.302, f32[16,8,256]{2,1,0:T(8,128)S(1)} %copy.16), kind=kLoop, calls=%fused_computation.8 | loop fusion | flops 110592 | bytes 286720 | tf_op jit(solution)/shard_map/concatenate | solution.py:475
  19.1 17.2 %shard_map.69.blocks_ref = f32[32,9,128]{2,1,0:T(8,128)} custom-call(s32[1]{0:T(128)} %get-tuple-element.21.anchor_ref, f32[16,9,256]{2,1,0:T(8,128)} %select_maximum_fusion.sent_ref), custom_call_target="tpu_custom_call" | custom-call | tf_op jit(solution)/shard_map/pallas_call | solution.py:184
  36.3 31.3 %shard_map.70 = (f32[32,9,128]{2,1,0:T(8,128)}, f32[16,128]{1,0:T(8,128)}) custom-call(f32[32,9,128]{2,1,0:T(8,128)} %shard_map.69.blocks_ref), custom_call_target="tpu_custom_call" | custom-call | tf_op jit(solution)/shard_map/pallas_call | solution.py:289
  67.6 0.9 %slice.47 = f32[32,8,128]{2,1,0:T(8,128)S(1)} slice(f32[32,9,128]{2,1,0:T(8,128)} %get-tuple-element.4), slice={[0:32], [0:8], [0:128]} | slice | bytes 262144 | tf_op jit(solution)/shard_map/slice | solution.py:306
  68.6 0.7 reshape.306
  69.3 0.2 copy.17
  69.5 0.5 convolution_bitcast_fusion.1
  70.0 0.2 copy.20
  70.2 0.9 %reshape.305 = f32[16,2,2,2,256]{4,3,2,1,0:T(2,128)} reshape(f32[32,2,2,4,64]{4,3,2,1,0:T(4,128)S(1)} %copy.20) | data formatting | bytes 262144 | tf_op jit(solution)/shard_map/reshape | solution.py:482
  (10 shorter events, 0.1 us)
Async XLA Ops:
  0.6 0.7 copy-start.5
  1.3 0.7 copy-start.3
  4.8 0.7 copy-start.4
  8.1 1.1 %copy-start = (bf16[2,2,12,12,2,256]{5,4,3,2,1,0:T(2,128)(2,1)S(1)}, bf16[2,2,12,12,2,256]{5,4,3,2,1,0:T(2,128)(2,1)}, u32[]{:S(2)}) copy-start(bf16[2,2,12,12,2,256]{5,4,3,2,1,0:T(2,128)(2,1)} %param.5) | copy-start | bytes 1769476
  9.1 1.1 %copy-start.1 = (bf16[2,2,12,12,2,256]{5,4,3,2,1,0:T(2,128)(2,1)S(1)}, bf16[2,2,12,12,2,256]{5,4,3,2,1,0:T(2,128)(2,1)}, u32[]{:S(2)}) copy-start(bf16[2,2,12,12,2,256]{5,4,3,2,1,0:T(2,128)(2,1)} %param.6) | copy-start | bytes 1769476
  67.6 0.9 %copy-start.2 = (f32[16,128]{1,0:T(8,128)S(1)}, f32[16,128]{1,0:T(8,128)}, u32[]{:S(2)}) copy-start(f32[16,128]{1,0:T(8,128)} %get-tuple-element.5) | copy-start | bytes 24580
